TPU v7x, 128 devices: a whole 4x4x4 slice. The times are simulated.
128 devices in a mesh: dp: 2 (over core), row: 16 (over y, x), col: 4 (over z).
Axes of the slice: x: 4, y: 4, z: 4, core: 2. Of those that a mesh axis runs over, the one named last changes fastest.
Arguments:
- inputs: bfloat16 [768, 32768], P('col', ('dp', 'row')), may hold values from -6 to 6
- teacher: bfloat16 [768, 32768], P('col', ('dp', 'row')), may hold values from -6 to 6
- lengths: int32 [32], P(('dp', 'row')), may hold values from 256 to 1024
- query_weight: bfloat16 [768, 768], P('row', 'col'), may hold values from -0.21875 to 0.21875
- query_bias: float32 [768], P('col'), may hold values from -3 to 3
- key_weight: bfloat16 [768, 768], P('row', 'col'), may hold values from -0.21875 to 0.21875
- value_weight: bfloat16 [768, 768], P('row', 'col'), may hold values from -0.21875 to 0.21875
- value_bias: float32 [768], P('col'), may hold values from -3 to 3
- output_weight: bfloat16 [768, 768], P('col', 'row'), may hold values from -6 to 6
- output_bias: float32 [768], P('col'), may hold values from -3 to 3
- first_gain: float32 [768], P('col'), may hold values from 0.5 to 1.5
- first_shift: float32 [768], P('col'), may hold values from -3 to 3
- up_weight: bfloat16 [768, 3072], P('row', 'col'), may hold values from -0.21875 to 0.21875
- up_bias: float32 [3072], P('col'), may hold values from -3 to 3
- down_weight: bfloat16 [768, 3072], P('row', 'col'), may hold values from -0.109375 to 0.109375
- down_bias: float32 [768], P('col'), may hold values from -3 to 3
- second_gain: float32 [768], P('col'), may hold values from 0.5 to 1.5
- second_shift: float32 [768], P('col'), may hold values from -3 to 3
Outputs:
- output: bfloat16 [768, 32768], P('col', ('dp', 'row'))
- distill_loss: float32 [], replicated
- grad_inputs: float32 [768, 32768], P('col', ('dp', 'row'))
- grad_query_weight: float32 [768, 768], P('row', 'col')
- grad_query_bias: float32 [768], P('col')
- grad_key_weight: float32 [768, 768], P('row', 'col')
- grad_value_weight: float32 [768, 768], P('row', 'col')
- grad_value_bias: float32 [768], P('col')
- grad_output_weight: float32 [768, 768], P('col', 'row')
- grad_output_bias: float32 [768], P('col')
- grad_first_gain: float32 [768], P('col')
- grad_first_shift: float32 [768], P('col')
- grad_up_weight: float32 [768, 3072], P('row', 'col')
- grad_up_bias: float32 [3072], P('col')
- grad_down_weight: float32 [768, 3072], P('row', 'col')
- grad_down_bias: float32 [768], P('col')
- grad_second_gain: float32 [768], P('col')
- grad_second_shift: float32 [768], P('col')
All inputs are finite; a program needn't handle non-finite values.
Results may differ from a plain program's by a relative error of at most 0.018.
Values may be sent and summed in bfloat16 or wider, within the bound.
A program may use at most 64 MiB of HBM per device.

v0:
```python
import functools

import jax
import jax.numpy as jnp
from jax import lax
from jax.sharding import Mesh
from jax.sharding import PartitionSpec as P

HEAD_DIM = 64
D = 768
LEN = 1024
SEQ_ROW = 1
ROW = ("row_0", "row_1")
DP_ROW_COL = ("dp", "row_0", "row_1", "col")
DP_ROW = ("dp", "row_0", "row_1")


norm_eps = 1e-12
mask_value = -1e30
root_half = 0.7071067811865476
inv_root_tau = 0.3989422804014327


def sent_to_all(shard, axis):
    size = lax.axis_size(axis)
    return lax.all_to_all(
        jnp.broadcast_to(shard[None], (size, *shard.shape)), axis, 0, 0, tiled=True
    )


def joined_along(pieces, dim):
    shape = list(pieces.shape[1:])
    shape[dim] *= pieces.shape[0]
    return jnp.moveaxis(pieces, 0, dim).reshape(shape)


def collect(shard, axis, dim):
    pieces = sent_to_all(shard, axis)
    return joined_along(pieces, dim)


def split_up(shard, dim, size):
    before, after = (shard.shape[:dim], shard.shape[dim + 1 :])
    return jnp.moveaxis(shard.reshape(*before, size, -1, *after), dim, 0)


def sum_at_owner(shard, axis, dim):
    size = lax.axis_size(axis)
    pieces = lax.all_to_all(split_up(shard, dim, size), axis, 0, 0, tiled=True)
    return jnp.sum(pieces, axis=0)


def over_copies(shard, axis):
    return sent_to_all(shard, axis).sum(axis=0)


def packed_total(arrays, axis):
    ends = [0]
    for a in arrays:
        ends.append(ends[-1] + a.size)
    subtotal = over_copies(jnp.concatenate([a.ravel() for a in arrays]), axis)
    return tuple((subtotal[b:e].reshape(a.shape) for a, b, e in zip(arrays, ends, ends[1:])))


def sent_together(arrays, axis, dim, along):
    both = jnp.concatenate(arrays, axis=along)
    whole, at, done = (lax.all_gather(both, axis, axis=dim, tiled=True), 0, [])
    for a in arrays:
        done.append(lax.slice_in_dim(whole, at, at + a.shape[along], axis=along))
        at += a.shape[along]
    return tuple(done)


def over_axes(shard, axes):
    return functools.reduce(lax.psum, axes, shard)


def in_one_piece(arrays, axis, dim, along):
    ends, at = ([], 0)
    for a in arrays[:-1]:
        at += a.shape[along]
        ends.append(at)
    both = jnp.concatenate(arrays, axis=along)
    return tuple(
        jnp.split(lax.psum_scatter(both, axis, scatter_dimension=dim, tiled=True), ends, axis=along)
    )


def across_features(feature_rows, matrix):
    return lax.dot_general(
        feature_rows, matrix, (((0,), (0,)), ((), ())), preferred_element_type=jnp.float32
    )


def over_tokens(feature_rows, token_rows):
    return lax.dot_general(
        feature_rows, token_rows, (((1,), (0,)), ((), ())), preferred_element_type=jnp.float32
    )


def gather_features(block):
    return collect(block, "col", 0)


def spread_sum(matrix, token_rows):
    return sum_at_owner(
        lax.dot_general(
            matrix, token_rows, (((1,), (1,)), ((), ())), preferred_element_type=jnp.float32
        ),
        "col",
        0,
    )


def feature_total(first_term, second_term):
    return packed_total((jnp.sum(first_term, axis=0), jnp.sum(second_term, axis=0)), "col")


def normalize(resid, gain, shift):
    totals, squares = feature_total(resid, resid * resid)
    average = totals / D
    variance = squares / D - average * average
    inv_scale = lax.rsqrt(variance + norm_eps)
    normed = (resid - average[None, :]) * inv_scale[None, :]
    return (normed * gain[:, None] + shift[:, None], normed, inv_scale)


def normalize_back(upstream, normed, inv_scale, gain):
    scaled = upstream * gain[:, None]
    totals, crossed = feature_total(scaled, scaled * normed)
    return inv_scale[None, :] * (scaled - totals[None, :] / D - normed * crossed[None, :] / D)


def group_major(grad, row_count, group_count):
    rows_each = grad.shape[0] // (row_count * group_count)
    shaped = grad.reshape(row_count, group_count, rows_each, grad.shape[1])
    return jnp.swapaxes(shaped, 0, 1).reshape(grad.shape)


def masked_scores(rows_block, keys_all, keys_ok, scale):
    score = (
        jnp.einsum("qhd,khd->hqk", rows_block, keys_all, preferred_element_type=jnp.float32) * scale
    )
    return jnp.where(keys_ok[None, None, :], score, mask_value)


def attend_forward(queries, keys_all, values_all, length, block_rows):
    keys_ok = jnp.arange(keys_all.shape[0]) < length
    scale = queries.shape[-1] ** (-0.5)
    blocks = queries.reshape(-1, block_rows, queries.shape[1], queries.shape[2])

    def one_block(rows_block):
        score = masked_scores(rows_block, keys_all, keys_ok, scale)
        highest = jnp.max(score, axis=-1, keepdims=True)
        expo = jnp.exp(score - highest)
        totals = jnp.sum(expo, axis=-1, keepdims=True)
        probs_low = (expo / totals).astype(jnp.bfloat16)
        context = jnp.einsum(
            "hqk,khd->qhd", probs_low, values_all, preferred_element_type=jnp.float32
        )
        return (context, highest[..., 0] + jnp.log(totals[..., 0]))

    context, log_sums = lax.map(one_block, blocks)
    return (context.reshape(queries.shape), log_sums)


def attend_backward(queries, keys_all, values_all, length, log_sums, context_grad, block_rows):
    keys_ok = jnp.arange(keys_all.shape[0]) < length
    scale = queries.shape[-1] ** (-0.5)
    blocks = queries.reshape(-1, block_rows, queries.shape[1], queries.shape[2])
    grad_blocks = context_grad.reshape(blocks.shape)

    def one_block(carry, items):
        key_acc, value_acc = carry
        rows_block, grad_rows, log_block = items
        score = masked_scores(rows_block, keys_all, keys_ok, scale)
        probs = jnp.exp(score - log_block[..., None])
        probs_low = probs.astype(jnp.bfloat16)
        value_acc = value_acc + jnp.einsum(
            "hqk,qhd->khd", probs_low, grad_rows, preferred_element_type=jnp.float32
        )
        prob_grad = jnp.einsum(
            "qhd,khd->hqk", grad_rows, values_all, preferred_element_type=jnp.float32
        )
        inner = jnp.sum(probs * prob_grad, axis=-1, keepdims=True)
        score_grad = (probs * (prob_grad - inner)).astype(jnp.bfloat16)
        query_part = (
            jnp.einsum("hqk,khd->qhd", score_grad, keys_all, preferred_element_type=jnp.float32)
            * scale
        )
        key_acc = (
            key_acc
            + jnp.einsum("hqk,qhd->khd", score_grad, rows_block, preferred_element_type=jnp.float32)
            * scale
        )
        return ((key_acc, value_acc), query_part)

    zeros = jnp.zeros(keys_all.shape, jnp.float32)
    (key_grad, value_grad), query_grad = lax.scan(
        one_block, (zeros, zeros), (blocks, grad_blocks, log_sums)
    )
    return (query_grad.reshape(queries.shape), key_grad, value_grad)


def local(
    inputs,
    teacher,
    lengths,
    query_weight,
    query_bias,
    key_weight,
    value_weight,
    value_bias,
    output_weight,
    output_bias,
    first_gain,
    first_shift,
    up_weight,
    up_bias,
    down_weight,
    down_bias,
    second_gain,
    second_shift,
):
    head_cols = query_weight.shape[1]
    heads_here = head_cols // HEAD_DIM
    token_count = inputs.shape[1]
    block_rows = min(512, LEN)
    seq_shape = (SEQ_ROW, LEN, heads_here, HEAD_DIM)
    joint_local = jnp.concatenate([query_weight, key_weight, value_weight], axis=1)
    joint_full, output_full, up_full, down_full = sent_together(
        (joint_local, output_weight.T, up_weight, down_weight), ROW, 0, 1
    )
    joint_bias = jnp.concatenate([query_bias, jnp.zeros_like(query_bias), value_bias])
    input_rows = gather_features(inputs)
    joint = (across_features(input_rows, joint_full) + joint_bias).astype(jnp.bfloat16)
    queries = joint[:, :head_cols].reshape(seq_shape)
    keys_all = joint[:, head_cols : 2 * head_cols].reshape(seq_shape)
    values_all = joint[:, 2 * head_cols :].reshape(seq_shape)

    def forward_one(items):
        return attend_forward(items[0], items[1], items[2], items[3], block_rows)

    context, log_sums = lax.map(forward_one, (queries, keys_all, values_all, lengths))
    context = context.reshape(token_count, head_cols).astype(jnp.bfloat16)
    first_resid = (
        inputs.astype(jnp.float32) + spread_sum(output_full, context) + output_bias[:, None]
    )
    hidden, first_normed, first_inv = normalize(first_resid, first_gain, first_shift)
    hidden_low = hidden.astype(jnp.bfloat16)
    hidden_rows = gather_features(hidden_low)
    pre_act = across_features(hidden_rows, up_full) + up_bias
    activation = (0.5 * pre_act * (1.0 + lax.erf(pre_act * root_half))).astype(jnp.bfloat16)
    second_resid = hidden + spread_sum(down_full, activation) + down_bias[:, None]
    final, second_normed, second_inv = normalize(second_resid, second_gain, second_shift)
    token = jnp.arange(token_count)
    owner = jnp.arange(lengths.shape[0])
    limit = jnp.sum(
        jnp.where((token // LEN)[:, None] == owner[None, :], lengths[None, :], 0), axis=1
    )
    valid = token % LEN < limit
    difference = final - teacher.astype(jnp.float32)
    squared_part = jnp.sum(jnp.where(valid[None, :], difference * difference, 0.0))
    leader = lax.axis_index("col") == 0
    own_count = jnp.where(leader, jnp.sum(lengths), 0).astype(jnp.float32)
    squared_total, count = (over_axes(squared_part, DP_ROW_COL), over_axes(own_count, DP_ROW_COL))
    distill_loss = squared_total / (2.0 * D * count)
    slots = lengths.shape[0] * LEN * lax.axis_size("dp") * lax.axis_size(ROW)
    final_grad = jnp.where(valid[None, :], difference, 0.0) * (slots / count)
    second_grad = normalize_back(final_grad, second_normed, second_inv, second_gain)
    second_gain_grad = jnp.sum(final_grad * second_normed, axis=1)
    second_shift_grad = jnp.sum(final_grad, axis=1)
    down_grad_low = second_grad.astype(jnp.bfloat16)
    down_bias_grad = jnp.sum(down_grad_low, axis=1, dtype=jnp.float32)
    down_rows = gather_features(down_grad_low)
    act_grad = across_features(down_rows, down_full)
    down_weight_grad = over_tokens(down_rows, activation)
    slope = (
        0.5 * (1.0 + lax.erf(pre_act * root_half))
        + pre_act * jnp.exp(-0.5 * pre_act * pre_act) * inv_root_tau
    )
    pre_grad = (act_grad * slope).astype(jnp.bfloat16)
    up_bias_grad = jnp.sum(pre_grad, axis=0, dtype=jnp.float32)
    up_weight_grad = over_tokens(hidden_rows, pre_grad)
    hidden_grad = second_grad + spread_sum(up_full, pre_grad)
    first_grad = normalize_back(hidden_grad, first_normed, first_inv, first_gain)
    first_gain_grad = jnp.sum(hidden_grad * first_normed, axis=1)
    first_shift_grad = jnp.sum(hidden_grad, axis=1)
    branch_grad = first_grad.astype(jnp.bfloat16)
    output_bias_grad = jnp.sum(branch_grad, axis=1, dtype=jnp.float32)
    branch_rows = gather_features(branch_grad)
    output_weight_grad = over_tokens(branch_rows, context)
    context_grad = across_features(branch_rows, output_full).astype(jnp.bfloat16).reshape(seq_shape)

    def backward_one(items):
        return attend_backward(
            items[0], items[1], items[2], items[3], items[4], items[5], block_rows
        )

    query_grad, key_grad, value_grad = lax.map(
        backward_one, (queries, keys_all, values_all, lengths, log_sums, context_grad)
    )
    joint_grad = jnp.concatenate(
        [
            query_grad.reshape(-1, head_cols),
            key_grad.reshape(-1, head_cols),
            value_grad.reshape(-1, head_cols),
        ],
        axis=1,
    ).astype(jnp.bfloat16)
    query_bias_grad = jnp.sum(joint_grad[:, :head_cols], axis=0, dtype=jnp.float32)
    value_bias_grad = jnp.sum(joint_grad[:, 2 * head_cols :], axis=0, dtype=jnp.float32)
    joint_weight_grad = over_tokens(input_rows, joint_grad)
    grad_inputs = first_grad + spread_sum(joint_full, joint_grad)
    (
        query_bias_grad,
        value_bias_grad,
        output_bias_grad,
        first_gain_grad,
        first_shift_grad,
        up_bias_grad,
        down_bias_grad,
        second_gain_grad,
        second_shift_grad,
    ) = packed_total(
        (
            query_bias_grad,
            value_bias_grad,
            output_bias_grad,
            first_gain_grad,
            first_shift_grad,
            up_bias_grad,
            down_bias_grad,
            second_gain_grad,
            second_shift_grad,
        ),
        DP_ROW,
    )
    row_count = lax.axis_size(ROW)
    group_count = lax.axis_size("dp")
    parted = tuple(
        (
            part.astype(jnp.float32)
            for part in in_one_piece(
                (
                    group_major(joint_weight_grad, row_count, group_count).astype(jnp.bfloat16),
                    group_major(output_weight_grad, row_count, group_count).astype(jnp.bfloat16),
                    group_major(up_weight_grad, row_count, group_count).astype(jnp.bfloat16),
                    group_major(down_weight_grad, row_count, group_count).astype(jnp.bfloat16),
                ),
                DP_ROW,
                0,
                1,
            )
        )
    )
    joint_summed, output_summed, up_summed, down_summed = tuple(
        (
            part.astype(jnp.float32)
            for part in sent_together(
                (
                    parted[0].astype(jnp.bfloat16),
                    parted[1].astype(jnp.bfloat16),
                    parted[2].astype(jnp.bfloat16),
                    parted[3].astype(jnp.bfloat16),
                ),
                "dp",
                0,
                1,
            )
        )
    )
    return (
        final.astype(jnp.bfloat16),
        distill_loss,
        grad_inputs,
        joint_summed[:, :head_cols],
        query_bias_grad,
        joint_summed[:, head_cols : 2 * head_cols],
        joint_summed[:, 2 * head_cols :],
        value_bias_grad,
        output_summed.T,
        output_bias_grad,
        first_gain_grad,
        first_shift_grad,
        up_summed,
        up_bias_grad,
        down_summed,
        down_bias_grad,
        second_gain_grad,
        second_shift_grad,
    )


def solution(mesh):
    split = Mesh(
        mesh.devices.reshape(mesh.shape["dp"], 4, 4, mesh.shape["col"]),
        ("dp", "row_0", "row_1", "col"),
    )
    placed = (
        P("col", DP_ROW),
        P("col", DP_ROW),
        P(DP_ROW),
        P(ROW, "col"),
        P("col"),
        P(ROW, "col"),
        P(ROW, "col"),
        P("col"),
        P("col", ROW),
        P("col"),
        P("col"),
        P("col"),
        P(ROW, "col"),
        P("col"),
        P(ROW, "col"),
        P("col"),
        P("col"),
        P("col"),
    )
    return jax.shard_map(
        local,
        mesh=split,
        in_specs=placed,
        out_specs=(
            P("col", DP_ROW),
            P(),
            P("col", DP_ROW),
            P(ROW, "col"),
            P("col"),
            P(ROW, "col"),
            P(ROW, "col"),
            P("col"),
            P("col", ROW),
            P("col"),
            P("col"),
            P("col"),
            P(ROW, "col"),
            P("col"),
            P(ROW, "col"),
            P("col"),
            P("col"),
            P("col"),
        ),
        check_vma=False,
    )
```

profile of v0, /device:TPU:1, one launch (start us, length us, event | category | flops | bytes accessed | tf_op | source)
XLA Modules:
  0.0 456.5 jit_solution(14530233342852276493)
XLA Ops:
  11.4 5.9 %all-to-all-start = ((bf16[4,192,1024]{2,1,0:T(8,128)(2,1)}), bf16[4,192,1024]{2,1,0:T(8,128)(2,1)S(1)}, u32[]{:S(2)}, u32[]{:S(2)}) async-start(bf16[4,192,1024]{2,1,0:T(8,128)(2,1)} %broadcast_in_dim.88), calls=%async_computation | async-start | bytes 3145728 | tf_op jit(solution)/shard_map/all_to_all | solution.py:26
  17.4 19.7 %all-to-all-done = bf16[4,192,1024]{2,1,0:T(8,128)(2,1)S(1)} async-done(((bf16[4,192,1024]{2,1,0:T(8,128)(2,1)}), bf16[4,192,1024]{2,1,0:T(8,128)(2,1)S(1)}, u32[]{:S(2)}, u32[]{:S(2)}) %all-to-all-start) | async-done | bytes 1572896 | tf_op jit(solution)/shard_map/all_to_all | solution.py:26
  37.1 25.7 %all-gather.2.cloned.1.call-done = bf16[768,2304]{1,0:T(8,128)(2,1)} async-done(((bf16[48,2304]{1,0:T(8,128)(2,1)}), bf16[768,2304]{1,0:T(8,128)(2,1)}) %all-gather.2.cloned.1.call-update) | async-done | bytes 3538960 | tf_op jit(solution)/shard_map/all_gather | solution.py:67
  65.5 10.8 %while.48 = (s32[]{:T(128)}, bf16[2,512,3,64]{1,3,2,0:T(8,128)(2,1)S(1)}, f32[2,3,512]{2,1,0:T(4,128)S(1)}, bf16[2,512,3,64]{1,3,2,0:T(8,128)(2,1)S(1)}, bf16[10...) while((s32[]{:T(128)}, ...), condition=%wide.region_3.4_spmd.clone, body=%wide.region_0.3_spmd.clone.sunk | while | flops 421527040 | bytes 20314220 | solution.py:163
  78.9 40.0 %all_to_all.72 = f32[4,192,1024]{2,1,0:T(8,128)} all-to-all(f32[4,192,1024]{2,1,0:T(8,128)S(1)} %fusion.112), channel_id=1, replica_groups=mesh['dp'=2,'row_0'=4,'row_1'=4,'col'=4] {'col'}, dimensions={0} | all-to-all | bytes 6291456 | tf_op jit(solution)/shard_map/all_to_all | solution.py:49
  121.5 6.7 %all_to_all.73 = f32[4,1,2048]{2,1,0:T(1,128)S(1)} all-to-all(f32[4,1,2048]{2,1,0:T(1,128)S(1)} %broadcast_in_dim.90), channel_id=1, replica_groups=mesh['dp'=2,'row_0'=4,'row_1'=4,'col'=4] {'col'}, dimensions={0} | all-to-all | bytes 65536 | tf_op jit(solution)/shard_map/all_to_all | solution.py:26
  128.6 19.6 %all_to_all.70 = bf16[4,192,1024]{2,1,0:T(8,128)(2,1)S(1)} all-to-all(bf16[4,192,1024]{2,1,0:T(8,128)(2,1)S(1)} %broadcast_in_dim.91), channel_id=1, replica_groups=mesh['dp'=2,'row_0'=4,'row_1'=4,'col'=4] {'col'}, dimensions={0} | all-to-all | bytes 3145728 | tf_op jit(solution)/shard_map/all_to_all | solution.py:26
  148.3 3.5 multiply_convert_fusion.1
  154.8 4.6 %all-to-all-start.4 = ((f32[4,192,1024]{2,1,0:T(8,128)}), f32[4,192,1024]{2,1,0:T(8,128)}, u32[]{:S(2)}, u32[]{:S(2)}) async-start(f32[4,192,1024]{2,1,0:T(8,128)} %bitcast.175), calls=%async_computation.4 | async-start | bytes 6291456 | tf_op jit(solution)/shard_map/all_to_all | solution.py:49
  160.2 7.3 %psum.60 = f32[]{:T(128)} all-reduce(f32[]{:T(128)S(6)} %convert_element_type.137), channel_id=1, replica_groups=mesh['dp'=2,'row_0'=4,'row_1'=4,'col'=4] {'dp'}, use_global_device_ids=true, to_apply=%region_17.18 | all-reduce | flops 1 | bytes 8 | tf_op jit(solution)/shard_map/psum | solution.py:75
  167.4 10.2 %psum.61 = f32[]{:T(128)} all-reduce(f32[]{:T(128)} %psum.60), channel_id=1, replica_groups=mesh['dp'=2,'row_0'=4,'row_1'=4,'col'=4] {'row_0'}, use_global_device_ids=true, to_apply=%region_18.19 | all-reduce | flops 1 | bytes 8 | tf_op jit(solution)/shard_map/psum | solution.py:75
  177.6 7.4 %psum.62 = f32[]{:T(128)} all-reduce(f32[]{:T(128)} %psum.61), channel_id=1, replica_groups=mesh['dp'=2,'row_0'=4,'row_1'=4,'col'=4] {'row_1'}, use_global_device_ids=true, to_apply=%region_19.20 | all-reduce | flops 1 | bytes 8 | tf_op jit(solution)/shard_map/psum | solution.py:75
  185.0 7.5 %all-to-all-done.4 = f32[4,192,1024]{2,1,0:T(8,128)} async-done(((f32[4,192,1024]{2,1,0:T(8,128)}), f32[4,192,1024]{2,1,0:T(8,128)}, u32[]{:S(2)}, u32[]{:S(2)}) %all-to-all-start.4) | async-done | bytes 3145760 | tf_op jit(solution)/shard_map/all_to_all | solution.py:49
  201.0 9.3 %psum.63 = f32[]{:T(128)} all-reduce(f32[]{:T(128)} %psum.62), channel_id=1, replica_groups=mesh['dp'=2,'row_0'=4,'row_1'=4,'col'=4] {'col'}, use_global_device_ids=true, to_apply=%region_20.21 | all-reduce | flops 1 | bytes 8 | tf_op jit(solution)/shard_map/psum | solution.py:75
  212.3 6.7 %all_to_all.74 = f32[4,1,2048]{2,1,0:T(1,128)S(1)} all-to-all(f32[4,1,2048]{2,1,0:T(1,128)S(1)} %broadcast_in_dim.95), channel_id=1, replica_groups=mesh['dp'=2,'row_0'=4,'row_1'=4,'col'=4] {'col'}, dimensions={0} | all-to-all | bytes 65536 | tf_op jit(solution)/shard_map/all_to_all | solution.py:26
  221.3 15.0 %all_to_all.71 = bf16[4,192,1024]{2,1,0:T(8,128)(2,1)S(1)} all-to-all(bf16[4,192,1024]{2,1,0:T(8,128)(2,1)S(1)} %broadcast_in_dim.96), channel_id=1, replica_groups=mesh['dp'=2,'row_0'=4,'row_1'=4,'col'=4] {'col'}, dimensions={0} | all-to-all | bytes 3145728 | tf_op jit(solution)/shard_map/all_to_all | solution.py:26
  236.4 3.5 convert_reduce_fusion
  241.3 30.8 %all_to_all.75 = f32[4,192,1024]{2,1,0:T(8,128)} all-to-all(f32[4,192,1024]{2,1,0:T(8,128)S(1)} %bitcast.176), channel_id=1, replica_groups=mesh['dp'=2,'row_0'=4,'row_1'=4,'col'=4] {'col'}, dimensions={0} | all-to-all | bytes 6291456 | tf_op jit(solution)/shard_map/all_to_all | solution.py:49
  278.7 6.7 %all_to_all.76 = f32[4,1,2048]{2,1,0:T(1,128)S(1)} all-to-all(f32[4,1,2048]{2,1,0:T(1,128)S(1)} %broadcast_in_dim.97), channel_id=1, replica_groups=mesh['dp'=2,'row_0'=4,'row_1'=4,'col'=4] {'col'}, dimensions={0} | all-to-all | bytes 65536 | tf_op jit(solution)/shard_map/all_to_all | solution.py:26
  288.4 4.3 all-to-all-start.10
  315.9 19.8 %while.49 = (s32[]{:T(128)}, f32[1024,3,64]{0,2,1:T(8,128)S(1)}, f32[1024,3,64]{0,2,1:T(8,128)}, bf16[2,512,3,64]{1,3,2,0:T(8,128)(2,1)}, bf16[2,512,3,64]{1,3,2...) while((s32[]{:T(128)}, f32[1024,3,64]{0,2,1:T(8,128)S(1)}, ...), condition=%wide.region_30.31_spmd.clone, body=%wide.region_28.30_spmd.clone.sunk | while | flops 1031306752 | bytes 63752492 | solution.py:199
  344.9 6.3 %concatenate.37 = bf16[768,2304]{1,0:T(8,128)(2,1)} concatenate(bf16[768,576]{1,0:T(8,128)(2,1)} %bitcast.172, bf16[768,192]{1,0:T(8,128)(2,1)S(1)} %bitcast.177, bf16[768,768]{1,0:T(8,128)(2,1)} %bitcast.171, bf16[768,768]{1,0:T(8,128)(2,1)S(1)} %bitcast.170), dimensions={1} | concatenate | bytes 7077888 | tf_op jit(solution)/shard_map/concatenate | solution.py:83
  353.4 20.4 %all-to-all-start.12 = ((f32[32,1,2304]{2,1,0:T(1,128)}), f32[32,1,2304]{2,1,0:T(1,128)S(1)}, u32[]{:S(2)}, u32[]{:S(2)}) async-start(f32[32,1,2304]{2,1,0:T(1,128)} %broadcast_in_dim.102), calls=%async_computation.13 | async-start | bytes 589824 | tf_op jit(solution)/shard_map/all_to_all | solution.py:26
  373.8 4.3 fusion.77
  378.1 4.2 all-to-all-done.12
  382.3 4.7 %all-to-all-start.11 = ((f32[4,192,1024]{2,1,0:T(8,128)}), f32[4,192,1024]{2,1,0:T(8,128)}, u32[]{:S(2)}, u32[]{:S(2)}) async-start(f32[4,192,1024]{2,1,0:T(8,128)} %bitcast.174), calls=%async_computation.11 | async-start | bytes 6291456 | tf_op jit(solution)/shard_map/all_to_all | solution.py:49
  387.0 3.9 psum.56
  391.0 7.9 %psum.57 = f32[]{:T(128)} all-reduce(f32[]{:T(128)} %psum.56), channel_id=1, replica_groups=mesh['dp'=2,'row_0'=4,'row_1'=4,'col'=4] {'row_0'}, use_global_device_ids=true, to_apply=%region_14.15 | all-reduce | flops 1 | bytes 8 | tf_op jit(solution)/shard_map/psum | solution.py:75
  398.9 8.7 %psum.58 = f32[]{:T(128)} all-reduce(f32[]{:T(128)} %psum.57), channel_id=1, replica_groups=mesh['dp'=2,'row_0'=4,'row_1'=4,'col'=4] {'row_1'}, use_global_device_ids=true, to_apply=%region_15.16 | all-reduce | flops 1 | bytes 8 | tf_op jit(solution)/shard_map/psum | solution.py:75
  408.2 17.6 %psum.59 = f32[]{:T(128)} all-reduce(f32[]{:T(128)} %psum.58), channel_id=1, replica_groups=mesh['dp'=2,'row_0'=4,'row_1'=4,'col'=4] {'col'}, use_global_device_ids=true, to_apply=%region_16.17 | all-reduce | flops 1 | bytes 8 | tf_op jit(solution)/shard_map/psum | solution.py:75
  431.4 11.0 %reduce-scatter.2.cloned.1.call-done = bf16[24,2304]{1,0:T(8,128)(2,1)} async-done(((bf16[768,2304]{1,0:T(8,128)(2,1)}), bf16[24,2304]{1,0:T(8,128)(2,1)}) %reduce-scatter.2.cloned.1.call-update) | async-done | bytes 110608 | tf_op jit(solution)/shard_map/reduce_scatter | solution.py:85
  442.4 4.0 all_gather.7
  (218 shorter events, 110.4 us)
Async XLA Ops:
  7.2 10.1 %copy-start.40 = (f32[192]{0:T(256)S(1)}, f32[192]{0:T(256)}, u32[]{:S(2)}) copy-start(f32[192]{0:T(256)} %param.29) | copy-start | bytes 2308
  7.2 10.1 %copy-start.41 = (f32[192]{0:T(256)S(1)}, f32[192]{0:T(256)}, u32[]{:S(2)}) copy-start(f32[192]{0:T(256)} %param.26) | copy-start | bytes 2308
  7.2 55.5 %all-gather.2.cloned.1.call-start = ((), (), s32[]{:S(2)}) async-start(), calls=%async_computation.14 | async-start | bytes 3760128 | tf_op jit(solution)/shard_map/all_gather | solution.py:67
  11.4 25.7 %all-to-all-start = ((bf16[4,192,1024]{2,1,0:T(8,128)(2,1)}), bf16[4,192,1024]{2,1,0:T(8,128)(2,1)S(1)}, u32[]{:S(2)}, u32[]{:S(2)}) async-start(bf16[4,192,1024]{2,1,0:T(8,128)(2,1)} %broadcast_in_dim.88), calls=%async_computation | async-start | bytes 3145728 | tf_op jit(solution)/shard_map/all_to_all | solution.py:26
  37.1 25.7 %copy-start.5 = (bf16[4,192,1024]{2,1,0:T(8,128)(2,1)}, bf16[4,192,1024]{2,1,0:T(8,128)(2,1)S(1)}, u32[]{:S(2)}) copy-start(bf16[4,192,1024]{2,1,0:T(8,128)(2,1)S(1)} %all-to-all-done) | copy-start | bytes 4718596
  76.7 42.2 %copy-start.3 = (bf16[2,512,3,64]{1,0,3,2:T(2,128)(2,1)}, bf16[2,512,3,64]{1,0,3,2:T(2,128)(2,1)S(1)}, u32[]{:S(2)}) copy-start(bf16[2,512,3,64]{1,0,3,2:T(2,128)(2,1)S(1)} %copy.70) | copy-start | bytes 1179652
  118.9 9.3 %copy-start.25 = (f32[192]{0:T(256)S(1)}, f32[192]{0:T(256)}, u32[]{:S(2)}) copy-start(f32[192]{0:T(256)} %param.32) | copy-start | bytes 2308
  118.9 9.3 %copy-start.30 = (f32[192]{0:T(256)S(1)}, f32[192]{0:T(256)}, u32[]{:S(2)}) copy-start(f32[192]{0:T(256)} %param.33) | copy-start | bytes 2308
  128.2 20.1 %copy-start.21 = (bf16[768,2304]{1,0:T(8,128)(2,1)S(1)}, bf16[768,2304]{1,0:T(8,128)(2,1)}, u32[]{:S(2)}) copy-start(bf16[768,2304]{1,0:T(8,128)(2,1)} %all-gather.2.cloned.1.call-done) | copy-start | bytes 10616836
  128.2 20.0 %copy-start.42 = (f32[768]{0:T(1024)S(1)}, f32[768]{0:T(1024)}, u32[]{:S(2)}) copy-start(f32[768]{0:T(1024)} %param.35) | copy-start | bytes 9220
  148.3 3.5 copy-start.7
  154.8 37.7 %all-to-all-start.4 = ((f32[4,192,1024]{2,1,0:T(8,128)}), f32[4,192,1024]{2,1,0:T(8,128)}, u32[]{:S(2)}, u32[]{:S(2)}) async-start(f32[4,192,1024]{2,1,0:T(8,128)} %bitcast.175), calls=%async_computation.4 | async-start | bytes 6291456 | tf_op jit(solution)/shard_map/all_to_all | solution.py:49
  159.5 36.2 %copy-start.39 = (f32[192]{0:T(256)S(1)}, f32[192]{0:T(256)}, u32[]{:S(2)}) copy-start(f32[192]{0:T(256)} %param.37) | copy-start | bytes 2308
  185.0 26.0 %copy-start.2 = (bf16[192,1024]{1,0:T(8,128)(2,1)S(1)}, bf16[192,1024]{1,0:T(8,128)(2,1)}, u32[]{:S(2)}) copy-start(bf16[192,1024]{1,0:T(8,128)(2,1)} %param.23) | copy-start | bytes 1179652
  185.0 26.0 %copy-start.27 = (f32[192]{0:T(256)S(1)}, f32[192]{0:T(256)}, u32[]{:S(2)}) copy-start(f32[192]{0:T(256)} %param.39) | copy-start | bytes 2308
  185.0 26.0 %copy-start.28 = (f32[192]{0:T(256)S(1)}, f32[192]{0:T(256)}, u32[]{:S(2)}) copy-start(f32[192]{0:T(256)} %param.38) | copy-start | bytes 2308
  197.7 13.3 %all-to-all-start.5 = ((f32[4,1,2048]{2,1,0:T(1,128)}), f32[4,1,2048]{2,1,0:T(1,128)S(1)}, u32[]{:S(2)}, u32[]{:S(2)}) async-start(f32[4,1,2048]{2,1,0:T(1,128)} %broadcast_in_dim.92), calls=%async_computation.5 | async-start | bytes 65536 | tf_op jit(solution)/shard_map/all_to_all | solution.py:26
  201.0 11.3 %copy-start.29 = (pred[1024]{0:T(1024)(128)(4,1)}, pred[1024]{0:T(1024)(128)(4,1)S(1)}, u32[]{:S(2)}) copy-start(pred[1024]{0:T(1024)(128)(4,1)S(1)} %fusion.83) | copy-start | bytes 3076
  219.1 17.3 %copy-start.22 = (bf16[768,2304]{1,0:T(8,128)(2,1)S(1)}, bf16[768,2304]{1,0:T(8,128)(2,1)}, u32[]{:S(2)}) copy-start(bf16[768,2304]{1,0:T(8,128)(2,1)} %all-gather.2.cloned.1.call-done) | copy-start | bytes 10616836
  219.1 17.3 %copy-start.43 = (f32[768]{0:T(1024)S(1)}, f32[768]{0:T(1024)}, u32[]{:S(2)}) copy-start(f32[768]{0:T(1024)} %param.35) | copy-start | bytes 9220
  219.1 17.3 %copy-start.44 = (f32[1024,768]{1,0:T(8,128)S(1)}, f32[1024,768]{1,0:T(8,128)}, u32[]{:S(2)}) copy-start(f32[1024,768]{1,0:T(8,128)} %get-tuple-element.388) | copy-start | bytes 9437188
  236.3 3.5 copy-start.9
  288.4 17.0 %all-to-all-start.10 = ((bf16[4,192,1024]{2,1,0:T(8,128)(2,1)}), bf16[4,192,1024]{2,1,0:T(8,128)(2,1)}, u32[]{:S(2)}, u32[]{:S(2)}) async-start(bf16[4,192,1024]{2,1,0:T(8,128)(2,1)} %broadcast_in_dim.98), calls=%async_computation.10 | async-start | bytes 3145728 | tf_op jit(solution)/shard_map/all_to_all | solution.py:26
  292.8 149.6 %reduce-scatter.2.cloned.1.call-start = ((), (), s32[]{:S(2)}) async-start(), calls=%async_computation.15 | async-start | bytes 3649536 | tf_op jit(solution)/shard_map/reduce_scatter | solution.py:85
  294.8 4.6 %copy-start.8 = (bf16[4,192,1024]{2,1,0:T(8,128)(2,1)S(1)}, bf16[4,192,1024]{2,1,0:T(8,128)(2,1)}, u32[]{:S(2)}) copy-start(bf16[4,192,1024]{2,1,0:T(8,128)(2,1)} %copy-done.7) | copy-start | bytes 4718596
  294.8 4.6 %copy-start.47 = (bf16[1024,768]{1,0:T(8,128)(2,1)S(1)}, bf16[1024,768]{1,0:T(8,128)(2,1)}, u32[]{:S(2)}) copy-start(bf16[1024,768]{1,0:T(8,128)(2,1)} %copy-done.46) | copy-start | bytes 4718596
  340.3 4.6 %copy-start.1 = (bf16[2,16,24,768]{3,2,1,0:T(8,128)(2,1)S(1)}, bf16[2,16,24,768]{3,2,1,0:T(8,128)(2,1)}, u32[]{:S(2)}) copy-start(bf16[2,16,24,768]{3,2,1,0:T(8,128)(2,1)} %copy.82) | copy-start | bytes 3538948
  340.3 4.6 %copy-start.4 = (bf16[2,16,24,192]{3,2,1,0:T(8,128)(2,1)S(1)}, bf16[2,16,24,192]{3,2,1,0:T(8,128)(2,1)}, u32[]{:S(2)}) copy-start(bf16[2,16,24,192]{3,2,1,0:T(8,128)(2,1)} %copy.80) | copy-start | bytes 884740
  351.3 22.5 %copy-start.19 = (bf16[1024,3,64]{0,2,1:T(8,128)(2,1)S(1)}, bf16[1024,3,64]{0,2,1:T(8,128)(2,1)}, u32[]{:S(2)}) copy-start(bf16[1024,3,64]{0,2,1:T(8,128)(2,1)} %copy-done.18) | copy-start | bytes 1179652
  353.4 28.9 %all-to-all-start.12 = ((f32[32,1,2304]{2,1,0:T(1,128)}), f32[32,1,2304]{2,1,0:T(1,128)S(1)}, u32[]{:S(2)}, u32[]{:S(2)}) async-start(f32[32,1,2304]{2,1,0:T(1,128)} %broadcast_in_dim.102), calls=%async_computation.13 | async-start | bytes 589824 | tf_op jit(solution)/shard_map/all_to_all | solution.py:26
  382.3 45.6 %all-to-all-start.11 = ((f32[4,192,1024]{2,1,0:T(8,128)}), f32[4,192,1024]{2,1,0:T(8,128)}, u32[]{:S(2)}, u32[]{:S(2)}) async-start(f32[4,192,1024]{2,1,0:T(8,128)} %bitcast.174), calls=%async_computation.11 | async-start | bytes 6291456 | tf_op jit(solution)/shard_map/all_to_all | solution.py:49
  387.0 43.2 %copy-start.26 = (f32[192]{0:T(256)S(1)}, f32[192]{0:T(256)}, u32[]{:S(2)}) copy-start(f32[192]{0:T(256)} %param.32) | copy-start | bytes 2308
  (29 other events, 44.7 us)
Sparse Core Ops, SparseCore 0:
  10.8 51.9 all-gather.1
  351.4 90.8 reduce-scatter.1
where the time goes:
time: 459 us; the launch traced here: 457 us
  blocking collectives  202 us (44%)
  waiting for transfers between devices  71.6 us (16%)
  matrix products  49.8 us (11%)
  starting transfers between devices  43.2 us (9%)
  local copies, waits for them, and re-layouts  37.9 us (8%)
  other arithmetic  33.6 us (7%)
  between operations  18.6 us (4%)
    psum x8, blocking collectives, over_axes(): return functools.reduce(lax.psum, axes, shard)  72.2 us
    all_to_all x2, blocking collectives, sum_at_owner(): pieces = lax.all_to_all(split_up(shard, dim, size), axis, 0, 0, tiled=True)  70.8 us
    all_to_all x5, blocking collectives, sent_to_all(): lax.all_to_all(jnp.broadcast_to(shard[None], (size, *shard.shape)), axis,...  54.6 us
    all_to_all x4, starting transfers between devices, sent_to_all(): lax.all_to_all(jnp.broadcast_to(shard[None], (size, *shard.shape)), axis,...  33.8 us
    all_to_all x4, waiting for transfers between devices, sent_to_all(): lax.all_to_all(jnp.broadcast_to(shard[None], (size, *shard.shape)), axis,...  27.4 us
    all_gather x1, waiting for transfers between devices, sent_together(): whole, at, done = (lax.all_gather(both, axis, axis=dim, tiled=True), 0, [])  25.7 us
    dot_general x4, matrix products, across_features(): lax.dot_general(feature_rows, matrix, (((0,), (0,)), ((), ())), preferred...  12.3 us
    reduce_scatter x1, waiting for transfers between devices, in_one_piece(): lax.psum_scatter(both, axis, scatter_dimension=dim, tiled=True)  11 us
  transfers between devices with their start and end apart: 8, of which 6 were waited for; matrix products, arithmetic and copies ran while one was open for 5% of the time, Pallas kernels for 0%

commit v1 on v0

v1 whole, which is shorter than its diff:
```python
import jax
import jax.numpy as jnp
from jax import lax
from jax.experimental import pallas as pl
from jax.experimental.pallas import tpu as pltpu
from jax.sharding import Mesh
from jax.sharding import PartitionSpec as P

D = 768
FF = 3072
LEN = 1024
HD = 64
HEADS = 3
C = 192
TOK = 256
RB = 48
SLOTS = 32768
EPS = 1e-12
MASK = -1e30
ROOT_HALF = 0.7071067811865476
INV_ROOT_TAU = 0.3989422804014327
AXES = ("dp", "row_0", "row_1", "col")
ROW = ("row_0", "row_1")
DP_ROW = ("dp", "row_0", "row_1")
N_SEM = 192
f32 = jnp.float32
bf16 = jnp.bfloat16


def mm(a, b):
    return lax.dot_general(a, b, (((1,), (0,)), ((), ())), preferred_element_type=f32)


def mt(a, b):
    return lax.dot_general(a, b, (((1,), (1,)), ((), ())), preferred_element_type=f32)


def transposed(a):
    return jnp.transpose(a, (1, 0))


class Sent:
    def __init__(self, copy):
        self.copy, self.open_send, self.open_recv = copy, True, True

    def wait_send(self):
        if self.open_send:
            self.copy.wait_send()
        self.open_send = False

    def wait_recv(self):
        if self.open_recv:
            self.copy.wait_recv()
        self.open_recv = False

    def wait(self):
        self.wait_send()
        self.wait_recv()


class Links:
    def __init__(self, ssem, rsem):
        self.ssem, self.rsem, self.n, self.all = ssem, rsem, 0, []

    def send(self, src, dst, dev):
        copy = pltpu.make_async_remote_copy(
            src_ref=src,
            dst_ref=dst,
            send_sem=self.ssem.at[self.n],
            recv_sem=self.rsem.at[self.n],
            device_id=dev,
            device_id_type=pl.DeviceIdType.MESH,
        )
        copy.start()
        self.n += 1
        self.all.append(Sent(copy))
        return self.all[-1]


def layer(
    x_in, t_in, len_in, wqkv_in, wo_in, up_in, down_in, vec_in, ub_in,
    out_o, gi_o, dw2_o, dwo_o, dqkv_o, sv_o, svq_o,
    xf, tf, wqkv, wo, w2, vec, ub, vcol, qkvt, ktm, qaug, vaug, vtm, pst, linv,
    ctxt, ctxa, hid, nrm, sg, bstore, astore, slope, brecv, arecv,
    g2, go, gq, dctx, dct, outt, delta,
    dqkvt, dxp, dxo, rx, r1, s1, r2, s2, r3, ro1, so1, ro2, so2, ro3, rq1, sq1, rq2,
    x1, xo1, xq1, gcol, sv, rsv, wown,
    lsem, ssem, rsem,
):
    d = lax.axis_index("dp")
    y = lax.axis_index("row_0")
    x = lax.axis_index("row_1")
    c = lax.axis_index("col")
    e = 1 - d
    r = 4 * y + x
    a_me = x * e + y * d
    b_me = y * e + x * d

    def ridx(a, b):
        return (4 * b + a) * e + (4 * a + b) * d

    def zdev(k):
        return {"col": lax.rem(c + k, 4)}

    def adev(k):
        return {"row_0": lax.rem(y + k * d, 4), "row_1": lax.rem(x + k * e, 4)}

    def bdev(k):
        return {"row_0": lax.rem(y + k * e, 4), "row_1": lax.rem(x + k * d, 4)}

    sib = {"dp": e}
    links = Links(ssem, rsem)

    def rows48(i):
        return pl.ds(pl.multiple_of(i * RB, 16), RB)

    n_local = [0]

    def local(src, dst):
        copy = pltpu.make_async_copy(src, dst, lsem.at[n_local[0]])
        copy.start()
        n_local[0] += 1
        return copy

    xrows = pl.ds(pl.multiple_of(c * C, 16), C)
    cx = local(x_in, xf.at[xrows])
    cq = local(wqkv_in, wqkv.at[rows48(r)])
    cup = local(up_in, wown.at[0])
    cdn = local(down_in, wown.at[1])
    cwo = local(wo_in, wo.at[r, c])
    cvec = local(vec_in, vec.at[c])
    cub = local(ub_in, ub.at[c])
    tcols = pl.ds(pl.multiple_of(c * TOK, 128), TOK)
    ct = local(t_in.at[:, tcols], tf.at[c])
    bar = pltpu.get_barrier_semaphore()
    for k in (1, 2, 3):
        for dev in (zdev(k), adev(k), bdev(k)):
            pl.semaphore_signal(bar, inc=1, device_id=dev, device_id_type=pl.DeviceIdType.MESH)
    pl.semaphore_signal(bar, inc=1, device_id=sib, device_id_type=pl.DeviceIdType.MESH)
    pl.semaphore_wait(bar, 10)

    def xhalf(i, top):
        return xf.at[pl.ds(pl.multiple_of(i * C + (0 if top else C // 2), 16), C // 2)]

    cx.wait()
    xs = {}
    for k, order in ((1, (True, False)), (3, (False, True))):
        for top in order:
            xs[k, top] = links.send(xhalf(c, top), xhalf(c, top), zdev(k))
    cq.wait()
    qa = [links.send(wqkv.at[rows48(r)], wqkv.at[rows48(r)], adev(k)) for k in (1, 2, 3)]
    cwo.wait()
    oz = [links.send(wo.at[r, c], wo.at[r, c], zdev(k)) for k in (1, 2, 3)]
    cvec.wait()
    vz = [links.send(vec.at[c], vec.at[c], zdev(k)) for k in (1, 2, 3)]
    cub.wait()
    uz = [links.send(ub.at[c], ub.at[c], zdev(k)) for k in (1, 2, 3)]
    cup.wait()
    cdn.wait()
    own_cols = pl.ds(pl.multiple_of(c * D, 128), D)
    wz = []
    for k in (1, 2, 3):
        wz.append(links.send(wown.at[d], w2.at[d, r, :, own_cols], zdev(k)))
    w2[d, r, :, own_cols] = wown[d]
    xs[1, True].wait_recv()
    left = lax.rem(c + 3, 4)
    xs["f", 1] = links.send(xhalf(left, True), xhalf(left, True), zdev(1))
    xs[3, False].wait_recv()
    right = lax.rem(c + 1, 4)
    xs["f", 3] = links.send(xhalf(right, False), xhalf(right, False), zdev(3))
    for copy in oz:
        copy.wait_recv()
    oa = [links.send(wo.at[r], wo.at[r], adev(k)) for k in (1, 2, 3)]
    for copy in qa:
        copy.wait_recv()
    qb = []
    for k in (1, 2, 3):
        for j in range(4):
            ref = wqkv.at[rows48(ridx(j, b_me))]
            qb.append(links.send(ref, ref, bdev(k)))
    for copy in wz:
        copy.wait_recv()
    wa = [links.send(w2.at[d, r], w2.at[d, r], adev(k)) for k in (1, 2, 3)]
    w_sib = [links.send(w2.at[d, r], w2.at[d, r], sib)]
    for copy in oa:
        copy.wait_recv()
    ob = []
    for k in (1, 2, 3):
        for j in range(4):
            ref = wo.at[ridx(j, b_me)]
            ob.append(links.send(ref, ref, bdev(k)))
    for copy in wa:
        copy.wait_recv()
    wb = []
    for k in (1, 2, 3):
        for j in range(4):
            ref = w2.at[d, ridx(j, b_me)]
            wb.append(links.send(ref, ref, bdev(k)))
    for k in (1, 2, 3):
        i = ridx(lax.rem(a_me + 4 - k, 4), b_me)
        w_sib.append(links.send(w2.at[d, i], w2.at[d, i], sib))

    for copy in vz + uz:
        copy.wait_recv()
    for i in range(4):
        vcol[i * C : (i + 1) * C, 0:16] = transposed(vec[i])
    vown = transposed(vec[c])
    length = len_in[0]

    for key in ((1, False), (3, True), ("f", 1), ("f", 3)):
        xs[key].wait_recv()
    for copy in qb:
        copy.wait_recv()
    wq_t = transposed(wqkv[:, 0:C])
    wk_t = transposed(wqkv[:, C : 2 * C])
    wv_t = transposed(wqkv[:, 2 * C :])
    dxp[0, :, 0:D] = wq_t
    dxp[1, :, 0:D] = wk_t
    dxp[2, :, 0:D] = wv_t
    q_bias = vown[:, 10:11]
    v_bias = vown[:, 11:12]
    lane_iota = lax.broadcasted_iota(jnp.int32, (1, TOK), 1)
    first_row = lax.broadcasted_iota(jnp.int32, (HD, TOK), 0) == 0

    def qkv_chunk(i, carry):
        cols = pl.ds(pl.multiple_of(i * TOK, 128), TOK)
        tok = xf[:, cols]
        q = (mm(dxp[0, :, 0:D], tok) + q_bias).astype(bf16)
        k = mm(dxp[1, :, 0:D], tok).astype(bf16)
        v = (mm(dxp[2, :, 0:D], tok) + v_bias).astype(bf16)
        q = (q.astype(f32) * (HD**-0.5)).astype(bf16)
        qkvt[0:C, cols] = q
        qkvt[C : 2 * C, cols] = k
        bias = jnp.where(lane_iota + i * TOK < length, 0.0, MASK)
        bias = jnp.where(first_row, jnp.broadcast_to(bias, (HD, TOK)), 0.0).astype(bf16)
        ones = jnp.where(first_row, 1.0, 0.0).astype(bf16)
        for h in range(HEADS):
            hs = slice(h * HD, (h + 1) * HD)
            qaug[h, 0:HD, cols] = q[hs]
            qaug[h, HD : 2 * HD, cols] = ones
            vaug[h, 0:HD, cols] = v[hs]
            vaug[h, HD : HD + 16, cols] = ones[0:16]
            ktm[h, cols, :] = transposed(jnp.concatenate([k[hs], bias], axis=0))
            vtm[h, cols, :] = transposed(jnp.concatenate([v[hs], ones], axis=0))
        return carry

    lax.fori_loop(0, 4, qkv_chunk, 0)

    def fwd_tile(n, carry):
        h = n // 4
        cols = pl.ds(pl.multiple_of(lax.rem(n, 4) * TOK, 128), TOK)
        score = mm(ktm[h], qaug[h, :, cols])
        top = jnp.max(score, axis=0, keepdims=True)
        probs = jnp.exp(score - top).astype(bf16)
        pst[h, :, cols] = probs
        both = mm(vaug[h], probs)
        inv = 1.0 / both[HD : HD + 1]
        linv[h, 0:1, cols] = inv
        ctxt[pl.ds(pl.multiple_of(h * HD, 16), HD), cols] = (both[0:HD] * inv).astype(bf16)
        return carry

    lax.fori_loop(0, 4 * HEADS, fwd_tile, 0)

    cc = []
    ctxa[c] = ctxt[:, tcols]
    for k in (1, 2, 3):
        there = pl.ds(pl.multiple_of(lax.rem(c + k, 4) * TOK, 128), TOK)
        cc.append(links.send(ctxt.at[:, there], ctxa.at[c], zdev(k)))
    tt = []
    ct.wait()
    for k in (1, 2, 3):
        there = pl.ds(pl.multiple_of(lax.rem(c + k, 4) * TOK, 128), TOK)
        tt.append(links.send(t_in.at[:, there], tf.at[c], zdev(k)))
    for copy in ob:
        copy.wait_recv()
    for k in (1, 2, 3):
        for j in range(4):
            wb[4 * (k - 1) + j].wait_recv()
            i = ridx(j, lax.rem(b_me + 4 - k, 4))
            w_sib.append(links.send(w2.at[d, i], w2.at[d, i], sib))
    for copy in cc:
        copy.wait_recv()

    def proj(i, carry):
        row = pl.ds(pl.multiple_of(i * C, 16), C)
        blocks = wo[pl.ds(i * 4, 4)]
        acc = xf[row, tcols].astype(f32) + vcol[row, 0:1]
        for j in range(4):
            acc = acc + mm(blocks[:, j].reshape(C, C), ctxa[j])
        hid[row] = acc
        return carry

    lax.fori_loop(0, 4, proj, 0)

    def norm_stats(ref):
        v = ref[...]
        mean = jnp.sum(v, axis=0, keepdims=True) * (1.0 / D)
        square = jnp.sum(v * v, axis=0, keepdims=True) * (1.0 / D)
        return mean, lax.rsqrt(square - mean * mean + EPS)

    mean1, inv1 = norm_stats(hid)

    def norm1(i, carry):
        row = pl.ds(pl.multiple_of(i * C, 16), C)
        n = (hid[row] - mean1) * inv1
        nrm[row] = n
        h = n * vcol[row, 1:2] + vcol[row, 2:3]
        hid[row] = h
        astore[0, row] = h.astype(bf16)
        return carry

    lax.fori_loop(0, 4, norm1, 0)
    outt[...] = transposed(astore[0])

    for copy in w_sib:
        copy.wait_recv()

    def up_chunk(i, carry):
        cols = pl.ds(pl.multiple_of(i * D, 128), D)
        pre = mm(outt[...], w2[0, :, :, cols].reshape(D, D)) + ub[i, 0:1]
        half = 0.5 * (1.0 + lax.erf(pre * ROOT_HALF))
        bstore[1, :, cols] = (pre * half).astype(bf16)
        slope[:, cols] = half + pre * jnp.exp(-0.5 * pre * pre) * INV_ROOT_TAU
        return carry

    lax.fori_loop(0, 4, up_chunk, 0)

    def down_chunk(i, carry):
        row = pl.ds(pl.multiple_of(i * C, 16), C)
        w = w2[1, pl.ds(i * 4, 4)].reshape(C, FF)
        hid[row] = hid[row] + mt(w, bstore[1]) + vcol[row, 3:4]
        return carry

    lax.fori_loop(0, 4, down_chunk, 0)

    mean2, inv2 = norm_stats(hid)
    for copy in tt:
        copy.wait_recv()
    valid = lane_iota + c * TOK < length
    gcol[...] = jnp.zeros(gcol.shape, f32)

    def norm2(i, carry):
        total, crossed, loss = carry
        row = pl.ds(pl.multiple_of(i * C, 16), C)
        n = (hid[row] - mean2) * inv2
        hid[row] = n
        final = n * vcol[row, 4:5] + vcol[row, 5:6]
        delta[row] = final.astype(bf16)
        g = jnp.where(valid, final - tf[i].astype(f32), 0.0)
        gcol[row, 4:5] = jnp.sum(g * n, axis=1, keepdims=True)
        gcol[row, 5:6] = jnp.sum(g, axis=1, keepdims=True)
        s = g * vcol[row, 4:5]
        sg[row] = s
        return (
            total + jnp.sum(s, axis=0, keepdims=True),
            crossed + jnp.sum(s * n, axis=0, keepdims=True),
            loss + jnp.sum(g * g, axis=0, keepdims=True),
        )

    zero = jnp.zeros((1, TOK), f32)
    total2, crossed2, loss_row = lax.fori_loop(0, 4, norm2, (zero, zero, zero))
    fo = []
    out_o_own = local(delta.at[xrows], out_o.at[:, tcols])
    for k in (1, 2, 3):
        there = pl.ds(pl.multiple_of(lax.rem(c + k, 4) * C, 16), C)
        fo.append(links.send(delta.at[there], out_o.at[:, tcols], zdev(k)))

    def norm2_back(i, carry):
        row = pl.ds(pl.multiple_of(i * C, 16), C)
        s = inv2 * (sg[row] - total2 * (1.0 / D) - hid[row] * (crossed2 * (1.0 / D)))
        sg[row] = s
        low = s.astype(bf16)
        astore[1, row] = low
        gcol[row, 3:4] = jnp.sum(low.astype(f32), axis=1, keepdims=True)
        return carry

    lax.fori_loop(0, 4, norm2_back, 0)
    outt[...] = transposed(astore[1])

    def act_chunk(i, carry):
        cols = pl.ds(pl.multiple_of(i * D, 128), D)
        g = mm(outt[...], w2[1, :, :, cols].reshape(D, D)) * slope[:, cols]
        low = g.astype(bf16)
        bstore[0, :, cols] = low
        sv[pl.ds(8 + i, 1)] = jnp.sum(low.astype(f32), axis=0, keepdims=True)
        return carry

    lax.fori_loop(0, 4, act_chunk, 0)
    ex = [
        links.send(astore.at[e], arecv, sib),
        links.send(bstore.at[e], brecv, sib),
    ]

    def hidden_back(i, carry):
        total, crossed = carry
        row = pl.ds(pl.multiple_of(i * C, 16), C)
        w = w2[0, pl.ds(i * 4, 4)].reshape(C, FF)
        g = sg[row] + mt(w, bstore[0])
        n = nrm[row]
        gcol[row, 1:2] = jnp.sum(g * n, axis=1, keepdims=True)
        gcol[row, 2:3] = jnp.sum(g, axis=1, keepdims=True)
        s = g * vcol[row, 1:2]
        sg[row] = s
        return (
            total + jnp.sum(s, axis=0, keepdims=True),
            crossed + jnp.sum(s * n, axis=0, keepdims=True),
        )

    total1, crossed1 = lax.fori_loop(0, 4, hidden_back, (zero, zero))

    def norm1_back(i, carry):
        row = pl.ds(pl.multiple_of(i * C, 16), C)
        s = inv1 * (sg[row] - total1 * (1.0 / D) - nrm[row] * (crossed1 * (1.0 / D)))
        sg[row] = s
        low = s.astype(bf16)
        delta[row] = low
        gcol[row, 0:1] = jnp.sum(low.astype(f32), axis=1, keepdims=True)
        return carry

    for copy in fo:
        copy.wait_send()
    out_o_own.wait()
    lax.fori_loop(0, 4, norm1_back, 0)
    outt[...] = transposed(delta[...])

    for j in range(4):
        dct[j] = transposed(mm(outt[...], wo[:, j].reshape(D, C)).astype(bf16))
    dctx[:, tcols] = dct[c]
    dc = []
    for k in (1, 2, 3):
        dc.append(links.send(dct.at[lax.rem(c + k, 4)], dctx.at[:, tcols], zdev(k)))

    for copy in ex:
        copy.wait_recv()
    s1_sends = {}

    def g2_block(i, carry):
        for j in range(4):
            cols = slice(j * D, (j + 1) * D)
            row = pl.ds(pl.multiple_of(i * C, 16), C)
            g = mm(astore[d, row], bstore[d, :, cols]) + mm(arecv[row], brecv[:, cols])
            g2[pl.ds(i * 4, 4), :, cols] = g.astype(bf16).reshape(4, RB, D)
        return carry

    lax.fori_loop(0, 4, g2_block, 0)
    for j in range(4):
        for k in (1, 2, 3):
            i = ridx(j, lax.rem(b_me + k, 4))
            s1_sends[j, k] = links.send(g2.at[i], r1.at[k - 1, j], bdev(k))
    for j in range(4):
        go[:, j] = mt(delta[...], ctxa[j]).astype(bf16).reshape(16, RB, C)
    o1_sends = {}
    for j in range(4):
        for k in (1, 2, 3):
            i = ridx(j, lax.rem(b_me + k, 4))
            o1_sends[j, k] = links.send(go.at[i], ro1.at[k - 1, j], bdev(k))

    for copy in dc:
        copy.wait_recv()

    dk = jnp.zeros((HD, LEN), f32)

    def bwd_head(h, carry):
        hrow = pl.ds(pl.multiple_of(h * HD, 16), HD)
        krow = pl.ds(pl.multiple_of(C + h * HD, 16), HD)
        vrow = pl.ds(pl.multiple_of(2 * C + h * HD, 16), HD)

        def bwd_tile(n, acc):
            dk, dv = acc
            cols = pl.ds(pl.multiple_of(n * TOK, 128), TOK)
            inv = linv[h, 0:1, cols]
            dc = dctx[hrow, cols].astype(f32)
            inner = jnp.sum(dc * ctxt[hrow, cols].astype(f32), axis=0, keepdims=True) * inv
            dcs = (dc * inv).astype(bf16)
            probs = pst[h, :, cols]
            dp = mm(vtm[h, :, 0:HD], dcs) - inner
            ds = (probs.astype(f32) * dp).astype(bf16)
            dqkvt[hrow, cols] = (mm(qkvt[krow, :], ds) * (HD**-0.5)).astype(bf16)
            dk = dk + mt(qkvt[hrow, cols], ds)
            dv = dv + mt(dcs, probs)
            return dk, dv

        dk, dv = lax.fori_loop(
            0, 4, bwd_tile, (jnp.zeros((HD, LEN), f32), jnp.zeros((HD, LEN), f32))
        )
        dqkvt[krow] = dk.astype(bf16)
        dqkvt[vrow] = dv.astype(bf16)
        return carry

    lax.fori_loop(0, HEADS, bwd_head, 0)

    xsend = []

    def dx_part(i):
        row = pl.ds(pl.multiple_of(i * C, 16), C)
        return row, mm(wqkv[row], dqkvt[...])

    for k in (2, 1, 3):
        i = lax.rem(c + k, 4)
        row, g = dx_part(i)
        dxo[...] = g
        dxo[:, tcols] = dxo[:, tcols] + sg[row]
        dxp[k - 1] = dxo[...].astype(bf16)
        xsend.append(links.send(dxp.at[k - 1], rx.at[k - 1], zdev(k)))
    row, g = dx_part(c)
    dxo[...] = g
    dxo[:, tcols] = dxo[:, tcols] + sg[row]

    for i in range(4):
        g = mt(xf[i * C : (i + 1) * C], dqkvt[...])
        gq[i * 4 : (i + 1) * 4] = g.astype(bf16).reshape(4, RB, 3 * C)
    q1_sends = {}
    for j in range(4):
        for k in (1, 2, 3):
            i = ridx(j, lax.rem(b_me + k, 4))
            q1_sends[j, k] = links.send(gq.at[i], rq1.at[k - 1, j], bdev(k))

    sv[0:8] = transposed(gcol[...])[0:8]
    sv[6:7] = jnp.broadcast_to(jnp.sum(loss_row, axis=1, keepdims=True), (1, D))
    sv[7:8] = jnp.broadcast_to(length.astype(f32), (1, D))
    bias_sum = mm_ones(dqkvt)
    sv[12:16] = jnp.zeros((4, D), f32)
    sv[12:13, 0 : 3 * C] = bias_sum
    v1 = [links.send(sv, rsv.at[0], sib)]
    for copy in v1:
        copy.wait()
    sv[...] = sv[...] + rsv[0]
    n_sv = 1
    for stage, dev in enumerate((adev, bdev, zdev)):
        if stage == 2:
            svq_o[...] = sv[8:16]
        vs = []
        for k in (1, 2, 3):
            vs.append(links.send(sv, rsv.at[n_sv], dev(k)))
            n_sv += 1
        for copy in vs:
            copy.wait()
        sv[...] = sv[...] + rsv[n_sv - 3] + rsv[n_sv - 2] + rsv[n_sv - 1]
    sv_o[...] = sv[...]

    def first_sums(sends, own, recv, summed, peer_recv):
        done = []
        for j in range(4):
            for k in (1, 2, 3):
                sends[j, k].wait_recv()
            i = ridx(j, b_me)
            total = own[i].astype(f32)
            for k in (1, 2, 3):
                total = total + recv[k - 1, j].astype(f32)
            summed[j] = total.astype(bf16)
        for k in (1, 2, 3):
            done.append(
                links.send(summed.at[lax.rem(a_me + k, 4)], peer_recv.at[k - 1], adev(k))
            )
        return done

    w2_sends = first_sums(s1_sends, g2, r1, s1, r2)
    o2_sends = first_sums(o1_sends, go, ro1, so1, ro2)
    q2_sends = first_sums(q1_sends, gq, rq1, sq1, rq2)

    for copy in xsend:
        copy.wait_recv()
    gi_o[...] = dxo[...] + rx[0].astype(f32) + rx[1].astype(f32) + rx[2].astype(f32)

    def second_sum(sends, summed, recv):
        for copy in sends:
            copy.wait_recv()
        total = summed[a_me].astype(f32)
        for k in range(3):
            total = total + recv[k].astype(f32)
        return total

    s2[...] = second_sum(w2_sends, s1, r2).astype(bf16)
    w3 = []
    for k in (1, 2, 3):
        there = pl.ds(pl.multiple_of(lax.rem(c + k, 4) * D, 128), D)
        w3.append(links.send(s2.at[:, there], r3.at[k - 1], zdev(k)))
    so2[...] = second_sum(o2_sends, so1, ro2).astype(bf16)
    o3 = []
    for k in (1, 2, 3):
        o3.append(links.send(so2.at[lax.rem(c + k, 4)], ro3.at[k - 1], zdev(k)))
    dqkv = second_sum(q2_sends, sq1, rq2)
    xq1[0] = dqkv
    q3 = links.send(xq1.at[0], xq1.at[1], sib)
    for copy in w3:
        copy.wait_recv()
    total = s2[:, own_cols].astype(f32)
    for k in range(3):
        total = total + r3[k].astype(f32)
    x1[0] = total
    w4 = links.send(x1.at[0], x1.at[1], sib)
    for copy in o3:
        copy.wait_recv()
    ototal = so2[c].astype(f32)
    for k in range(3):
        ototal = ototal + ro3[k].astype(f32)
    xo1[0] = ototal
    o4 = links.send(xo1.at[0], xo1.at[1], sib)
    q3.wait_recv()
    dqkv_o[...] = dqkv + xq1[1]
    w4.wait_recv()
    dw2_o[d] = total
    dw2_o[e] = x1[1]
    o4.wait_recv()
    dwo_o[...] = ototal + xo1[1]

    for copy in links.all:
        copy.wait()


def mm_ones(ref):
    ones = jnp.ones((8, LEN), bf16)
    return mt(ones, ref[...])[0:1]


def local_step(
    inputs, teacher, lengths, query_weight, query_bias, key_weight, value_weight, value_bias,
    output_weight, output_bias, first_gain, first_shift, up_weight, up_bias, down_weight,
    down_bias, second_gain, second_shift,
):
    wqkv = jnp.concatenate([query_weight, key_weight, value_weight], axis=1)
    zero = jnp.zeros_like(query_bias)
    up_rows = up_bias.reshape(4, C)
    vec = jnp.stack(
        [output_bias, first_gain, first_shift, down_bias, second_gain, second_shift,
         up_rows[0], up_rows[1], up_rows[2], up_rows[3], query_bias, value_bias,
         zero, zero, zero, zero]
    )
    ub = jnp.broadcast_to(up_bias[None], (8, D))
    anyspec = pl.BlockSpec(memory_space=pl.ANY)
    vm = pl.BlockSpec(memory_space=pltpu.VMEM)
    sds = jax.ShapeDtypeStruct
    V = pltpu.VMEM
    out, gi, dw2, dwo, dqkv, sv, svq = pl.pallas_call(
        layer,
        name="layer",
        out_shape=(
            sds((C, LEN), bf16),
            sds((C, LEN), f32),
            sds((2, RB, D), f32),
            sds((RB, C), f32),
            sds((RB, 3 * C), f32),
            sds((16, D), f32),
            sds((8, D), f32),
        ),
        in_specs=[
            anyspec, anyspec, pl.BlockSpec(memory_space=pltpu.SMEM),
            anyspec, anyspec, anyspec, anyspec, anyspec, anyspec,
        ],
        out_specs=(anyspec, vm, vm, vm, vm, vm, vm),
        scratch_shapes=[
            V((D, LEN), bf16),
            V((4, C, TOK), bf16),
            V((D, 3 * C), bf16),
            V((16, 4, RB, C), bf16),
            V((2, 16, RB, FF), bf16),
            V((4, 16, C), f32),
            V((4, 8, D), f32),
            V((D, 128), f32),
            V((2 * C, LEN), bf16),
            V((HEADS, LEN, 2 * HD), bf16),
            V((HEADS, 2 * HD, LEN), bf16),
            V((HEADS, HD + 16, LEN), bf16),
            V((HEADS, LEN, 2 * HD), bf16),
            V((HEADS, LEN, LEN), bf16),
            V((HEADS, 8, LEN), f32),
            V((C, LEN), bf16),
            V((4, C, TOK), bf16),
            V((D, TOK), f32),
            V((D, TOK), f32),
            V((D, TOK), f32),
            V((2, TOK, FF), bf16),
            V((2, D, TOK), bf16),
            V((TOK, FF), f32),
            V((TOK, FF), bf16),
            V((D, TOK), bf16),
            V((16, RB, FF), bf16),
            V((16, 4, RB, C), bf16),
            V((16, RB, 3 * C), bf16),
            V((C, LEN), bf16),
            V((4, C, TOK), bf16),
            V((TOK, D), bf16),
            V((D, TOK), bf16),
            V((3 * C, LEN), bf16),
            V((3, C, LEN), bf16),
            V((C, LEN), f32),
            V((3, C, LEN), bf16),
            V((3, 4, RB, FF), bf16),
            V((4, RB, FF), bf16),
            V((3, RB, FF), bf16),
            V((RB, FF), bf16),
            V((3, RB, D), bf16),
            V((3, 4, 4, RB, C), bf16),
            V((4, 4, RB, C), bf16),
            V((3, 4, RB, C), bf16),
            V((4, RB, C), bf16),
            V((3, RB, C), bf16),
            V((3, 4, RB, 3 * C), bf16),
            V((4, RB, 3 * C), bf16),
            V((3, RB, 3 * C), bf16),
            V((2, RB, D), f32),
            V((2, RB, C), f32),
            V((2, RB, 3 * C), f32),
            V((D, 128), f32),
            V((16, D), f32),
            V((10, 16, D), f32),
            V((2, RB, D), bf16),
            pltpu.SemaphoreType.DMA((12,)),
            pltpu.SemaphoreType.DMA((N_SEM,)),
            pltpu.SemaphoreType.DMA((N_SEM,)),
        ],
        compiler_params=pltpu.CompilerParams(
            collective_id=0, has_side_effects=True, vmem_limit_bytes=62 * 2**20
        ),
    )(inputs, teacher, lengths, wqkv, output_weight.T, up_weight, down_weight, vec, ub)
    c = lax.axis_index("col")
    count = sv[7, 0] * 0.25
    factor = SLOTS / count
    loss = sv[6, 0] / (2.0 * D * count)
    mine = lax.dynamic_slice_in_dim(sv[0:6], c * C, C, axis=1) * factor
    up_b = lax.dynamic_slice_in_dim(sv[8:12], c, 1, axis=0)[0] * factor
    dqkv = dqkv * factor
    bq = svq[4] * factor
    return (
        out,
        loss,
        gi * factor,
        dqkv[:, :C],
        bq[0:C],
        dqkv[:, C : 2 * C],
        dqkv[:, 2 * C :],
        bq[2 * C : 3 * C],
        dwo.T * factor,
        mine[0],
        mine[1],
        mine[2],
        dw2[0] * factor,
        up_b,
        dw2[1] * factor,
        mine[3],
        mine[4],
        mine[5],
    )


def solution(mesh):
    split = Mesh(
        mesh.devices.reshape(mesh.shape["dp"], 4, 4, mesh.shape["col"]), AXES
    )
    tokens = P("col", DP_ROW)
    weight = P(ROW, "col")
    vector = P("col")
    return jax.shard_map(
        local_step,
        mesh=split,
        in_specs=(
            tokens, tokens, P(DP_ROW), weight, vector, weight, weight, vector,
            P("col", ROW), vector, vector, vector, weight, vector, weight,
            vector, vector, vector,
        ),
        out_specs=(
            tokens, P(), tokens, weight, vector, weight, weight, vector,
            P("col", ROW), vector, vector, vector, weight, vector, weight,
            vector, vector, vector,
        ),
        check_vma=False,
    )
```

time: 459 us -> 184 us (0.40)
  blocking collectives: 202 us -> 0 us
  Pallas kernels: 0 us -> 162 us
  waiting for transfers between devices: 71.6 us -> 0 us
  matrix products: 49.8 us -> 0 us
  starting transfers between devices: 43.2 us -> 0 us
  local copies, waits for them, and re-layouts: 37.9 us -> 9.51 us
  other arithmetic: 33.6 us -> 7.21 us
  between operations: 18.6 us -> 4.51 us
    pallas_call x0 -> x1, Pallas kernels: none -> 162 us  [local_step(): pl.pallas_call(layer, name='layer', out_shape=(sds((C, LEN), bf16), sds((...]
    all_to_all x7 -> x0, blocking collectives: 125 us -> none  [the longest x2 70.8 us: sum_at_owner(): pieces = lax.all_to_all(split_up(shard, dim, size), axis, 0, 0, tiled=True)]
    psum x8 -> x0, blocking collectives: 72.2 us -> none  [over_axes(): return functools.reduce(lax.psum, axes, shard)]
    dot_general x26 -> x0, matrix products: 49.8 us -> none  [the longest x4 12.3 us: across_features(): lax.dot_general(feature_rows, matrix, (((0,), (0,)), ((), ())), preferred...]
    all_to_all x6 -> x0, starting transfers between devices: 43.1 us -> none  [the longest x4 33.8 us: sent_to_all(): lax.all_to_all(jnp.broadcast_to(shard[None], (size, *shard.shape)), axis,...]
    all_to_all x6 -> x0, waiting for transfers between devices: 34.8 us -> none  [the longest x4 27.4 us: sent_to_all(): lax.all_to_all(jnp.broadcast_to(shard[None], (size, *shard.shape)), axis,...]
    all_gather x1 -> x0, waiting for transfers between devices: 25.7 us -> none  [sent_together(): whole, at, done = (lax.all_gather(both, axis, axis=dim, tiled=True), 0, [])]
    reduce_sum x18 -> x0, other arithmetic: 24.5 us -> none  [the longest x4 10.8 us: sum_at_owner(): return jnp.sum(pieces, axis=0)]
  transfers between devices with their start and end apart: 8 -> 0, of which waited for: 6 -> 0; matrix products, arithmetic and copies ran while one was open for 5% -> 0% of each run, Pallas kernels for 0% -> 0%
where the time goes in v1:
time: 184 us; the launch traced here: 183 us
  Pallas kernels  162 us (88%)
  local copies, waits for them, and re-layouts  9.51 us (5%)
  other arithmetic  7.21 us (4%)
  between operations  4.51 us (2%)
    pallas_call x1, Pallas kernels, local_step(): pl.pallas_call(layer, name='layer', out_shape=(sds((C, LEN), bf16), sds((...  162 us

profile of v1, /device:TPU:1, one launch (start us, length us, event | category | flops | bytes accessed | tf_op | source)
XLA Modules:
  0.0 182.9 jit_solution(8874293831283304166)
XLA Ops:
  0.7 0.0 copy-start.4
  0.7 0.9 fusion.3
  1.6 0.0 copy-start.6
  1.6 0.0 copy-start.3
  1.6 0.0 copy-start.2
  1.6 0.6 copy-done.6
  2.3 0.0 copy-done.7
  2.3 2.6 %stack.39.vec_in = f32[16,192]{1,0:T(8,128)} concatenate(f32[1,192]{1,0:T(1,128)S(1)} %bitcast.34, f32[1,192]{1,0:T(1,128)S(1)} %bitcast.35, f32[1,192]{1,0:T(1,128)} %bitcast.36, f32[1,192]{1,0:T(1,128)} %bitcast.37, f32[1,192]{1,0:T(1,128)} %bitcast.38, f32[1,192]{1,0:T(1,128)} %bitcast.39, f32[1,192]{1,0:T(1,128)S(1)} %bitcast.33, f32[1,192]{1,0:T(1,128)S(1)} %bitcast.32, ...), dimensions={0} | concatenate | bytes 24576 | tf_op jit(solution)/shard_map/stack | solution.py:624
  4.9 0.0 copy-done.4
  4.9 0.0 copy-done.3
  4.9 0.0 copy-done.2
  4.9 0.0 copy-start.5
  4.9 0.7 pad_maximum_fusion.wqkv_in
  5.7 0.0 copy-done.5
  5.7 0.6 broadcast_in_dim.2.ub_in
  6.9 161.7 %layer.1 = (bf16[192,1024]{1,0:T(8,128)(2,1)}, f32[192,1024]{1,0:T(8,128)}, f32[2,48,768]{2,1,0:T(8,128)}, f32[48,192]{1,0:T(8,128)}, f32[48,576]{1,0:T(8,128)}, /*index=5*/f32[16,768]{1,0:T(8,128)}, f32[8,768]{1,0:T(8,128)}) custom-call(bf16[192,1024]{1,0:T(8,128)(2,1)} %x_in.1, bf16[192,1024]{1,0:T(8,128)(2,1)} %t_in.1, s32[1]{0:T(128)S(6)} %copy.37.len_in, ...), custom_call_target="tpu_custom_call" | custom-call | tf_op jit(solution)/shard_map/layer/pallas_call | solution.py:634
  168.6 0.0 copy-start
  168.6 1.3 fusion.1
  170.6 0.9 broadcast_multiply_fusion.1
  171.5 1.5 fusion
  173.0 0.7 slice.107
  173.7 1.3 multiply_reduce_fusion
  175.1 0.6 fusion.4
  175.6 0.7 slice.102
  176.4 0.1 dynamic-slice_multiply_fusion
  176.5 0.6 fusion.2
  177.1 1.7 multiply_bitcast_fusion
  178.8 0.0 copy-done
  178.8 0.0 copy-start.1
  178.8 0.9 broadcast_multiply_fusion
  181.0 0.0 copy-done.1
  181.0 0.7 copy.38
  (2 shorter events, 0.0 us)
Async XLA Ops:
  0.7 4.3 %copy-start.4 = (bf16[48,192]{1,0:T(8,128)(2,1)S(1)}, bf16[48,192]{1,0:T(8,128)(2,1)}, u32[]{:S(2)}) copy-start(bf16[48,192]{1,0:T(8,128)(2,1)} %param.21) | copy-start | bytes 55300
  1.6 0.7 copy-start.6
  1.6 0.7 copy-start.7
  1.6 3.3 %copy-start.3 = (bf16[48,192]{1,0:T(8,128)(2,1)S(1)}, bf16[48,192]{1,0:T(8,128)(2,1)}, u32[]{:S(2)}) copy-start(bf16[48,192]{1,0:T(8,128)(2,1)} %param.23) | copy-start | bytes 55300
  1.6 3.3 %copy-start.2 = (bf16[48,192]{1,0:T(8,128)(2,1)S(1)}, bf16[48,192]{1,0:T(8,128)(2,1)}, u32[]{:S(2)}) copy-start(bf16[48,192]{1,0:T(8,128)(2,1)} %param.24) | copy-start | bytes 55300
  4.9 0.7 copy-start.5
  168.6 10.2 %copy-start = (f32[192,1024]{1,0:T(8,128)S(1)}, f32[192,1024]{1,0:T(8,128)}, u32[]{:S(2)}) copy-start(f32[192,1024]{1,0:T(8,128)} %get-tuple-element.27) | copy-start | bytes 2359300
  178.8 2.2 %copy-start.1 = (bf16[192,1024]{1,0:T(8,128)(2,1)S(1)}, bf16[192,1024]{1,0:T(8,128)(2,1)}, u32[]{:S(2)}) copy-start(bf16[192,1024]{1,0:T(8,128)(2,1)} %get-tuple-element.72) | copy-start | bytes 1179652

commit v2 on v1

v2 whole, which is shorter than its diff:
```python
import jax
import jax.numpy as jnp
from jax import lax
from jax.experimental import pallas as pl
from jax.experimental.pallas import tpu as pltpu
from jax.sharding import Mesh
from jax.sharding import PartitionSpec as P

D = 768
FF = 3072
LEN = 1024
HD = 64
HEADS = 3
C = 192
TOK = 256
RB = 48
SLOTS = 32768
EPS = 1e-12
MASK = -1e30
ROOT_HALF = 0.7071067811865476
INV_ROOT_TAU = 0.3989422804014327
AXES = ("dp", "row_0", "row_1", "col")
ROW = ("row_0", "row_1")
DP_ROW = ("dp", "row_0", "row_1")
N_SEM = 256
f32 = jnp.float32
bf16 = jnp.bfloat16


def mm(a, b):
    return lax.dot_general(a, b, (((1,), (0,)), ((), ())), preferred_element_type=f32)


def mt(a, b):
    return lax.dot_general(a, b, (((1,), (1,)), ((), ())), preferred_element_type=f32)


def transposed(a):
    return jnp.transpose(a, (1, 0))


class Sent:
    def __init__(self, copy):
        self.copy, self.open_send, self.open_recv = copy, True, True

    def wait_send(self):
        if self.open_send:
            self.copy.wait_send()
        self.open_send = False

    def wait_recv(self):
        if self.open_recv:
            self.copy.wait_recv()
        self.open_recv = False

    def wait(self):
        self.wait_send()
        self.wait_recv()


class Links:
    def __init__(self, ssem, rsem):
        self.ssem, self.rsem, self.n, self.all = ssem, rsem, 0, []

    def send(self, src, dst, dev):
        copy = pltpu.make_async_remote_copy(
            src_ref=src,
            dst_ref=dst,
            send_sem=self.ssem.at[self.n],
            recv_sem=self.rsem.at[self.n],
            device_id=dev,
            device_id_type=pl.DeviceIdType.MESH,
        )
        copy.start()
        self.n += 1
        self.all.append(Sent(copy))
        return self.all[-1]


def layer(
    x_in, t_in, len_in, wq_in, wk_in, wv_in, wo_in, up_in, down_in,
    ob_in, g1_in, b1_in, db_in, g2_in, b2_in, qb_in, vb_in, ub_in,
    out_o, gi_o, dw2_o, dwo_o, dqkv_o, sv_o,
    xf, tf, w2, aux, wo4, wqkvt, vec, ub, vcol, qkvt, ktm, qaug, vaug, vtm, pst, linv,
    ctxt, ctxa, hid, nrm, sg, bstore, astore, slope, brecv, arecv,
    g2, ga, gar, dctx, dct, outt, delta,
    dqkvt, dxp, dxo, rx, im, rm, s1, r2, s2, r3, ia, ra, sa1, ra2, sa2, ra3,
    x1, xa1, xo1, gcol, sv, rsv, wown,
    lsem, ssem, rsem,
):
    d = lax.axis_index("dp")
    y = lax.axis_index("row_0")
    x = lax.axis_index("row_1")
    c = lax.axis_index("col")
    e = 1 - d
    r = 4 * y + x
    a_me = x * e + y * d
    b_me = y * e + x * d
    b_left = lax.rem(b_me + 3, 4)
    b_right = lax.rem(b_me + 1, 4)
    b_far = lax.rem(b_me + 2, 4)

    def ridx(a, b):
        return (4 * b + a) * e + (4 * a + b) * d

    def zdev(k):
        return {"col": lax.rem(c + k, 4)}

    def adev(k):
        return {"row_0": lax.rem(y + k * d, 4), "row_1": lax.rem(x + k * e, 4)}

    def bdev(k):
        return {"row_0": lax.rem(y + k * e, 4), "row_1": lax.rem(x + k * d, 4)}

    sib = {"dp": e}
    links = Links(ssem, rsem)

    def wait_all(copies):
        for copy in copies:
            copy.wait_recv()

    n_local = [0]

    def local(src, dst):
        copy = pltpu.make_async_copy(src, dst, lsem.at[n_local[0]])
        copy.start()
        n_local[0] += 1
        return copy

    xrows = pl.ds(pl.multiple_of(c * C, 16), C)
    tcols = pl.ds(pl.multiple_of(c * TOK, 128), TOK)
    own_cols = pl.ds(pl.multiple_of(c * D, 128), D)
    bar = pltpu.get_barrier_semaphore()
    for k in (1, 2, 3):
        for dev in (zdev(k), adev(k), bdev(k)):
            pl.semaphore_signal(bar, inc=1, device_id=dev, device_id_type=pl.DeviceIdType.MESH)
    pl.semaphore_signal(bar, inc=1, device_id=sib, device_id_type=pl.DeviceIdType.MESH)
    cup = local(up_in, wown.at[0])
    cdn = local(down_in, wown.at[1])
    cx = local(x_in, xf.at[xrows])
    ct = local(t_in.at[:, tcols], tf.at[c])
    wo4[c] = transposed(wo_in[...])
    for i, ref in enumerate((ob_in, g1_in, b1_in, db_in, g2_in, b2_in, qb_in, vb_in)):
        vec[c, i : i + 1, :] = ref[...].reshape(1, C)
    ub[c, 0:1, :] = ub_in[...].reshape(1, D)
    own_qkv = jnp.concatenate(
        [wq_in[...], wk_in[...], wv_in[...], jnp.zeros((RB, C), bf16)], axis=1
    )
    cup.wait()
    cdn.wait()
    pl.semaphore_wait(bar, 10)

    oz = [links.send(wo4.at[c], wo4.at[c], zdev(k)) for k in (1, 3, 2)]
    wz = [links.send(wown.at[d], w2.at[d, r, :, own_cols], zdev(k)) for k in (1, 3, 2)]
    vz = [links.send(vec.at[c], vec.at[c], zdev(k)) for k in (1, 2, 3)]
    uz = [links.send(ub.at[c], ub.at[c], zdev(k)) for k in (1, 2, 3)]
    w2[d, r, :, own_cols] = wown[d]

    def xhalf(i, top):
        return xf.at[pl.ds(pl.multiple_of(i * C + (0 if top else C // 2), 16), C // 2)]

    cx.wait()
    xs = {}
    for k, order in ((1, (True, False)), (3, (False, True))):
        for top in order:
            xs[k, top] = links.send(xhalf(c, top), xhalf(c, top), zdev(k))

    def along_a(buf):
        return [links.send(buf.at[d, r], buf.at[d, r], adev(k)) for k in (1, 3, 2)]

    def block(k, b):
        return ridx(lax.rem(a_me + 4 - k, 4), b)

    def along_b(buf, k):
        ref = buf.at[d, block(k, b_me)]
        return (links.send(ref, ref, bdev(1)), links.send(ref, ref, bdev(3)))

    def to_sibling(buf, k, b):
        ref = buf.at[d, block(k, b)]
        return links.send(ref, ref, sib)

    FWD_PLUS, FWD_MINUS = (0, 2), (1, 3)

    def forward(buf, sent):
        far = {}
        for k in FWD_PLUS:
            sent[k][0].wait_recv()
            ref = buf.at[d, block(k, b_left)]
            far[k] = links.send(ref, ref, bdev(1))
        for k in FWD_MINUS:
            sent[k][1].wait_recv()
            ref = buf.at[d, block(k, b_right)]
            far[k] = links.send(ref, ref, bdev(3))
        return far

    wait_all(oz)
    own_wo = jnp.concatenate([wo4[j] for j in range(4)], axis=1)
    aux[d, r] = jnp.where(d == 0, own_qkv, own_wo)
    aux_a = along_a(aux)
    aux_b = {0: along_b(aux, 0)}
    aux_s = [to_sibling(aux, 0, b_me)]
    wait_all(wz)
    w_a = along_a(w2)
    wait_all(aux_a)
    for k in (1, 3, 2):
        aux_b[k] = along_b(aux, k)
    w_b = {0: along_b(w2, 0)}
    for k in (1, 3, 2):
        aux_s.append(to_sibling(aux, k, b_me))
    xs[1, True].wait_recv()
    left = lax.rem(c + 3, 4)
    xs["f", 1] = links.send(xhalf(left, True), xhalf(left, True), zdev(1))
    xs[3, False].wait_recv()
    right = lax.rem(c + 1, 4)
    xs["f", 3] = links.send(xhalf(right, False), xhalf(right, False), zdev(3))
    w_s = [to_sibling(w2, 0, b_me)]
    aux_far = forward(aux, aux_b)
    for i, k in enumerate((1, 3, 2)):
        w_a[i].wait_recv()
        w_b[k] = along_b(w2, k)
        w_s.append(to_sibling(w2, k, b_me))
    for k in range(4):
        aux_b[k][0].wait_recv()
        aux_s.append(to_sibling(aux, k, b_left))
        aux_b[k][1].wait_recv()
        aux_s.append(to_sibling(aux, k, b_right))
    for k in range(4):
        aux_far[k].wait_recv()
        aux_s.append(to_sibling(aux, k, b_far))

    wait_all(vz + uz)
    for i in range(4):
        vcol[i * C : (i + 1) * C, 0:16] = transposed(vec[i])
    vown = transposed(vec[c])
    length = len_in[0]

    wait_all([xs[key] for key in ((1, False), (3, True), ("f", 1), ("f", 3))])
    wait_all(aux_s)
    for i in range(3):
        wqkvt[i] = transposed(aux[0].reshape(D, D)[:, i * C : (i + 1) * C])
    q_bias = vown[:, 6:7]
    v_bias = vown[:, 7:8]
    lane_iota = lax.broadcasted_iota(jnp.int32, (1, TOK), 1)
    first_row = lax.broadcasted_iota(jnp.int32, (HD, TOK), 0) == 0

    def qkv_chunk(i, carry):
        cols = pl.ds(pl.multiple_of(i * TOK, 128), TOK)
        tok = xf[:, cols]
        q = (mm(wqkvt[0], tok) + q_bias).astype(bf16)
        k = mm(wqkvt[1], tok).astype(bf16)
        v = (mm(wqkvt[2], tok) + v_bias).astype(bf16)
        q = (q.astype(f32) * (HD**-0.5)).astype(bf16)
        qkvt[0:C, cols] = q
        qkvt[C : 2 * C, cols] = k
        bias = jnp.where(lane_iota + i * TOK < length, 0.0, MASK)
        bias = jnp.where(first_row, jnp.broadcast_to(bias, (HD, TOK)), 0.0).astype(bf16)
        ones = jnp.where(first_row, 1.0, 0.0).astype(bf16)
        for h in range(HEADS):
            hs = slice(h * HD, (h + 1) * HD)
            qaug[h, 0:HD, cols] = q[hs]
            qaug[h, HD : 2 * HD, cols] = ones
            vaug[h, 0:HD, cols] = v[hs]
            vaug[h, HD : HD + 16, cols] = ones[0:16]
            ktm[h, cols, :] = transposed(jnp.concatenate([k[hs], bias], axis=0))
            vtm[h, cols, :] = transposed(jnp.concatenate([v[hs], ones], axis=0))
        return carry

    lax.fori_loop(0, 4, qkv_chunk, 0)
    ct.wait()
    tt = []
    for k in (1, 3, 2):
        there = pl.ds(pl.multiple_of(lax.rem(c + k, 4) * TOK, 128), TOK)
        tt.append(links.send(t_in.at[:, there], tf.at[c], zdev(k)))

    def fwd_head(h):
        def fwd_tile(n, carry):
            cols = pl.ds(pl.multiple_of(n * TOK, 128), TOK)
            score = mm(ktm[h], qaug[h, :, cols])
            top = jnp.max(score, axis=0, keepdims=True)
            probs = jnp.exp(score - top).astype(bf16)
            pst[h, :, cols] = probs
            both = mm(vaug[h], probs)
            inv = 1.0 / both[HD : HD + 1]
            linv[h, 0:1, cols] = inv
            ctxt[pl.ds(pl.multiple_of(h * HD, 16), HD), cols] = (both[0:HD] * inv).astype(bf16)
            return carry

        lax.fori_loop(0, 4, fwd_tile, 0)

    def fwd_heads(lo, hi):
        lax.fori_loop(lo, hi, lambda h, carry: (fwd_head(h), carry)[1], 0)

    fwd_heads(0, 1)
    w_far = forward(w2, w_b)
    fwd_heads(1, 3)

    cc = []
    ctxa[c] = ctxt[:, tcols]
    for k in (1, 3, 2):
        there = pl.ds(pl.multiple_of(lax.rem(c + k, 4) * TOK, 128), TOK)
        cc.append(links.send(ctxt.at[:, there], ctxa.at[c], zdev(k)))
    for k in range(4):
        w_b[k][0].wait_recv()
        w_s.append(to_sibling(w2, k, b_left))
        w_b[k][1].wait_recv()
        w_s.append(to_sibling(w2, k, b_right))
    wait_all(cc)

    def proj(i, carry):
        row = pl.ds(pl.multiple_of(i * C, 16), C)
        acc = xf[row, tcols].astype(f32) + vcol[row, 0:1]
        w = aux[1, pl.ds(i * 4, 4)].reshape(C, D)
        hid[row] = acc + mm(w, ctxa[...].reshape(D, TOK))
        return carry

    lax.fori_loop(0, 4, proj, 0)

    def norm_stats(ref):
        v = ref[...]
        mean = jnp.sum(v, axis=0, keepdims=True) * (1.0 / D)
        square = jnp.sum(v * v, axis=0, keepdims=True) * (1.0 / D)
        return mean, lax.rsqrt(square - mean * mean + EPS)

    mean1, inv1 = norm_stats(hid)

    def norm1(i, carry):
        row = pl.ds(pl.multiple_of(i * C, 16), C)
        n = (hid[row] - mean1) * inv1
        nrm[row] = n
        h = n * vcol[row, 1:2] + vcol[row, 2:3]
        hid[row] = h
        astore[0, row] = h.astype(bf16)
        return carry

    lax.fori_loop(0, 4, norm1, 0)
    outt[...] = transposed(astore[0])
    for k in range(4):
        w_far[k].wait_recv()
        w_s.append(to_sibling(w2, k, b_far))

    wait_all(w_s)

    def up_chunk(i, carry):
        cols = pl.ds(pl.multiple_of(i * D, 128), D)
        pre = mm(outt[...], w2[0, :, :, cols].reshape(D, D)) + ub[i, 0:1]
        half = 0.5 * (1.0 + lax.erf(pre * ROOT_HALF))
        bstore[1, :, cols] = (pre * half).astype(bf16)
        slope[:, cols] = half + pre * jnp.exp(-0.5 * pre * pre) * INV_ROOT_TAU
        return carry

    lax.fori_loop(0, 4, up_chunk, 0)

    def down_chunk(i, carry):
        row = pl.ds(pl.multiple_of(i * C, 16), C)
        w = w2[1, pl.ds(i * 4, 4)].reshape(C, FF)
        hid[row] = hid[row] + mt(w, bstore[1]) + vcol[row, 3:4]
        return carry

    lax.fori_loop(0, 4, down_chunk, 0)

    mean2, inv2 = norm_stats(hid)
    wait_all(tt)
    valid = lane_iota + c * TOK < length
    gcol[...] = jnp.zeros(gcol.shape, f32)

    def norm2(i, carry):
        total, crossed, loss = carry
        row = pl.ds(pl.multiple_of(i * C, 16), C)
        n = (hid[row] - mean2) * inv2
        hid[row] = n
        final = n * vcol[row, 4:5] + vcol[row, 5:6]
        delta[row] = final.astype(bf16)
        g = jnp.where(valid, final - tf[i].astype(f32), 0.0)
        gcol[row, 4:5] = jnp.sum(g * n, axis=1, keepdims=True)
        gcol[row, 5:6] = jnp.sum(g, axis=1, keepdims=True)
        s = g * vcol[row, 4:5]
        sg[row] = s
        return (
            total + jnp.sum(s, axis=0, keepdims=True),
            crossed + jnp.sum(s * n, axis=0, keepdims=True),
            loss + jnp.sum(g * g, axis=0, keepdims=True),
        )

    zero = jnp.zeros((1, TOK), f32)
    total2, crossed2, loss_row = lax.fori_loop(0, 4, norm2, (zero, zero, zero))
    fo = []
    out_o_own = local(delta.at[xrows], out_o.at[:, tcols])
    for k in (1, 3, 2):
        there = pl.ds(pl.multiple_of(lax.rem(c + k, 4) * C, 16), C)
        fo.append(links.send(delta.at[there], out_o.at[:, tcols], zdev(k)))

    def norm2_back(i, carry):
        row = pl.ds(pl.multiple_of(i * C, 16), C)
        s = inv2 * (sg[row] - total2 * (1.0 / D) - hid[row] * (crossed2 * (1.0 / D)))
        sg[row] = s
        low = s.astype(bf16)
        astore[1, row] = low
        gcol[row, 3:4] = jnp.sum(low.astype(f32), axis=1, keepdims=True)
        return carry

    lax.fori_loop(0, 4, norm2_back, 0)
    outt[...] = transposed(astore[1])

    def act_chunk(i, carry):
        cols = pl.ds(pl.multiple_of(i * D, 128), D)
        g = mm(outt[...], w2[1, :, :, cols].reshape(D, D)) * slope[:, cols]
        low = g.astype(bf16)
        bstore[0, :, cols] = low
        sv[pl.ds(8 + i, 1)] = jnp.sum(low.astype(f32), axis=0, keepdims=True)
        return carry

    lax.fori_loop(0, 4, act_chunk, 0)
    ex = [
        links.send(astore.at[e], arecv, sib),
        links.send(bstore.at[e], brecv, sib),
    ]

    def hidden_back(i, carry):
        total, crossed = carry
        row = pl.ds(pl.multiple_of(i * C, 16), C)
        w = w2[0, pl.ds(i * 4, 4)].reshape(C, FF)
        g = sg[row] + mt(w, bstore[0])
        n = nrm[row]
        gcol[row, 1:2] = jnp.sum(g * n, axis=1, keepdims=True)
        gcol[row, 2:3] = jnp.sum(g, axis=1, keepdims=True)
        s = g * vcol[row, 1:2]
        sg[row] = s
        return (
            total + jnp.sum(s, axis=0, keepdims=True),
            crossed + jnp.sum(s * n, axis=0, keepdims=True),
        )

    total1, crossed1 = lax.fori_loop(0, 4, hidden_back, (zero, zero))

    def norm1_back(i, carry):
        row = pl.ds(pl.multiple_of(i * C, 16), C)
        s = inv1 * (sg[row] - total1 * (1.0 / D) - nrm[row] * (crossed1 * (1.0 / D)))
        sg[row] = s
        low = s.astype(bf16)
        delta[row] = low
        gcol[row, 0:1] = jnp.sum(low.astype(f32), axis=1, keepdims=True)
        return carry

    for copy in fo:
        copy.wait_send()
    out_o_own.wait()
    lax.fori_loop(0, 4, norm1_back, 0)
    outt[...] = transposed(delta[...])

    dc = []
    for j in range(4):
        w = aux[1].reshape(D, D)[:, j * C : (j + 1) * C]
        dct[j] = transposed(mm(outt[...], w).astype(bf16))
    dctx[:, tcols] = dct[c]
    for k in (1, 3, 2):
        dc.append(links.send(dct.at[lax.rem(c + k, 4)], dctx.at[:, tcols], zdev(k)))

    sv[0:8] = transposed(gcol[...])[0:8]
    sv[6:7] = jnp.broadcast_to(jnp.sum(loss_row, axis=1, keepdims=True), (1, D))
    sv[7:8] = jnp.broadcast_to(length.astype(f32), (1, D))
    sv[12:16] = jnp.zeros((4, D), f32)
    n_sv = [1]
    v_sent = [links.send(sv, rsv.at[0], sib)]

    def sv_add():
        got = []
        for copy in v_sent:
            copy.wait()
        lo = n_sv[0] - len(v_sent)
        total = sv[...]
        for i in range(len(v_sent)):
            total = total + rsv[lo + i]
        sv[...] = total
        v_sent.clear()

    def sv_send(dev):
        for k in (1, 3, 2):
            v_sent.append(links.send(sv, rsv.at[n_sv[0]], dev(k)))
            n_sv[0] += 1

    wait_all(ex)

    def g2_block(i, carry):
        for j in range(4):
            cols = slice(j * D, (j + 1) * D)
            row = pl.ds(pl.multiple_of(i * C, 16), C)
            g = mm(astore[d, row], bstore[d, :, cols]) + mm(arecv[row], brecv[:, cols])
            g2[pl.ds(i * 4, 4), :, cols] = g.astype(bf16).reshape(4, RB, D)
        return carry

    lax.fori_loop(0, 4, g2_block, 0)
    sv_add()
    sv_send(bdev)

    VIA_PLUS, VIA_MINUS = (0, 1), (2, 3)

    def sum_start(own, mid, recv):
        m = {}
        for j in VIA_PLUS:
            m[j] = links.send(own(ridx(j, b_far)), mid.at[j], bdev(1))
        for j in VIA_MINUS:
            m[j] = links.send(own(ridx(j, b_far)), mid.at[j], bdev(3))
        got = {}
        for j in VIA_MINUS:
            got[0, j] = links.send(own(ridx(j, b_right)), recv.at[0, j], bdev(1))
        for j in VIA_PLUS:
            got[1, j] = links.send(own(ridx(j, b_left)), recv.at[1, j], bdev(3))
        return m, got

    def sum_mid(own, mid, recv, m, got):
        for j in VIA_PLUS:
            m[j].wait_recv()
            mid[j] = (own(ridx(j, b_right))[...].astype(f32) + mid[j].astype(f32)).astype(bf16)
            got[0, j] = links.send(mid.at[j], recv.at[0, j], bdev(1))
        for j in VIA_MINUS:
            m[j].wait_recv()
            mid[j] = (own(ridx(j, b_left))[...].astype(f32) + mid[j].astype(f32)).astype(bf16)
            got[1, j] = links.send(mid.at[j], recv.at[1, j], bdev(3))

    def sum_end(own, recv, got, summed, peer_recv):
        for j in range(4):
            got[0, j].wait_recv()
            got[1, j].wait_recv()
            total = own(ridx(j, b_me))[...].astype(f32)
            total = total + recv[0, j].astype(f32) + recv[1, j].astype(f32)
            summed[j] = total.astype(bf16)
        return [
            links.send(summed.at[lax.rem(a_me + k, 4)], peer_recv.at[k - 1], adev(k))
            for k in (1, 3, 2)
        ]

    def sum_a(sends, summed, recv):
        wait_all(sends)
        total = summed[a_me].astype(f32)
        for k in range(3):
            total = total + recv[k].astype(f32)
        return total

    def own_w(i):
        return g2.at[i]

    def own_aux(i):
        return ga.at[d, i]

    w_mid, w_got = sum_start(own_w, im, rm)
    g = mt(delta[...], ctxa[...].reshape(D, TOK)).astype(bf16)
    ga[1] = g.reshape(16, RB, D)

    wait_all(dc)

    def bwd_head(h, carry):
        hrow = pl.ds(pl.multiple_of(h * HD, 16), HD)
        krow = pl.ds(pl.multiple_of(C + h * HD, 16), HD)
        vrow = pl.ds(pl.multiple_of(2 * C + h * HD, 16), HD)

        def bwd_tile(n, acc):
            dk, dv = acc
            cols = pl.ds(pl.multiple_of(n * TOK, 128), TOK)
            inv = linv[h, 0:1, cols]
            dc = dctx[hrow, cols].astype(f32)
            inner = jnp.sum(dc * ctxt[hrow, cols].astype(f32), axis=0, keepdims=True) * inv
            dcs = (dc * inv).astype(bf16)
            probs = pst[h, :, cols]
            dp = mm(vtm[h, :, 0:HD], dcs) - inner
            ds = (probs.astype(f32) * dp).astype(bf16)
            dqkvt[hrow, cols] = (mm(qkvt[krow, :], ds) * (HD**-0.5)).astype(bf16)
            dk = dk + mt(qkvt[hrow, cols], ds)
            dv = dv + mt(dcs, probs)
            return dk, dv

        dk, dv = lax.fori_loop(
            0, 4, bwd_tile, (jnp.zeros((HD, LEN), f32), jnp.zeros((HD, LEN), f32))
        )
        dqkvt[krow] = dk.astype(bf16)
        dqkvt[vrow] = dv.astype(bf16)
        return carry

    lax.fori_loop(0, 1, bwd_head, 0)
    sv_add()
    sv_send(adev)
    lax.fori_loop(1, 2, bwd_head, 0)
    sum_mid(own_w, im, rm, w_mid, w_got)
    sv_add()
    sv_send(zdev)
    lax.fori_loop(2, 3, bwd_head, 0)

    ones = jnp.ones((8, LEN), bf16)
    bias_sum = mt(ones, dqkvt[...])[0:1]
    row_iota = lax.broadcasted_iota(jnp.int32, (RB, C), 0)
    bias_rows = jnp.where(
        row_iota == 0,
        jnp.broadcast_to(bias_sum[:, 0:C], (RB, C)),
        jnp.where(row_iota == 1, jnp.broadcast_to(bias_sum[:, 2 * C :], (RB, C)), 0.0),
    ).astype(bf16)

    def dqkv_block(i, carry):
        row = pl.ds(pl.multiple_of(i * C, 16), C)
        g = mt(xf[row], dqkvt[...])
        ga[0, pl.ds(i * 4, 4), :, 0 : 3 * C] = g.astype(bf16).reshape(4, RB, 3 * C)
        ga[0, pl.ds(i * 4, 4), :, 3 * C :] = jnp.broadcast_to(bias_rows[None], (4, RB, C))
        return carry

    lax.fori_loop(0, 4, dqkv_block, 0)
    gx = links.send(ga.at[e], gar, sib)

    xsend = []

    def dx_part(i):
        row = pl.ds(pl.multiple_of(i * C, 16), C)
        w = aux[0, pl.ds(i * 4, 4)].reshape(C, D)[:, 0 : 3 * C]
        return row, mm(w, dqkvt[...])

    for k in (2, 1, 3):
        i = lax.rem(c + k, 4)
        row, g = dx_part(i)
        dxo[...] = g
        dxo[:, tcols] = dxo[:, tcols] + sg[row]
        dxp[k - 1] = dxo[...].astype(bf16)
        xsend.append(links.send(dxp.at[k - 1], rx.at[k - 1], zdev(k)))
    row, g = dx_part(c)
    dxo[...] = g
    dxo[:, tcols] = dxo[:, tcols] + sg[row]

    gx.wait_recv()

    def add_sibling(i, carry):
        ga[d, i] = (ga[d, i].astype(f32) + gar[i].astype(f32)).astype(bf16)
        return carry

    lax.fori_loop(0, 16, add_sibling, 0)
    a_mid, a_got = sum_start(own_aux, ia, ra)
    w_sum = sum_end(own_w, rm, w_got, s1, r2)
    sv_add()
    sv_o[...] = sv[...]
    sum_mid(own_aux, ia, ra, a_mid, a_got)
    s2[...] = sum_a(w_sum, s1, r2).astype(bf16)
    w3 = []
    for k in (1, 3, 2):
        there = pl.ds(pl.multiple_of(lax.rem(c + k, 4) * D, 128), D)
        w3.append(links.send(s2.at[:, there], r3.at[k - 1], zdev(k)))
    a_sum = sum_end(own_aux, ra, a_got, sa1, ra2)
    wait_all(xsend)
    gi_o[...] = dxo[...] + rx[0].astype(f32) + rx[1].astype(f32) + rx[2].astype(f32)
    dqkv = sum_a(a_sum, sa1, ra2)
    xa1[0] = dqkv
    for j in range(4):
        sa2[j] = dqkv[:, j * C : (j + 1) * C].astype(bf16)
    o3 = [links.send(sa2.at[lax.rem(c + k, 4)], ra3.at[k - 1], zdev(k)) for k in (1, 3, 2)]
    q3 = links.send(xa1.at[0], xa1.at[1], sib)
    wait_all(w3)
    total = s2[:, own_cols].astype(f32)
    for k in range(3):
        total = total + r3[k].astype(f32)
    x1[0] = total
    w4 = links.send(x1.at[0], x1.at[1], sib)
    wait_all(o3)
    ototal = sa2[c].astype(f32)
    for k in range(3):
        ototal = ototal + ra3[k].astype(f32)
    xo1[0] = ototal
    o4 = links.send(xo1.at[0], xo1.at[1], sib)
    q3.wait_recv()
    dqkv_o[...] = jnp.where(d == 0, dqkv, xa1[1])
    w4.wait_recv()
    dw2_o[d] = total
    dw2_o[e] = x1[1]
    o4.wait_recv()
    dwo_o[...] = jnp.where(d == 1, ototal, xo1[1])
    for copy in links.all:
        copy.wait()


def finish(
    out_i, gi_i, dw2_i, dwo_i, dqkv_i, sv_i,
    out, loss, gi, gwq, gbq, gwk, gwv, gbv, gwo, gob, gg1, gb1, gup, gub, gdn, gdb, gg2, gb2,
    sem,
):
    c = lax.axis_index("col")
    copy = pltpu.make_async_copy(out_i, out, sem)
    copy.start()
    count = sv_i[7:8, 0:1] * 0.25
    factor = SLOTS / count
    loss[...] = sv_i[6:7, 0:1] / (2.0 * D * count)
    gi[...] = gi_i[...] * factor
    dqkv = dqkv_i[...] * factor
    gwq[...] = dqkv[:, 0:C]
    gwk[...] = dqkv[:, C : 2 * C]
    gwv[...] = dqkv[:, 2 * C : 3 * C]
    gbq[...] = dqkv[0:1, 3 * C :]
    gbv[...] = dqkv[1:2, 3 * C :]
    gwo[...] = transposed(dwo_i[...] * factor)
    gup[...] = dw2_i[0] * factor
    gdn[...] = dw2_i[1] * factor
    sums = sv_i[...] * factor
    for j in range(4):

        @pl.when(c == j)
        def _(j=j):
            gub[...] = sums[8 + j : 9 + j]
            for i, ref in enumerate((gob, gg1, gb1, gdb, gg2, gb2)):
                ref[...] = sums[i : i + 1, j * C : (j + 1) * C]

    copy.wait()


def local_step(
    inputs, teacher, lengths, query_weight, query_bias, key_weight, value_weight, value_bias,
    output_weight, output_bias, first_gain, first_shift, up_weight, up_bias, down_weight,
    down_bias, second_gain, second_shift,
):
    anyspec = pl.BlockSpec(memory_space=pl.ANY)
    vm = pl.BlockSpec(memory_space=pltpu.VMEM)
    sds = jax.ShapeDtypeStruct
    V = pltpu.VMEM
    vectors = [
        v.reshape(1, -1)
        for v in (
            output_bias, first_gain, first_shift, down_bias, second_gain, second_shift,
            query_bias, value_bias, up_bias,
        )
    ]
    got = pl.pallas_call(
        layer,
        name="layer",
        out_shape=(
            sds((C, LEN), bf16),
            sds((C, LEN), f32),
            sds((2, RB, D), f32),
            sds((RB, C), f32),
            sds((RB, D), f32),
            sds((16, D), f32),
        ),
        in_specs=[anyspec, anyspec, pl.BlockSpec(memory_space=pltpu.SMEM)]
        + [vm] * 4
        + [anyspec] * 2
        + [vm] * 9,
        out_specs=(anyspec, vm, vm, vm, vm, vm),
        scratch_shapes=[
            V((D, LEN), bf16),
            V((4, C, TOK), bf16),
            V((2, 16, RB, FF), bf16),
            V((2, 16, RB, D), bf16),
            V((4, RB, C), bf16),
            V((3, C, D), bf16),
            V((4, 16, C), f32),
            V((4, 8, D), f32),
            V((D, 128), f32),
            V((2 * C, LEN), bf16),
            V((HEADS, LEN, 2 * HD), bf16),
            V((HEADS, 2 * HD, LEN), bf16),
            V((HEADS, HD + 16, LEN), bf16),
            V((HEADS, LEN, 2 * HD), bf16),
            V((HEADS, LEN, LEN), bf16),
            V((HEADS, 8, LEN), f32),
            V((C, LEN), bf16),
            V((4, C, TOK), bf16),
            V((D, TOK), f32),
            V((D, TOK), f32),
            V((D, TOK), f32),
            V((2, TOK, FF), bf16),
            V((2, D, TOK), bf16),
            V((TOK, FF), f32),
            V((TOK, FF), bf16),
            V((D, TOK), bf16),
            V((16, RB, FF), bf16),
            V((2, 16, RB, D), bf16),
            V((16, RB, D), bf16),
            V((C, LEN), bf16),
            V((4, C, TOK), bf16),
            V((TOK, D), bf16),
            V((D, TOK), bf16),
            V((3 * C, LEN), bf16),
            V((3, C, LEN), bf16),
            V((C, LEN), f32),
            V((3, C, LEN), bf16),
            V((4, RB, FF), bf16),
            V((2, 4, RB, FF), bf16),
            V((4, RB, FF), bf16),
            V((3, RB, FF), bf16),
            V((RB, FF), bf16),
            V((3, RB, D), bf16),
            V((4, RB, D), bf16),
            V((2, 4, RB, D), bf16),
            V((4, RB, D), bf16),
            V((3, RB, D), bf16),
            V((4, RB, C), bf16),
            V((3, RB, C), bf16),
            V((2, RB, D), f32),
            V((2, RB, D), f32),
            V((2, RB, C), f32),
            V((D, 128), f32),
            V((16, D), f32),
            V((10, 16, D), f32),
            V((2, RB, D), bf16),
            pltpu.SemaphoreType.DMA((12,)),
            pltpu.SemaphoreType.DMA((N_SEM,)),
            pltpu.SemaphoreType.DMA((N_SEM,)),
        ],
        compiler_params=pltpu.CompilerParams(
            collective_id=0, has_side_effects=True, vmem_limit_bytes=62 * 2**20
        ),
    )(
        inputs, teacher, lengths, query_weight, key_weight, value_weight, output_weight,
        up_weight, down_weight, *vectors,
    )
    vector = sds((1, C), f32)
    weight = sds((RB, C), f32)
    wide = sds((RB, D), f32)
    done = pl.pallas_call(
        finish,
        name="finish",
        out_shape=(
            sds((C, LEN), bf16), sds((1, 1), f32), sds((C, LEN), f32),
            weight, vector, weight, weight, vector, sds((C, RB), f32),
            vector, vector, vector, wide, sds((1, D), f32), wide, vector, vector, vector,
        ),
        in_specs=[anyspec] + [vm] * 5,
        out_specs=(anyspec,) + (vm,) * 17,
        scratch_shapes=[pltpu.SemaphoreType.DMA],
    )(*got)
    shapes = [
        (C, LEN), (), (C, LEN), (RB, C), (C,), (RB, C), (RB, C), (C,), (C, RB), (C,), (C,), (C,),
        (RB, D), (D,), (RB, D), (C,), (C,), (C,),
    ]
    return tuple(o.reshape(shape) for o, shape in zip(done, shapes))


def solution(mesh):
    split = Mesh(
        mesh.devices.reshape(mesh.shape["dp"], 4, 4, mesh.shape["col"]), AXES
    )
    tokens = P("col", DP_ROW)
    weight = P(ROW, "col")
    vector = P("col")
    return jax.shard_map(
        local_step,
        mesh=split,
        in_specs=(
            tokens, tokens, P(DP_ROW), weight, vector, weight, weight, vector,
            P("col", ROW), vector, vector, vector, weight, vector, weight,
            vector, vector, vector,
        ),
        out_specs=(
            tokens, P(), tokens, weight, vector, weight, weight, vector,
            P("col", ROW), vector, vector, vector, weight, vector, weight,
            vector, vector, vector,
        ),
        check_vma=False,
    )
```

time: 184 us -> 149 us (0.81)
  Pallas kernels: 162 us -> 143 us
  other arithmetic: 7.21 us -> 0.6 us
  local copies, waits for them, and re-layouts: 9.51 us -> 4.26 us
  between operations: 4.51 us -> 1.34 us
    pallas_call x1, Pallas kernels: 162 us -> 127 us  [local_step(): pl.pallas_call(layer, name='layer', out_shape=(sds((C, LEN), bf16), sds((...]
    pallas_call x0 -> x1, Pallas kernels: none -> 15.4 us  [local_step(): pl.pallas_call(finish, name='finish', out_shape=(sds((C, LEN), bf16), sds...]
    mul x5 -> x0, other arithmetic: 4.98 us -> none  [the longest x1 1.71 us: local_step(): dw2[1] * factor]
    slice x6 -> x0, local copies, waits for them, and re-layouts: 4.81 us -> none  [the longest x1 1.27 us: local_step(): count = sv[7, 0] * 0.25]
    another operation x2 -> x0, local copies, waits for them, and re-layouts: 2.65 us -> none  [local_step(): jnp.stack([output_bias, first_gain, first_shift, down_bias, second_gain,...]
where the time goes in v2:
time: 149 us
  Pallas kernels  143 us (96%)
  local copies, waits for them, and re-layouts  4.26 us (3%)
    pallas_call x1, Pallas kernels, local_step(): pl.pallas_call(layer, name='layer', out_shape=(sds((C, LEN), bf16), sds((...  127 us
    pallas_call x1, Pallas kernels, local_step(): pl.pallas_call(finish, name='finish', out_shape=(sds((C, LEN), bf16), sds...  15.4 us
    unnamed x6, local copies, waits for them, and re-layouts  3 us

profile of v2, /device:TPU:1, one launch (start us, length us, event | category | flops | bytes accessed | tf_op | source)
XLA Modules:
  0.0 148.7 jit_solution(3267908441349342289)
XLA Ops:
  0.7 0.0 copy-start
  1.3 1.3 reshape.101.ub_in
  2.6 0.0 copy-done
  2.6 0.7 copy.36.wo_in
  3.3 127.1 %layer.1 = (bf16[192,1024]{1,0:T(8,128)(2,1)}, f32[192,1024]{1,0:T(8,128)}, f32[2,48,768]{2,1,0:T(8,128)}, f32[48,192]{1,0:T(8,128)}, f32[48,768]{1,0:T(8,128)}, /*index=5*/f32[16,768]{1,0:T(8,128)}) custom-call(bf16[192,1024]{1,0:T(8,128)(2,1)} %x_in.1, bf16[192,1024]{1,0:T(8,128)(2,1)} %t_in.1, s32[1]{0:T(128)S(6)} %copy.38.len_in, bf16[48,192]{1,0:T(8,128)(2,1)} %wq_in.1, ...), custom_call_target="tpu_custom_call" | custom-call | tf_op jit(solution)/shard_map/layer/pallas_call | solution.py:722
  130.4 15.4 %finish.1 = (bf16[192,1024]{1,0:T(8,128)(2,1)}, f32[1,1]{1,0:T(1,128)}, f32[192,1024]{1,0:T(8,128)}, f32[48,192]{1,0:T(8,128)}, f32[1,192]{1,0:T(1,128)}, /*inde...) custom-call(bf16[192,1024]{1,0:T(8,128)(2,1)} %get-tuple-element.42., ...), custom_call_target="tpu_custom_call" | custom-call | tf_op jit(solution)/shard_map/finish/pallas_call | solution.py:809
  145.9 0.0 copy-start.1
  145.9 0.7 copy-done.1
  146.5 0.6 reduce
  147.2 1.6 %copy.37 = f32[192,48]{0,1:T(8,128)} copy(f32[192,48]{1,0:T(8,128)} %get-tuple-element.74) | data formatting | bytes 73728
Async XLA Ops:
  0.7 1.9 %copy-start = (bf16[192,48]{0,1:T(8,128)(2,1)S(1)}, bf16[192,48]{0,1:T(8,128)(2,1)}, u32[]{:S(2)}) copy-start(bf16[192,48]{0,1:T(8,128)(2,1)} %param.26) | copy-start | bytes 55300
  145.9 0.7 copy-start.1

commit v3 on v2

--- a/solution.py
+++ b/solution.py
@@ -23,6 +23,8 @@
 ROW = ("row_0", "row_1")
 DP_ROW = ("dp", "row_0", "row_1")
 N_SEM = 256
+QH = 288
+HW = 384
 f32 = jnp.float32
 bf16 = jnp.bfloat16
 
@@ -81,11 +83,11 @@
     x_in, t_in, len_in, wq_in, wk_in, wv_in, wo_in, up_in, down_in,
     ob_in, g1_in, b1_in, db_in, g2_in, b2_in, qb_in, vb_in, ub_in,
     out_o, gi_o, dw2_o, dwo_o, dqkv_o, sv_o,
-    xf, tf, w2, aux, wo4, wqkvt, vec, ub, vcol, qkvt, ktm, qaug, vaug, vtm, pst, linv,
+    xf, tf, w2, wq2, wo2, wo4, wqkvt, wqkv, vec, ub, vcol, qkvt, ktm, qaug, vaug, vtm, pst, linv,
     ctxt, ctxa, hid, nrm, sg, bstore, astore, slope, brecv, arecv,
-    g2, ga, gar, dctx, dct, outt, delta,
-    dqkvt, dxp, dxo, rx, im, rm, s1, r2, s2, r3, ia, ra, sa1, ra2, sa2, ra3,
-    x1, xa1, xo1, gcol, sv, rsv, wown,
+    g2, gaq, gqr, gao, gor, dctx, dct, outt, delta,
+    dqkvt, dxp, rxi, rx, im, rm, s1, r2, s2, r3, iq, rq, sq1, rq2, io, ro, so1, ro2, so2, so4, ro3,
+    x1, xq1, gcol, sv, rsv, wown,
     lsem, ssem, rsem,
 ):
     d = lax.axis_index("dp")
@@ -139,31 +141,16 @@
     cdn = local(down_in, wown.at[1])
     cx = local(x_in, xf.at[xrows])
     ct = local(t_in.at[:, tcols], tf.at[c])
-    wo4[c] = transposed(wo_in[...])
+    wo4[c] = wo_in[...]
     for i, ref in enumerate((ob_in, g1_in, b1_in, db_in, g2_in, b2_in, qb_in, vb_in)):
         vec[c, i : i + 1, :] = ref[...].reshape(1, C)
-    ub[c, 0:1, :] = ub_in[...].reshape(1, D)
-    own_qkv = jnp.concatenate(
-        [wq_in[...], wk_in[...], wv_in[...], jnp.zeros((RB, C), bf16)], axis=1
-    )
+    ub[c, 0:1, :] = jnp.concatenate([ub_in[i : i + 1] for i in range(6)], axis=1)
+    own_qkv = jnp.concatenate([wq_in[...], wk_in[...], wv_in[...]], axis=1)
+    own_qkv = jnp.where(d == 0, own_qkv[:, 0:QH], own_qkv[:, QH:])
+    wq2[d, r] = jnp.concatenate([own_qkv, jnp.zeros((RB, HW - QH), bf16)], axis=1)
     cup.wait()
     cdn.wait()
     pl.semaphore_wait(bar, 10)
-
-    oz = [links.send(wo4.at[c], wo4.at[c], zdev(k)) for k in (1, 3, 2)]
-    wz = [links.send(wown.at[d], w2.at[d, r, :, own_cols], zdev(k)) for k in (1, 3, 2)]
-    vz = [links.send(vec.at[c], vec.at[c], zdev(k)) for k in (1, 2, 3)]
-    uz = [links.send(ub.at[c], ub.at[c], zdev(k)) for k in (1, 2, 3)]
-    w2[d, r, :, own_cols] = wown[d]
-
-    def xhalf(i, top):
-        return xf.at[pl.ds(pl.multiple_of(i * C + (0 if top else C // 2), 16), C // 2)]
-
-    cx.wait()
-    xs = {}
-    for k, order in ((1, (True, False)), (3, (False, True))):
-        for top in order:
-            xs[k, top] = links.send(xhalf(c, top), xhalf(c, top), zdev(k))
 
     def along_a(buf):
         return [links.send(buf.at[d, r], buf.at[d, r], adev(k)) for k in (1, 3, 2)]
@@ -193,40 +180,60 @@
             far[k] = links.send(ref, ref, bdev(3))
         return far
 
+    wq_a = along_a(wq2)
+    wq_b = {0: along_b(wq2, 0)}
+
+    oz = [links.send(wo4.at[c], wo4.at[c], zdev(k)) for k in (1, 3, 2)]
+    wz = [links.send(wown.at[d], w2.at[d, r, :, own_cols], zdev(k)) for k in (1, 3, 2)]
+    vz = [links.send(vec.at[c], vec.at[c], zdev(k)) for k in (1, 2, 3)]
+    uz = [links.send(ub.at[c], ub.at[c], zdev(k)) for k in (1, 2, 3)]
+    w2[d, r, :, own_cols] = wown[d]
+
+    def xhalf(i, top):
+        return xf.at[pl.ds(pl.multiple_of(i * C + (0 if top else C // 2), 16), C // 2)]
+
+    cx.wait()
+    xs = {}
+    for k, order in ((1, (True, False)), (3, (False, True))):
+        for top in order:
+            xs[k, top] = links.send(xhalf(c, top), xhalf(c, top), zdev(k))
+
+    wait_all(wq_a)
+    for k in (1, 3, 2):
+        wq_b[k] = along_b(wq2, k)
+    wait_all(wz)
+    w_a = along_a(w2)
+    wq_s = [to_sibling(wq2, k, b_me) for k in range(4)]
     wait_all(oz)
     own_wo = jnp.concatenate([wo4[j] for j in range(4)], axis=1)
-    aux[d, r] = jnp.where(d == 0, own_qkv, own_wo)
-    aux_a = along_a(aux)
-    aux_b = {0: along_b(aux, 0)}
-    aux_s = [to_sibling(aux, 0, b_me)]
-    wait_all(wz)
-    w_a = along_a(w2)
-    wait_all(aux_a)
-    for k in (1, 3, 2):
-        aux_b[k] = along_b(aux, k)
-    w_b = {0: along_b(w2, 0)}
-    for k in (1, 3, 2):
-        aux_s.append(to_sibling(aux, k, b_me))
+    wo2[d, r] = jnp.where(d == 0, own_wo[:, 0:HW], own_wo[:, HW:])
+    wo_a = along_a(wo2)
+    wq_far = forward(wq2, wq_b)
     xs[1, True].wait_recv()
     left = lax.rem(c + 3, 4)
     xs["f", 1] = links.send(xhalf(left, True), xhalf(left, True), zdev(1))
     xs[3, False].wait_recv()
     right = lax.rem(c + 1, 4)
     xs["f", 3] = links.send(xhalf(right, False), xhalf(right, False), zdev(3))
+    w_b = {0: along_b(w2, 0)}
+    wo_b = {0: along_b(wo2, 0)}
+    for k in range(4):
+        wq_b[k][0].wait_recv()
+        wq_s.append(to_sibling(wq2, k, b_left))
+        wq_b[k][1].wait_recv()
+        wq_s.append(to_sibling(wq2, k, b_right))
     w_s = [to_sibling(w2, 0, b_me)]
-    aux_far = forward(aux, aux_b)
     for i, k in enumerate((1, 3, 2)):
         w_a[i].wait_recv()
         w_b[k] = along_b(w2, k)
         w_s.append(to_sibling(w2, k, b_me))
     for k in range(4):
-        aux_b[k][0].wait_recv()
-        aux_s.append(to_sibling(aux, k, b_left))
-        aux_b[k][1].wait_recv()
-        aux_s.append(to_sibling(aux, k, b_right))
-    for k in range(4):
-        aux_far[k].wait_recv()
-        aux_s.append(to_sibling(aux, k, b_far))
+        wq_far[k].wait_recv()
+        wq_s.append(to_sibling(wq2, k, b_far))
+    wait_all(wo_a)
+    for k in (1, 3, 2):
+        wo_b[k] = along_b(wo2, k)
+    wo_s = [to_sibling(wo2, k, b_me) for k in range(4)]
 
     wait_all(vz + uz)
     for i in range(4):
@@ -235,9 +242,9 @@
     length = len_in[0]
 
     wait_all([xs[key] for key in ((1, False), (3, True), ("f", 1), ("f", 3))])
-    wait_all(aux_s)
-    for i in range(3):
-        wqkvt[i] = transposed(aux[0].reshape(D, D)[:, i * C : (i + 1) * C])
+    wait_all(wq_s)
+    for i in range(2):
+        wqkvt[i * QH : (i + 1) * QH] = transposed(wq2[i].reshape(D, HW))[0:QH]
     q_bias = vown[:, 6:7]
     v_bias = vown[:, 7:8]
     lane_iota = lax.broadcasted_iota(jnp.int32, (1, TOK), 1)
@@ -246,9 +253,10 @@
     def qkv_chunk(i, carry):
         cols = pl.ds(pl.multiple_of(i * TOK, 128), TOK)
         tok = xf[:, cols]
-        q = (mm(wqkvt[0], tok) + q_bias).astype(bf16)
-        k = mm(wqkvt[1], tok).astype(bf16)
-        v = (mm(wqkvt[2], tok) + v_bias).astype(bf16)
+        qkv = mm(wqkvt[...], tok)
+        q = (qkv[0:C] + q_bias).astype(bf16)
+        k = qkv[C : 2 * C].astype(bf16)
+        v = (qkv[2 * C :] + v_bias).astype(bf16)
         q = (q.astype(f32) * (HD**-0.5)).astype(bf16)
         qkvt[0:C, cols] = q
         qkvt[C : 2 * C, cols] = k
@@ -290,27 +298,48 @@
     def fwd_heads(lo, hi):
         lax.fori_loop(lo, hi, lambda h, carry: (fwd_head(h), carry)[1], 0)
 
+    cc = []
+
+    def context_out(h):
+        hrow = pl.ds(h * HD, HD)
+        ctxa[c, hrow] = ctxt[hrow, tcols]
+        for k in (1, 3, 2):
+            there = pl.ds(pl.multiple_of(lax.rem(c + k, 4) * TOK, 128), TOK)
+            cc.append(links.send(ctxt.at[hrow, there], ctxa.at[c, hrow], zdev(k)))
+
     fwd_heads(0, 1)
+    context_out(0)
     w_far = forward(w2, w_b)
-    fwd_heads(1, 3)
-
-    cc = []
-    ctxa[c] = ctxt[:, tcols]
-    for k in (1, 3, 2):
-        there = pl.ds(pl.multiple_of(lax.rem(c + k, 4) * TOK, 128), TOK)
-        cc.append(links.send(ctxt.at[:, there], ctxa.at[c], zdev(k)))
+    wo_far = forward(wo2, wo_b)
+    fwd_heads(1, 2)
+    context_out(1)
     for k in range(4):
         w_b[k][0].wait_recv()
         w_s.append(to_sibling(w2, k, b_left))
         w_b[k][1].wait_recv()
         w_s.append(to_sibling(w2, k, b_right))
+    for k in range(4):
+        wo_b[k][0].wait_recv()
+        wo_s.append(to_sibling(wo2, k, b_left))
+        wo_b[k][1].wait_recv()
+        wo_s.append(to_sibling(wo2, k, b_right))
+    fwd_heads(2, 3)
+    context_out(2)
+    for i in range(2):
+        wqkv[:, i * QH : (i + 1) * QH] = wq2[i].reshape(D, HW)[:, 0:QH]
+    for k in range(4):
+        wo_far[k].wait_recv()
+        wo_s.append(to_sibling(wo2, k, b_far))
     wait_all(cc)
+    wait_all(wo_s)
 
     def proj(i, carry):
         row = pl.ds(pl.multiple_of(i * C, 16), C)
         acc = xf[row, tcols].astype(f32) + vcol[row, 0:1]
-        w = aux[1, pl.ds(i * 4, 4)].reshape(C, D)
-        hid[row] = acc + mm(w, ctxa[...].reshape(D, TOK))
+        for j in range(2):
+            w = wo2[j, pl.ds(i * 4, 4)].reshape(C, HW)
+            acc = acc + mm(w, ctxa[2 * j : 2 * j + 2].reshape(HW, TOK))
+        hid[row] = acc
         return carry
 
     lax.fori_loop(0, 4, proj, 0)
@@ -448,12 +477,22 @@
     outt[...] = transposed(delta[...])
 
     dc = []
-    for j in range(4):
-        w = aux[1].reshape(D, D)[:, j * C : (j + 1) * C]
-        dct[j] = transposed(mm(outt[...], w).astype(bf16))
+    for i in range(2):
+        part = transposed(mm(outt[...], wo2[i].reshape(D, HW)).astype(bf16))
+        dct[2 * i : 2 * i + 2] = part.reshape(2, C, TOK)
     dctx[:, tcols] = dct[c]
-    for k in (1, 3, 2):
-        dc.append(links.send(dct.at[lax.rem(c + k, 4)], dctx.at[:, tcols], zdev(k)))
+    for h in range(HEADS):
+        hrow = pl.ds(h * HD, HD)
+        dc.append(
+            [
+                links.send(dct.at[lax.rem(c + k, 4), hrow], dctx.at[hrow, tcols], zdev(k))
+                for k in (1, 3, 2)
+            ]
+        )
+    g = mt(delta[...], ctxa[...].reshape(D, TOK)).astype(bf16)
+    for i in range(2):
+        gao[i] = g[:, i * HW : (i + 1) * HW].reshape(16, RB, HW)
+    go_x = links.send(gao.at[e], gor, sib)
 
     sv[0:8] = transposed(gcol[...])[0:8]
     sv[6:7] = jnp.broadcast_to(jnp.sum(loss_row, axis=1, keepdims=True), (1, D))
@@ -539,14 +578,22 @@
     def own_w(i):
         return g2.at[i]
 
-    def own_aux(i):
-        return ga.at[d, i]
+    def own_q(i):
+        return gaq.at[d, i]
+
+    def own_o(i):
+        return gao.at[d, i]
+
+    def add_sibling(ref, other):
+        def add(i, carry):
+            ref[d, i] = (ref[d, i].astype(f32) + other[i].astype(f32)).astype(bf16)
+            return carry
+
+        lax.fori_loop(0, 16, add, 0)
 
     w_mid, w_got = sum_start(own_w, im, rm)
-    g = mt(delta[...], ctxa[...].reshape(D, TOK)).astype(bf16)
-    ga[1] = g.reshape(16, RB, D)
-
-    wait_all(dc)
+
+    wait_all(dc[0])
 
     def bwd_head(h, carry):
         hrow = pl.ds(pl.multiple_of(h * HD, 16), HD)
@@ -578,75 +625,97 @@
     lax.fori_loop(0, 1, bwd_head, 0)
     sv_add()
     sv_send(adev)
+    go_x.wait_recv()
+    add_sibling(gao, gor)
+    o_mid, o_got = sum_start(own_o, io, ro)
+    wait_all(dc[1])
     lax.fori_loop(1, 2, bwd_head, 0)
     sum_mid(own_w, im, rm, w_mid, w_got)
     sv_add()
     sv_send(zdev)
+    wait_all(dc[2])
     lax.fori_loop(2, 3, bwd_head, 0)
+    sum_mid(own_o, io, ro, o_mid, o_got)
 
     ones = jnp.ones((8, LEN), bf16)
     bias_sum = mt(ones, dqkvt[...])[0:1]
-    row_iota = lax.broadcasted_iota(jnp.int32, (RB, C), 0)
-    bias_rows = jnp.where(
-        row_iota == 0,
-        jnp.broadcast_to(bias_sum[:, 0:C], (RB, C)),
-        jnp.where(row_iota == 1, jnp.broadcast_to(bias_sum[:, 2 * C :], (RB, C)), 0.0),
-    ).astype(bf16)
-
-    def dqkv_block(i, carry):
-        row = pl.ds(pl.multiple_of(i * C, 16), C)
-        g = mt(xf[row], dqkvt[...])
-        ga[0, pl.ds(i * 4, 4), :, 0 : 3 * C] = g.astype(bf16).reshape(4, RB, 3 * C)
-        ga[0, pl.ds(i * 4, 4), :, 3 * C :] = jnp.broadcast_to(bias_rows[None], (4, RB, C))
+    spare = HW - QH
+    row_iota = lax.broadcasted_iota(jnp.int32, (RB, spare), 0)
+    bias_rows = []
+    for i in range(2):
+        rows = jnp.zeros((RB, spare), f32)
+        for j in range(3):
+            at = i * QH + j * spare
+            part = jnp.broadcast_to(bias_sum[:, at : at + spare], (RB, spare))
+            rows = jnp.where(row_iota == j, part, rows)
+        bias_rows.append(jnp.broadcast_to(rows.astype(bf16)[None], (4, RB, spare)))
+
+    def dqkv_block(n, carry):
+        row = pl.ds(pl.multiple_of(n * C, 16), C)
+        blocks = pl.ds(n * 4, 4)
+        for i in range(2):
+            g = mt(xf[row], dqkvt[i * QH : (i + 1) * QH])
+            gaq[i, blocks, :, 0:QH] = g.astype(bf16).reshape(4, RB, QH)
+            gaq[i, blocks, :, QH:] = bias_rows[i]
         return carry
 
     lax.fori_loop(0, 4, dqkv_block, 0)
-    gx = links.send(ga.at[e], gar, sib)
-
-    xsend = []
+    gx = links.send(gaq.at[e], gqr, sib)
 
     def dx_part(i):
         row = pl.ds(pl.multiple_of(i * C, 16), C)
-        w = aux[0, pl.ds(i * 4, 4)].reshape(C, D)[:, 0 : 3 * C]
-        return row, mm(w, dqkvt[...])
-
-    for k in (2, 1, 3):
-        i = lax.rem(c + k, 4)
-        row, g = dx_part(i)
-        dxo[...] = g
-        dxo[:, tcols] = dxo[:, tcols] + sg[row]
-        dxp[k - 1] = dxo[...].astype(bf16)
-        xsend.append(links.send(dxp.at[k - 1], rx.at[k - 1], zdev(k)))
-    row, g = dx_part(c)
-    dxo[...] = g
-    dxo[:, tcols] = dxo[:, tcols] + sg[row]
+        gi_o[...] = mm(wqkv[row], dqkvt[...])
+        gi_o[:, tcols] = gi_o[:, tcols] + sg[row]
+
+    H2 = C // 2
+    top, bottom = pl.ds(0, H2), pl.ds(H2, H2)
+    dx_part(lax.rem(c + 2, 4))
+    dxp[0] = gi_o[...].astype(bf16)
+    x_mid = [
+        links.send(dxp.at[0, top], rxi.at[0], zdev(1)),
+        links.send(dxp.at[0, bottom], rxi.at[1], zdev(3)),
+    ]
+    dx_part(right)
+    dxp[1] = gi_o[...].astype(bf16)
+    x_got = [links.send(dxp.at[1, bottom], rx.at[0, bottom], zdev(1))]
+    dx_part(left)
+    dxp[2] = gi_o[...].astype(bf16)
+    x_got.append(links.send(dxp.at[2, top], rx.at[1, top], zdev(3)))
+    dx_part(c)
 
     gx.wait_recv()
-
-    def add_sibling(i, carry):
-        ga[d, i] = (ga[d, i].astype(f32) + gar[i].astype(f32)).astype(bf16)
-        return carry
-
-    lax.fori_loop(0, 16, add_sibling, 0)
-    a_mid, a_got = sum_start(own_aux, ia, ra)
+    add_sibling(gaq, gqr)
+    q_mid, q_got = sum_start(own_q, iq, rq)
+    x_mid[0].wait_recv()
+    dxp[1, top] = (dxp[1, top].astype(f32) + rxi[0].astype(f32)).astype(bf16)
+    x_got.append(links.send(dxp.at[1, top], rx.at[0, top], zdev(1)))
+    x_mid[1].wait_recv()
+    dxp[2, bottom] = (dxp[2, bottom].astype(f32) + rxi[1].astype(f32)).astype(bf16)
+    x_got.append(links.send(dxp.at[2, bottom], rx.at[1, bottom], zdev(3)))
     w_sum = sum_end(own_w, rm, w_got, s1, r2)
+    o_sum = sum_end(own_o, ro, o_got, so1, ro2)
     sv_add()
     sv_o[...] = sv[...]
-    sum_mid(own_aux, ia, ra, a_mid, a_got)
+    sum_mid(own_q, iq, rq, q_mid, q_got)
+    so2[0] = sum_a(o_sum, so1, ro2).astype(bf16)
+    o_x = links.send(so2.at[0], so2.at[1], sib)
     s2[...] = sum_a(w_sum, s1, r2).astype(bf16)
     w3 = []
     for k in (1, 3, 2):
         there = pl.ds(pl.multiple_of(lax.rem(c + k, 4) * D, 128), D)
         w3.append(links.send(s2.at[:, there], r3.at[k - 1], zdev(k)))
-    a_sum = sum_end(own_aux, ra, a_got, sa1, ra2)
-    wait_all(xsend)
-    gi_o[...] = dxo[...] + rx[0].astype(f32) + rx[1].astype(f32) + rx[2].astype(f32)
-    dqkv = sum_a(a_sum, sa1, ra2)
-    xa1[0] = dqkv
-    for j in range(4):
-        sa2[j] = dqkv[:, j * C : (j + 1) * C].astype(bf16)
-    o3 = [links.send(sa2.at[lax.rem(c + k, 4)], ra3.at[k - 1], zdev(k)) for k in (1, 3, 2)]
-    q3 = links.send(xa1.at[0], xa1.at[1], sib)
+    o_x.wait_recv()
+    mine, other = so2[0], so2[1]
+    low, high = jnp.where(d == 0, mine, other), jnp.where(d == 0, other, mine)
+    so4[0], so4[1] = low[:, 0:C], low[:, C:]
+    so4[2], so4[3] = high[:, 0:C], high[:, C:]
+    o3 = [links.send(so4.at[lax.rem(c + k, 4)], ro3.at[k - 1], zdev(k)) for k in (1, 3, 2)]
+    q_sum = sum_end(own_q, rq, q_got, sq1, rq2)
+    wait_all(x_got)
+    gi_o[...] = gi_o[...] + rx[0].astype(f32) + rx[1].astype(f32)
+    dqkv = sum_a(q_sum, sq1, rq2)
+    xq1[0] = dqkv
+    q3 = links.send(xq1.at[0], xq1.at[1], sib)
     wait_all(w3)
     total = s2[:, own_cols].astype(f32)
     for k in range(3):
@@ -654,18 +723,16 @@
     x1[0] = total
     w4 = links.send(x1.at[0], x1.at[1], sib)
     wait_all(o3)
-    ototal = sa2[c].astype(f32)
+    ototal = so4[c].astype(f32)
     for k in range(3):
-        ototal = ototal + ra3[k].astype(f32)
-    xo1[0] = ototal
-    o4 = links.send(xo1.at[0], xo1.at[1], sib)
+        ototal = ototal + ro3[k].astype(f32)
+    dwo_o[...] = ototal
     q3.wait_recv()
-    dqkv_o[...] = jnp.where(d == 0, dqkv, xa1[1])
+    dqkv_o[d] = dqkv
+    dqkv_o[e] = xq1[1]
     w4.wait_recv()
     dw2_o[d] = total
     dw2_o[e] = x1[1]
-    o4.wait_recv()
-    dwo_o[...] = jnp.where(d == 1, ototal, xo1[1])
     for copy in links.all:
         copy.wait()
 
@@ -673,22 +740,20 @@
 def finish(
     out_i, gi_i, dw2_i, dwo_i, dqkv_i, sv_i,
     out, loss, gi, gwq, gbq, gwk, gwv, gbv, gwo, gob, gg1, gb1, gup, gub, gdn, gdb, gg2, gb2,
-    sem,
 ):
     c = lax.axis_index("col")
-    copy = pltpu.make_async_copy(out_i, out, sem)
-    copy.start()
+    out[...] = out_i[...]
     count = sv_i[7:8, 0:1] * 0.25
     factor = SLOTS / count
-    loss[...] = sv_i[6:7, 0:1] / (2.0 * D * count)
+    loss[0] = jnp.sum(sv_i[6:7, 0:1] / (2.0 * D * count))
     gi[...] = gi_i[...] * factor
-    dqkv = dqkv_i[...] * factor
-    gwq[...] = dqkv[:, 0:C]
-    gwk[...] = dqkv[:, C : 2 * C]
-    gwv[...] = dqkv[:, 2 * C : 3 * C]
-    gbq[...] = dqkv[0:1, 3 * C :]
-    gbv[...] = dqkv[1:2, 3 * C :]
-    gwo[...] = transposed(dwo_i[...] * factor)
+    low, high = dqkv_i[0] * factor, dqkv_i[1] * factor
+    gwq[...] = low[:, 0:C]
+    gwk[...] = jnp.concatenate([low[:, C:QH], high[:, 0 : QH - C]], axis=1)
+    gwv[...] = high[:, QH - C : QH]
+    gbq[...] = jnp.concatenate([low[0:1, QH:], low[1:2, QH:]], axis=1)
+    gbv[...] = jnp.concatenate([high[1:2, QH:], high[2:3, QH:]], axis=1)
+    gwo[...] = dwo_i[...] * factor
     gup[...] = dw2_i[0] * factor
     gdn[...] = dw2_i[1] * factor
     sums = sv_i[...] * factor
@@ -696,11 +761,10 @@
 
         @pl.when(c == j)
         def _(j=j):
-            gub[...] = sums[8 + j : 9 + j]
+            for i in range(6):
+                gub[i : i + 1] = sums[8 + j : 9 + j, i * 128 : (i + 1) * 128]
             for i, ref in enumerate((gob, gg1, gb1, gdb, gg2, gb2)):
                 ref[...] = sums[i : i + 1, j * C : (j + 1) * C]
-
-    copy.wait()
 
 
 def local_step(
@@ -716,9 +780,10 @@
         v.reshape(1, -1)
         for v in (
             output_bias, first_gain, first_shift, down_bias, second_gain, second_shift,
-            query_bias, value_bias, up_bias,
+            query_bias, value_bias,
         )
     ]
+    vectors.append(up_bias.reshape(6, 128))
     got = pl.pallas_call(
         layer,
         name="layer",
@@ -727,7 +792,7 @@
             sds((C, LEN), f32),
             sds((2, RB, D), f32),
             sds((RB, C), f32),
-            sds((RB, D), f32),
+            sds((2, RB, HW), f32),
             sds((16, D), f32),
         ),
         in_specs=[anyspec, anyspec, pl.BlockSpec(memory_space=pltpu.SMEM)]
@@ -739,9 +804,11 @@
             V((D, LEN), bf16),
             V((4, C, TOK), bf16),
             V((2, 16, RB, FF), bf16),
-            V((2, 16, RB, D), bf16),
+            V((2, 16, RB, HW), bf16),
+            V((2, 16, RB, HW), bf16),
             V((4, RB, C), bf16),
-            V((3, C, D), bf16),
+            V((3 * C, D), bf16),
+            V((D, 3 * C), bf16),
             V((4, 16, C), f32),
             V((4, 8, D), f32),
             V((D, 128), f32),
@@ -763,31 +830,37 @@
             V((TOK, FF), bf16),
             V((D, TOK), bf16),
             V((16, RB, FF), bf16),
-            V((2, 16, RB, D), bf16),
-            V((16, RB, D), bf16),
+            V((2, 16, RB, HW), bf16),
+            V((16, RB, HW), bf16),
+            V((2, 16, RB, HW), bf16),
+            V((16, RB, HW), bf16),
             V((C, LEN), bf16),
             V((4, C, TOK), bf16),
             V((TOK, D), bf16),
             V((D, TOK), bf16),
             V((3 * C, LEN), bf16),
             V((3, C, LEN), bf16),
-            V((C, LEN), f32),
-            V((3, C, LEN), bf16),
+            V((2, C // 2, LEN), bf16),
+            V((2, C, LEN), bf16),
             V((4, RB, FF), bf16),
             V((2, 4, RB, FF), bf16),
             V((4, RB, FF), bf16),
             V((3, RB, FF), bf16),
             V((RB, FF), bf16),
             V((3, RB, D), bf16),
-            V((4, RB, D), bf16),
-            V((2, 4, RB, D), bf16),
-            V((4, RB, D), bf16),
-            V((3, RB, D), bf16),
+            V((4, RB, HW), bf16),
+            V((2, 4, RB, HW), bf16),
+            V((4, RB, HW), bf16),
+            V((3, RB, HW), bf16),
+            V((4, RB, HW), bf16),
+            V((2, 4, RB, HW), bf16),
+            V((4, RB, HW), bf16),
+            V((3, RB, HW), bf16),
+            V((2, RB, HW), bf16),
             V((4, RB, C), bf16),
             V((3, RB, C), bf16),
             V((2, RB, D), f32),
-            V((2, RB, D), f32),
-            V((2, RB, C), f32),
+            V((2, RB, HW), f32),
             V((D, 128), f32),
             V((16, D), f32),
             V((10, 16, D), f32),
@@ -800,7 +873,7 @@
             collective_id=0, has_side_effects=True, vmem_limit_bytes=62 * 2**20
         ),
     )(
-        inputs, teacher, lengths, query_weight, key_weight, value_weight, output_weight,
+        inputs, teacher, lengths, query_weight, key_weight, value_weight, output_weight.T,
         up_weight, down_weight, *vectors,
     )
     vector = sds((1, C), f32)
@@ -810,19 +883,20 @@
         finish,
         name="finish",
         out_shape=(
-            sds((C, LEN), bf16), sds((1, 1), f32), sds((C, LEN), f32),
-            weight, vector, weight, weight, vector, sds((C, RB), f32),
-            vector, vector, vector, wide, sds((1, D), f32), wide, vector, vector, vector,
+            sds((C, LEN), bf16), sds((1,), f32), sds((C, LEN), f32),
+            weight, vector, weight, weight, vector, weight,
+            vector, vector, vector, wide, sds((6, 128), f32), wide, vector, vector, vector,
         ),
-        in_specs=[anyspec] + [vm] * 5,
-        out_specs=(anyspec,) + (vm,) * 17,
-        scratch_shapes=[pltpu.SemaphoreType.DMA],
+        in_specs=[vm] * 6,
+        out_specs=(vm, pl.BlockSpec(memory_space=pltpu.SMEM)) + (vm,) * 16,
     )(*got)
     shapes = [
-        (C, LEN), (), (C, LEN), (RB, C), (C,), (RB, C), (RB, C), (C,), (C, RB), (C,), (C,), (C,),
+        (C, LEN), (), (C, LEN), (RB, C), (C,), (RB, C), (RB, C), (C,), (RB, C), (C,), (C,), (C,),
         (RB, D), (D,), (RB, D), (C,), (C,), (C,),
     ]
-    return tuple(o.reshape(shape) for o, shape in zip(done, shapes))
+    done = [o.reshape(shape) for o, shape in zip(done, shapes)]
+    done[8] = done[8].T
+    return tuple(done)
 
 
 def solution(mesh):

time: 149 us -> 130 us (0.87)
  Pallas kernels: 143 us -> 128 us
  local copies, waits for them, and re-layouts: 4.26 us -> 0 us
    pallas_call x1, Pallas kernels: 15.4 us -> 2.88 us  [local_step(): pl.pallas_call(finish, name='finish', out_shape=(sds((C, LEN), bf16), sds...]
    unnamed x6 -> x0, local copies, waits for them, and re-layouts: 3 us -> none
    pallas_call x1, Pallas kernels: 127 us -> 125 us  [local_step(): pl.pallas_call(layer, name='layer', out_shape=(sds((C, LEN), bf16), sds((...]
where the time goes in v3:
time: 130 us
  Pallas kernels  128 us (98%)
  between operations  1.48 us (1%)
    pallas_call x1, Pallas kernels, local_step(): pl.pallas_call(layer, name='layer', out_shape=(sds((C, LEN), bf16), sds((...  125 us
    pallas_call x1, Pallas kernels, local_step(): pl.pallas_call(finish, name='finish', out_shape=(sds((C, LEN), bf16), sds...  2.88 us

profile of v3, /device:TPU:1, one launch (start us, length us, event | category | flops | bytes accessed | tf_op | source)
XLA Modules:
  0.0 129.6 jit_solution(709167992188023915)
XLA Ops:
  1.3 125.2 %layer.1 = (bf16[192,1024]{1,0:T(8,128)(2,1)}, f32[192,1024]{1,0:T(8,128)}, f32[2,48,768]{2,1,0:T(8,128)}, f32[48,192]{1,0:T(8,128)}, f32[2,48,384]{2,1,0:T(8,128)}, /*index=5*/f32[16,768]{1,0:T(8,128)}) custom-call(bf16[192,1024]{1,0:T(8,128)(2,1)} %x_in.1, bf16[192,1024]{1,0:T(8,128)(2,1)} %t_in.1, s32[1]{0:T(128)S(6)} %copy.36.len_in, ...), custom_call_target="tpu_custom_call" | custom-call | tf_op jit(solution)/shard_map/layer/pallas_call | solution.py:787
  126.5 2.9 %finish.1 = (bf16[192,1024]{1,0:T(8,128)(2,1)}, f32[1]{0:T(128)}, f32[192,1024]{1,0:T(8,128)}, f32[48,192]{1,0:T(8,128)}, f32[1,192]{1,0:T(1,128)}, /*index=5*/f...) custom-call(bf16[192,1024]{1,0:T(8,128)(2,1)} %get-tuple-element.42., ...), custom_call_target="tpu_custom_call" | custom-call | tf_op jit(solution)/shard_map/finish/pallas_call | solution.py:882

commit v4 on v3

v4 whole, which is shorter than its diff:
```python
import jax
import jax.numpy as jnp
from jax import lax
from jax.experimental import pallas as pl
from jax.experimental.pallas import tpu as pltpu
from jax.sharding import Mesh
from jax.sharding import PartitionSpec as P

D = 768
FF = 3072
LEN = 1024
HD = 64
HEADS = 3
C = 192
TOK = 256
RB = 48
SLOTS = 32768
EPS = 1e-12
MASK = -1e30
ROOT_HALF = 0.7071067811865476
INV_ROOT_TAU = 0.3989422804014327
AXES = ("dp", "row_0", "row_1", "col")
ROW = ("row_0", "row_1")
DP_ROW = ("dp", "row_0", "row_1")
N_SEM = 256
FA = 512
FB = 256
QH = 288
HW = 384
f32 = jnp.float32
bf16 = jnp.bfloat16


def mm(a, b):
    return lax.dot_general(a, b, (((1,), (0,)), ((), ())), preferred_element_type=f32)


def mt(a, b):
    return lax.dot_general(a, b, (((1,), (1,)), ((), ())), preferred_element_type=f32)


def transposed(a):
    return jnp.transpose(a, (1, 0))


class Sent:
    def __init__(self, copy):
        self.copy, self.open_send, self.open_recv = copy, True, True

    def wait_send(self):
        if self.open_send:
            self.copy.wait_send()
        self.open_send = False

    def wait_recv(self):
        if self.open_recv:
            self.copy.wait_recv()
        self.open_recv = False

    def wait(self):
        self.wait_send()
        self.wait_recv()


class Links:
    def __init__(self, ssem, rsem):
        self.ssem, self.rsem, self.n, self.all = ssem, rsem, 0, []

    def send(self, src, dst, dev):
        copy = pltpu.make_async_remote_copy(
            src_ref=src,
            dst_ref=dst,
            send_sem=self.ssem.at[self.n],
            recv_sem=self.rsem.at[self.n],
            device_id=dev,
            device_id_type=pl.DeviceIdType.MESH,
        )
        copy.start()
        self.n += 1
        self.all.append(Sent(copy))
        return self.all[-1]


class RingGather:
    def __init__(self, links, ref, plus, minus, via_plus, via_minus):
        self.links, self.ref, self.plus, self.minus = links, ref, plus, minus
        self.via_plus, self.via_minus = via_plus, via_minus
        self.from_left, self.from_right, self.far = {}, {}, {}

    def send(self, part):
        own = self.ref("me", part)
        self.from_left[part] = self.links.send(own, own, self.plus)
        self.from_right[part] = self.links.send(own, own, self.minus)

    def first(self):
        for part in self.via_plus:
            own = self.ref("me", part)
            self.from_left[part] = self.links.send(own, own, self.plus)
        for part in self.via_minus:
            own = self.ref("me", part)
            self.from_right[part] = self.links.send(own, own, self.minus)

    def rest(self):
        for part in self.via_minus:
            own = self.ref("me", part)
            self.from_left[part] = self.links.send(own, own, self.plus)
        for part in self.via_plus:
            own = self.ref("me", part)
            self.from_right[part] = self.links.send(own, own, self.minus)

    def forward(self):
        for part in self.via_plus:
            self.from_left[part].wait_recv()
            ref = self.ref("left", part)
            self.far[part] = self.links.send(ref, ref, self.plus)
        for part in self.via_minus:
            self.from_right[part].wait_recv()
            ref = self.ref("right", part)
            self.far[part] = self.links.send(ref, ref, self.minus)

    def wait(self):
        for copies in (self.from_left, self.from_right, self.far):
            for copy in copies.values():
                copy.wait_recv()


class RingSum:
    def __init__(self, links, own, mid, recv, plus, minus, via_plus, via_minus):
        self.links, self.own, self.mid, self.recv = links, own, mid, recv
        self.plus, self.minus, self.via_plus, self.via_minus = plus, minus, via_plus, via_minus
        self.m, self.got = {}, {}

    def first(self):
        for p in self.via_plus:
            self.m[p] = self.links.send(self.own("far", p), self.mid.at[p], self.plus)
        for p in self.via_minus:
            self.m[p] = self.links.send(self.own("far", p), self.mid.at[p], self.minus)

    def direct(self, right=True, left=True):
        if right:
            for p in self.via_minus:
                self.got[0, p] = self.links.send(
                    self.own("right", p), self.recv.at[0, p], self.plus
                )
        if left:
            for p in self.via_plus:
                self.got[1, p] = self.links.send(
                    self.own("left", p), self.recv.at[1, p], self.minus
                )

    def middle(self):
        for p in self.via_plus:
            self.m[p].wait_recv()
            self.mid[p] = self.plus_f32(self.own("right", p)[...], self.mid[p])
            self.got[0, p] = self.links.send(self.mid.at[p], self.recv.at[0, p], self.plus)
        for p in self.via_minus:
            self.m[p].wait_recv()
            self.mid[p] = self.plus_f32(self.own("left", p)[...], self.mid[p])
            self.got[1, p] = self.links.send(self.mid.at[p], self.recv.at[1, p], self.minus)

    @staticmethod
    def plus_f32(a, b):
        return (a.astype(f32) + b.astype(f32)).astype(bf16)

    def total(self, p):
        self.got[0, p].wait_recv()
        self.got[1, p].wait_recv()
        total = self.own("me", p)[...].astype(f32)
        return total + self.recv[0, p].astype(f32) + self.recv[1, p].astype(f32)


def layer(
    x_in, t_in, len_in, wq_in, wk_in, wv_in, wo_in, up_in, down_in,
    ob_in, g1_in, b1_in, db_in, g2_in, b2_in, qb_in, vb_in, ub_in,
    out_o, gi_o, dwa_o, dwb_o, dwo_o, dqkv_o, sv_o,
    xf, tf, wa, wb, wq2, wo2, wo4, wqkv, vec, ub, vcol, qkvt, ktm, qaug, vaug, vtm, pst, linv,
    ctxt, ctxa, hid, nrm, sg, bstore, astore, slope, brecv, arecv,
    ga, gb, gaq, gqr, gao, gor, dctx, dct, outt, delta,
    dqkvt, dxp, rxi, rx, im, rm, s1, r2, s2, r3, zi, zr, sb0, bi, br, sb1, rb2,
    iq, rq, sq1, rq2, io, ro, so1, ro2, so2, so4, ro3,
    x1, xb1, xq1, gcol, sv, rsv, wown,
    lsem, ssem, rsem,
):
    d = lax.axis_index("dp")
    y = lax.axis_index("row_0")
    x = lax.axis_index("row_1")
    c = lax.axis_index("col")
    e = 1 - d
    r = 4 * y + x
    a_me = x * e + y * d
    b_me = y * e + x * d

    def around(me):
        return {
            "me": me,
            "left": lax.rem(me + 3, 4),
            "right": lax.rem(me + 1, 4),
            "far": lax.rem(me + 2, 4),
        }

    b_at, c_at = around(b_me), around(c)

    def ridx(a, b):
        return (4 * b + a) * e + (4 * a + b) * d

    def zdev(k):
        return {"col": lax.rem(c + k, 4)}

    def adev(k):
        return {"row_0": lax.rem(y + k * d, 4), "row_1": lax.rem(x + k * e, 4)}

    def bdev(k):
        return {"row_0": lax.rem(y + k * e, 4), "row_1": lax.rem(x + k * d, 4)}

    sib = {"dp": e}
    links = Links(ssem, rsem)

    def wait_all(copies):
        for copy in copies:
            copy.wait_recv()

    def cols(i, width):
        return pl.ds(pl.multiple_of(i * width, 128), width)

    def rows(i, height):
        return pl.ds(pl.multiple_of(i * height, 16), height)

    n_local = [0]

    def local(src, dst):
        copy = pltpu.make_async_copy(src, dst, lsem.at[n_local[0]])
        copy.start()
        n_local[0] += 1
        return copy

    xrows = rows(c, C)
    tcols = cols(c, TOK)
    bar = pltpu.get_barrier_semaphore()
    for k in (1, 2, 3):
        for dev in (zdev(k), adev(k), bdev(k)):
            pl.semaphore_signal(bar, inc=1, device_id=dev, device_id_type=pl.DeviceIdType.MESH)
    pl.semaphore_signal(bar, inc=1, device_id=sib, device_id_type=pl.DeviceIdType.MESH)
    cup = local(up_in, wown.at[0])
    cdn = local(down_in, wown.at[1])
    cx = local(x_in, xf.at[xrows])
    ct = local(t_in.at[:, tcols], tf.at[c])
    wo4[c] = wo_in[...]
    for i, ref in enumerate((ob_in, g1_in, b1_in, db_in, g2_in, b2_in, qb_in, vb_in)):
        vec[c, i : i + 1, :] = ref[...].reshape(1, C)
    ub[c, 0:1, :] = jnp.concatenate([ub_in[i : i + 1] for i in range(6)], axis=1)
    own_qkv = jnp.concatenate([wq_in[...], wk_in[...], wv_in[...]], axis=1)
    own_qkv = jnp.where(d == 0, own_qkv[:, 0:QH], own_qkv[:, QH:])
    wq2[d, r] = jnp.concatenate([own_qkv, jnp.zeros((RB, HW - QH), bf16)], axis=1)
    cup.wait()
    cdn.wait()
    wa[d, r, :, cols(c, FA)] = wown[d, :, 0:FA]
    wb[d, r, :, cols(c, FB)] = wown[d, :, FA:]
    pl.semaphore_wait(bar, 10)

    def along_a(ref):
        return [links.send(ref, ref, adev(k)) for k in (1, 3, 2)]

    def gather_b(ref):
        return RingGather(
            links,
            lambda at, k: ref(ridx(lax.rem(a_me + 4 - k, 4), b_at[at])),
            bdev(1), bdev(3), (0, 2), (1, 3),
        )

    def to_sibling(ref):
        return links.send(ref, ref, sib)

    def wq_ref(i):
        return wq2.at[d, i]

    def wo_ref(i):
        return wo2.at[d, i]

    def wa_ref(i):
        return wa.at[d, i]

    def wb_ref(i):
        return wb.at[d, i, :, cols(c, FB)]

    wq_a = along_a(wq_ref(r))
    wq_b = gather_b(wq_ref)
    wq_b.send(0)
    wz = []
    for k in (1, 3, 2):
        wz.append(
            links.send(wown.at[d, :, pl.ds(0, FA)], wa.at[d, r, :, cols(c, FA)], zdev(k))
        )
    cx.wait()
    x_z = RingGather(
        links,
        lambda at, half: xf.at[rows(2 * c_at[at] + half, C // 2)],
        zdev(1), zdev(3), (0,), (1,),
    )
    x_z.first()
    wb_a = along_a(wb_ref(r))
    wb_b = gather_b(wb_ref)
    wb_b.send(0)

    wait_all(wq_a)
    for k in (1, 3, 2):
        wq_b.send(k)
    wq_s = [to_sibling(wq_ref(ridx(j, b_me))) for j in range(4)]
    wait_all(wb_a)
    for k in (1, 3, 2):
        wb_b.send(k)
    x_z.rest()
    wait_all(wz)
    wa_a = along_a(wa_ref(r))
    wa_b = gather_b(wa_ref)
    wa_b.send(0)
    wq_b.forward()
    for at in ("left", "right"):
        for k in range(4):
            (wq_b.from_left if at == "left" else wq_b.from_right)[k].wait_recv()
            wq_s.append(to_sibling(wq_b.ref(at, k)))
    wb_b.forward()
    x_z.forward()
    oz = [links.send(wo4.at[c], wo4.at[c], zdev(k)) for k in (1, 3, 2)]
    for k in range(4):
        wq_b.far[k].wait_recv()
        wq_s.append(to_sibling(wq_b.ref("far", k)))
    wa_s = [to_sibling(wa_ref(r))]
    for i, k in enumerate((1, 3, 2)):
        wa_a[i].wait_recv()
        wa_b.send(k)
        wa_s.append(to_sibling(wa_b.ref("me", k)))
    vown = transposed(vec[c])
    length = len_in[0]

    x_z.wait()
    wb_b.wait()

    def wb_z(at, half):
        return wb.at[d, pl.ds(half * 8, 8), :, cols(c_at[at], FB)]

    wb_zg = RingGather(links, wb_z, zdev(1), zdev(3), (0,), (1,))
    wb_zg.send(0)
    wb_zg.send(1)
    vz = [links.send(vec.at[c], vec.at[c], zdev(k)) for k in (1, 2, 3)]
    uz = [links.send(ub.at[c, 0:1], ub.at[c, 0:1], zdev(k)) for k in (1, 2, 3)]
    wb_s = [to_sibling(wb.at[d, :, :, cols(c, FB)])]
    wait_all(oz)
    own_wo = jnp.concatenate([wo4[j] for j in range(4)], axis=1)
    wo2[d, r] = jnp.where(d == 0, own_wo[:, 0:HW], own_wo[:, HW:])
    wo_a = along_a(wo_ref(r))
    wo_b = gather_b(wo_ref)
    wo_b.send(0)
    wo_s = [to_sibling(wo_ref(r))]
    wait_all(wq_s)
    w_low = transposed(wq2[0].reshape(D, HW))[0:QH]
    w_high = transposed(wq2[1].reshape(D, HW))[0:QH]
    dxp[0, :, 0:D] = w_low[0:C]
    dxp[1, 0 : QH - C, 0:D] = w_low[C:]
    dxp[1, QH - C :, 0:D] = w_high[0 : QH - C]
    dxp[2, :, 0:D] = w_high[QH - C :]
    q_bias = vown[:, 6:7]
    v_bias = vown[:, 7:8]
    lane_iota = lax.broadcasted_iota(jnp.int32, (1, TOK), 1)
    first_row = lax.broadcasted_iota(jnp.int32, (HD, TOK), 0) == 0

    def qkv_chunk(i, carry):
        at = cols(i, TOK)
        tok = xf[:, at]
        q = (mm(dxp[0, :, 0:D], tok) + q_bias).astype(bf16)
        k = mm(dxp[1, :, 0:D], tok).astype(bf16)
        v = (mm(dxp[2, :, 0:D], tok) + v_bias).astype(bf16)
        q = (q.astype(f32) * (HD**-0.5)).astype(bf16)
        qkvt[0:C, at] = q
        qkvt[C : 2 * C, at] = k
        bias = jnp.where(lane_iota + i * TOK < length, 0.0, MASK)
        bias = jnp.where(first_row, jnp.broadcast_to(bias, (HD, TOK)), 0.0).astype(bf16)
        ones = jnp.where(first_row, 1.0, 0.0).astype(bf16)
        for h in range(HEADS):
            hs = slice(h * HD, (h + 1) * HD)
            qaug[h, 0:HD, at] = q[hs]
            qaug[h, HD : 2 * HD, at] = ones
            vaug[h, 0:HD, at] = v[hs]
            vaug[h, HD : HD + 16, at] = ones[0:16]
            ktm[h, at, :] = transposed(jnp.concatenate([k[hs], bias], axis=0))
            vtm[h, at, :] = transposed(jnp.concatenate([v[hs], ones], axis=0))
        return carry

    lax.fori_loop(0, 4, qkv_chunk, 0)

    def fwd_head(h):
        def fwd_tile(n, carry):
            at = cols(n, TOK)
            score = mm(ktm[h], qaug[h, :, at])
            top = jnp.max(score, axis=0, keepdims=True)
            probs = jnp.exp(score - top).astype(bf16)
            pst[h, :, at] = probs
            both = mm(vaug[h], probs)
            inv = 1.0 / both[HD : HD + 1]
            linv[h, 0:1, at] = inv
            ctxt[h * HD : (h + 1) * HD, at] = (both[0:HD] * inv).astype(bf16)
            return carry

        lax.fori_loop(0, 4, fwd_tile, 0)

    cc = []

    def context_out(h):
        hrow = pl.ds(h * HD, HD)
        ctxa[c, hrow] = ctxt[hrow, tcols]
        for k in (1, 3, 2):
            there = cols(lax.rem(c + k, 4), TOK)
            cc.append(links.send(ctxt.at[hrow, there], ctxa.at[c, hrow], zdev(k)))

    for i, k in enumerate((1, 3, 2)):
        wo_a[i].wait_recv()
        wo_b.send(k)
        wo_s.append(to_sibling(wo_b.ref("me", k)))
    fwd_head(0)
    context_out(0)
    wa_b.forward()
    for k in range(4):
        wa_b.from_left[k].wait_recv()
        wa_s.append(to_sibling(wa_b.ref("left", k)))
        wa_b.from_right[k].wait_recv()
        wa_s.append(to_sibling(wa_b.ref("right", k)))
    fwd_head(1)
    context_out(1)
    wo_b.forward()
    wb_zg.forward()
    for k in range(4):
        wo_b.from_left[k].wait_recv()
        wo_s.append(to_sibling(wo_b.ref("left", k)))
        wo_b.from_right[k].wait_recv()
        wo_s.append(to_sibling(wo_b.ref("right", k)))
    wait_all(vz + uz)
    for i in range(4):
        vcol[i * C : (i + 1) * C, 0:16] = transposed(vec[i])
    fwd_head(2)
    context_out(2)
    for k in range(4):
        wo_b.far[k].wait_recv()
        wo_s.append(to_sibling(wo_b.ref("far", k)))
    for k in range(4):
        wa_b.far[k].wait_recv()
        wa_s.append(to_sibling(wa_b.ref("far", k)))
    for i in range(2):
        wqkv[:, i * QH : (i + 1) * QH] = wq2[i].reshape(D, HW)[:, 0:QH]
    wait_all(wo_s)
    wait_all(cc)
    ct.wait()
    tt = []
    for k in (1, 3, 2):
        there = cols(lax.rem(c + k, 4), TOK)
        tt.append(links.send(t_in.at[:, there], tf.at[c], zdev(k)))

    def proj(i, carry):
        row = rows(i, C)
        acc = xf[row, tcols].astype(f32) + vcol[row, 0:1]
        for j in range(2):
            w = wo2[j, pl.ds(i * 4, 4)].reshape(C, HW)
            acc = acc + mm(w, ctxa[2 * j : 2 * j + 2].reshape(HW, TOK))
        hid[row] = acc
        return carry

    lax.fori_loop(0, 4, proj, 0)

    def norm_stats(ref):
        v = ref[...]
        mean = jnp.sum(v, axis=0, keepdims=True) * (1.0 / D)
        square = jnp.sum(v * v, axis=0, keepdims=True) * (1.0 / D)
        return mean, lax.rsqrt(square - mean * mean + EPS)

    mean1, inv1 = norm_stats(hid)

    def norm1(i, carry):
        row = rows(i, C)
        n = (hid[row] - mean1) * inv1
        nrm[row] = n
        h = n * vcol[row, 1:2] + vcol[row, 2:3]
        hid[row] = h + vcol[row, 3:4]
        astore[0, row] = h.astype(bf16)
        return carry

    lax.fori_loop(0, 4, norm1, 0)
    outt[...] = transposed(astore[0])
    wb_zg.wait()
    for k in (1, 2, 3):
        wb_s.append(to_sibling(wb.at[d, :, :, cols(lax.rem(c + k, 4), FB)]))

    wait_all(wa_s)

    def w_chunk(ref, i):
        return ref[:, :, cols(i, FA)].reshape(D, FA)

    def up_of(ref, bias, first):
        def up_chunk(i, carry):
            at = cols(first + i, FA)
            pre = mm(outt[...], w_chunk(ref, i)) + bias(i)
            half = 0.5 * (1.0 + lax.erf(pre * ROOT_HALF))
            bstore[1, :, at] = (pre * half).astype(bf16)
            slope[:, at] = (half + pre * jnp.exp(-0.5 * pre * pre) * INV_ROOT_TAU).astype(bf16)
            return carry

        return up_chunk

    def bias_b(i):
        return jnp.concatenate([ub[2 * i, 0:1, FA:], ub[2 * i + 1, 0:1, FA:]], axis=1)

    lax.fori_loop(0, 4, up_of(wa.at[0], lambda i: ub[i, 0:1, 0:FA], 0), 0)
    wait_all(wb_s)
    lax.fori_loop(0, 2, up_of(wb.at[0], bias_b, 4), 0)

    def down_of(ref, first):
        def down_chunk(i, carry):
            hid[...] = hid[...] + mt(w_chunk(ref, i), bstore[1, :, cols(first + i, FA)])
            return carry

        return down_chunk

    lax.fori_loop(0, 4, down_of(wa.at[1], 0), 0)
    lax.fori_loop(0, 2, down_of(wb.at[1], 4), 0)

    mean2, inv2 = norm_stats(hid)
    wait_all(tt)
    valid = lane_iota + c * TOK < length
    gcol[...] = jnp.zeros(gcol.shape, f32)
    sv[...] = jnp.zeros(sv.shape, f32)

    def norm2(i, carry):
        total, crossed, loss = carry
        row = rows(i, C)
        n = (hid[row] - mean2) * inv2
        hid[row] = n
        final = n * vcol[row, 4:5] + vcol[row, 5:6]
        delta[row] = final.astype(bf16)
        g = jnp.where(valid, final - tf[i].astype(f32), 0.0)
        gcol[row, 4:5] = jnp.sum(g * n, axis=1, keepdims=True)
        gcol[row, 5:6] = jnp.sum(g, axis=1, keepdims=True)
        s = g * vcol[row, 4:5]
        sg[row] = s
        return (
            total + jnp.sum(s, axis=0, keepdims=True),
            crossed + jnp.sum(s * n, axis=0, keepdims=True),
            loss + jnp.sum(g * g, axis=0, keepdims=True),
        )

    zero = jnp.zeros((1, TOK), f32)
    total2, crossed2, loss_row = lax.fori_loop(0, 4, norm2, (zero, zero, zero))
    fo = []
    out_o_own = local(delta.at[xrows], out_o.at[:, tcols])
    for k in (1, 3, 2):
        there = rows(lax.rem(c + k, 4), C)
        fo.append(links.send(delta.at[there], out_o.at[:, tcols], zdev(k)))

    def norm2_back(i, carry):
        row = rows(i, C)
        s = inv2 * (sg[row] - total2 * (1.0 / D) - hid[row] * (crossed2 * (1.0 / D)))
        sg[row] = s
        low = s.astype(bf16)
        astore[1, row] = low
        gcol[row, 3:4] = jnp.sum(low.astype(f32), axis=1, keepdims=True)
        return carry

    lax.fori_loop(0, 4, norm2_back, 0)
    outt[...] = transposed(astore[1])

    def act_of(ref, first):
        def act_chunk(i, carry):
            at = cols(first + i, FA)
            g = mm(outt[...], w_chunk(ref, i)) * slope[:, at].astype(f32)
            low = g.astype(bf16)
            bstore[0, :, at] = low
            sv[pl.ds(8 + first + i, 1), 0:FA] = jnp.sum(low.astype(f32), axis=0, keepdims=True)
            return carry

        return act_chunk

    lax.fori_loop(0, 2, act_of(wb.at[1], 4), 0)
    lax.fori_loop(0, 4, act_of(wa.at[1], 0), 0)
    ex = [
        links.send(astore.at[e], arecv, sib),
        links.send(bstore.at[e], brecv, sib),
    ]

    def back_of(ref, first):
        def back_chunk(i, carry):
            sg[...] = sg[...] + mt(w_chunk(ref, i), bstore[0, :, cols(first + i, FA)])
            return carry

        return back_chunk

    lax.fori_loop(0, 2, back_of(wb.at[0], 4), 0)
    lax.fori_loop(0, 4, back_of(wa.at[0], 0), 0)

    def hidden_back(i, carry):
        total, crossed = carry
        row = rows(i, C)
        g = sg[row]
        n = nrm[row]
        gcol[row, 1:2] = jnp.sum(g * n, axis=1, keepdims=True)
        gcol[row, 2:3] = jnp.sum(g, axis=1, keepdims=True)
        s = g * vcol[row, 1:2]
        sg[row] = s
        return (
            total + jnp.sum(s, axis=0, keepdims=True),
            crossed + jnp.sum(s * n, axis=0, keepdims=True),
        )

    total1, crossed1 = lax.fori_loop(0, 4, hidden_back, (zero, zero))

    def norm1_back(i, carry):
        row = rows(i, C)
        s = inv1 * (sg[row] - total1 * (1.0 / D) - nrm[row] * (crossed1 * (1.0 / D)))
        sg[row] = s
        low = s.astype(bf16)
        delta[row] = low
        gcol[row, 0:1] = jnp.sum(low.astype(f32), axis=1, keepdims=True)
        return carry

    for copy in fo:
        copy.wait_send()
    out_o_own.wait()
    lax.fori_loop(0, 4, norm1_back, 0)
    outt[...] = transposed(delta[...])

    dc = []
    for i in range(2):
        part = transposed(mm(outt[...], wo2[i].reshape(D, HW)).astype(bf16))
        dct[2 * i : 2 * i + 2] = part.reshape(2, C, TOK)
    dctx[:, tcols] = dct[c]
    for h in range(HEADS):
        hrow = pl.ds(h * HD, HD)
        dc.append(
            [
                links.send(dct.at[lax.rem(c + k, 4), hrow], dctx.at[hrow, tcols], zdev(k))
                for k in (1, 3, 2)
            ]
        )

    sv[0:8] = transposed(gcol[...])[0:8]
    sv[6:7] = jnp.broadcast_to(jnp.sum(loss_row, axis=1, keepdims=True), (1, D))
    sv[7:8] = jnp.broadcast_to(length.astype(f32), (1, D))
    n_sv = [1]
    v_sent = [links.send(sv, rsv.at[0], sib)]

    def sv_add():
        for copy in v_sent:
            copy.wait()
        lo = n_sv[0] - len(v_sent)
        total = sv[...]
        for i in range(len(v_sent)):
            total = total + rsv[lo + i]
        sv[...] = total
        v_sent.clear()

    def sv_send(dev):
        for k in (1, 3, 2):
            v_sent.append(links.send(sv, rsv.at[n_sv[0]], dev(k)))
            n_sv[0] += 1

    wait_all(ex)

    def grad_of(ref, first):
        def grad_chunk(i, carry):
            at = cols(first + i, FA)
            g = mm(astore[d], bstore[d, :, at]) + mm(arecv[...], brecv[:, at])
            ref[:, :, cols(i, FA)] = g.astype(bf16).reshape(16, RB, FA)
            return carry

        return grad_chunk

    lax.fori_loop(0, 2, grad_of(gb, 4), 0)
    HALVES = ((0,), (1,))

    def zb_own(at, half):
        return gb.at[pl.ds(half * 8, 8), :, cols(c_at[at], FB)]

    zb_sum = RingSum(links, zb_own, zi, zr, zdev(1), zdev(3), *HALVES)
    lax.fori_loop(0, 4, grad_of(ga, 0), 0)
    sv_add()
    sv_send(bdev)

    def sum_b(own, mid, recv):
        return RingSum(
            links, lambda at, j: own(ridx(j, b_at[at])), mid, recv, bdev(1), bdev(3), (0, 1), (2, 3)
        )

    def end_b(ring, summed, peer_recv):
        for j in range(4):
            summed[j] = ring.total(j).astype(bf16)
        return [
            links.send(summed.at[lax.rem(a_me + k, 4)], peer_recv.at[k - 1], adev(k))
            for k in (1, 3, 2)
        ]

    def end_a(sends, summed, recv):
        wait_all(sends)
        total = summed[a_me].astype(f32)
        for k in range(3):
            total = total + recv[k].astype(f32)
        return total

    def add_sibling(ref, other):
        def add(i, carry):
            ref[d, i] = (ref[d, i].astype(f32) + other[i].astype(f32)).astype(bf16)
            return carry

        lax.fori_loop(0, 16, add, 0)

    wa_sum = sum_b(lambda i: ga.at[i], im, rm)
    wa_sum.first()
    zb_sum.first()
    g = mt(delta[...], ctxa[...].reshape(D, TOK)).astype(bf16)
    for i in range(2):
        gao[i] = g[:, i * HW : (i + 1) * HW].reshape(16, RB, HW)
    go_x = links.send(gao.at[e], gor, sib)

    def bwd_head(h):
        hrow = pl.ds(h * HD, HD)
        krow = pl.ds(C + h * HD, HD)
        vrow = pl.ds(2 * C + h * HD, HD)

        def bwd_tile(n, acc):
            dk, dv = acc
            at = cols(n, TOK)
            inv = linv[h, 0:1, at]
            dc = dctx[hrow, at].astype(f32)
            inner = jnp.sum(dc * ctxt[hrow, at].astype(f32), axis=0, keepdims=True) * inv
            dcs = (dc * inv).astype(bf16)
            probs = pst[h, :, at]
            dp = mm(vtm[h, :, 0:HD], dcs) - inner
            ds = (probs.astype(f32) * dp).astype(bf16)
            dqkvt[hrow, at] = (mm(qkvt[krow, :], ds) * (HD**-0.5)).astype(bf16)
            dk = dk + mt(qkvt[hrow, at], ds)
            dv = dv + mt(dcs, probs)
            return dk, dv

        dk, dv = lax.fori_loop(
            0, 4, bwd_tile, (jnp.zeros((HD, LEN), f32), jnp.zeros((HD, LEN), f32))
        )
        dqkvt[krow] = dk.astype(bf16)
        dqkvt[vrow] = dv.astype(bf16)

    wait_all(dc[0])
    bwd_head(0)
    wa_sum.direct()
    zb_sum.direct()
    sv_add()
    sv_send(adev)
    go_x.wait_recv()
    add_sibling(gao, gor)
    o_sum = sum_b(lambda i: gao.at[d, i], io, ro)
    o_sum.first()
    wait_all(dc[1])
    bwd_head(1)
    wa_sum.middle()
    zb_sum.middle()
    o_sum.direct()
    wait_all(dc[2])
    bwd_head(2)

    def dx_part(i):
        row = rows(i, C)
        gi_o[...] = mm(wqkv[row], dqkvt[...])
        gi_o[:, tcols] = gi_o[:, tcols] + sg[row]

    SLOT = {"far": 0, "right": 1, "left": 2}

    def dx_own(at, half):
        return dxp.at[SLOT[at], pl.ds(half * (C // 2), C // 2)]

    dx_sum = RingSum(links, dx_own, rxi, rx, zdev(1), zdev(3), *HALVES)
    dx_part(c_at["far"])
    dxp[0] = gi_o[...].astype(bf16)
    dx_sum.first()

    bias_sum = mt(jnp.ones((8, LEN), bf16), dqkvt[...])[0:1]
    spare = HW - QH
    row_iota = lax.broadcasted_iota(jnp.int32, (RB, spare), 0)
    bias_rows = []
    for i in range(2):
        part_rows = jnp.zeros((RB, spare), f32)
        for j in range(3):
            at = i * QH + j * spare
            part = jnp.broadcast_to(bias_sum[:, at : at + spare], (RB, spare))
            part_rows = jnp.where(row_iota == j, part, part_rows)
        bias_rows.append(jnp.broadcast_to(part_rows.astype(bf16)[None], (4, RB, spare)))

    def dqkv_block(n, carry):
        row = rows(n, C)
        blocks = pl.ds(n * 4, 4)
        for i in range(2):
            g = mt(xf[row], dqkvt[i * QH : (i + 1) * QH])
            gaq[i, blocks, :, 0:QH] = g.astype(bf16).reshape(4, RB, QH)
            gaq[i, blocks, :, QH:] = bias_rows[i]
        return carry

    lax.fori_loop(0, 4, dqkv_block, 0)
    gx = links.send(gaq.at[e], gqr, sib)
    o_sum.middle()
    wa_sends = end_b(wa_sum, s1, r2)

    dx_part(c_at["right"])
    dxp[1] = gi_o[...].astype(bf16)
    dx_sum.direct(left=False)
    dx_part(c_at["left"])
    dxp[2] = gi_o[...].astype(bf16)
    dx_sum.direct(right=False)
    dx_part(c)

    gx.wait_recv()
    add_sibling(gaq, gqr)
    q_sum = sum_b(lambda i: gaq.at[d, i], iq, rq)
    q_sum.first()
    for half in range(2):
        sb0[half * 8 : half * 8 + 8] = zb_sum.total(half).astype(bf16)
    wb_sum = sum_b(lambda i: sb0.at[i], bi, br)
    wb_sum.first()
    dx_sum.middle()
    q_sum.direct()
    wb_sum.direct()
    o_sends = end_b(o_sum, so1, ro2)
    sv_add()
    sv_send(zdev)
    q_sum.middle()
    wb_sum.middle()
    s2[...] = end_a(wa_sends, s1, r2).astype(bf16)
    w3 = []
    for k in (1, 3, 2):
        w3.append(links.send(s2.at[:, cols(lax.rem(c + k, 4), FA)], r3.at[k - 1], zdev(k)))
    so2[0] = end_a(o_sends, so1, ro2).astype(bf16)
    o_x = links.send(so2.at[0], so2.at[1], sib)
    q_sends = end_b(q_sum, sq1, rq2)
    wb_sends = end_b(wb_sum, sb1, rb2)
    o_x.wait_recv()
    mine, other = so2[0], so2[1]
    low, high = jnp.where(d == 0, mine, other), jnp.where(d == 0, other, mine)
    so4[0], so4[1] = low[:, 0:C], low[:, C:]
    so4[2], so4[3] = high[:, 0:C], high[:, C:]
    o3 = [links.send(so4.at[lax.rem(c + k, 4)], ro3.at[k - 1], zdev(k)) for k in (1, 3, 2)]
    sv_add()
    sv_o[...] = sv[...]
    for half in range(2):
        dx_sum.got[0, half].wait_recv()
        dx_sum.got[1, half].wait_recv()
        row = pl.ds(half * (C // 2), C // 2)
        gi_o[row] = gi_o[row] + rx[0, half].astype(f32) + rx[1, half].astype(f32)
    dqkv = end_a(q_sends, sq1, rq2)
    xq1[0] = dqkv
    q3 = links.send(xq1.at[0], xq1.at[1], sib)
    xb1[0] = end_a(wb_sends, sb1, rb2)
    wb4 = links.send(xb1.at[0], xb1.at[1], sib)
    wait_all(w3)
    total = s2[:, cols(c, FA)].astype(f32)
    for k in range(3):
        total = total + r3[k].astype(f32)
    x1[0] = total
    w4 = links.send(x1.at[0], x1.at[1], sib)
    wait_all(o3)
    ototal = so4[c].astype(f32)
    for k in range(3):
        ototal = ototal + ro3[k].astype(f32)
    dwo_o[...] = ototal
    wb4.wait_recv()
    dwb_o[d] = xb1[0]
    dwb_o[e] = xb1[1]
    q3.wait_recv()
    dqkv_o[d] = dqkv
    dqkv_o[e] = xq1[1]
    w4.wait_recv()
    dwa_o[d] = total
    dwa_o[e] = x1[1]
    for copy in links.all:
        copy.wait()


def finish(
    out_i, gi_i, dwa_i, dwb_i, dwo_i, dqkv_i, sv_i,
    out, loss, gi, gwq, gbq, gwk, gwv, gbv, gwo, gob, gg1, gb1, gup, gub, gdn, gdb, gg2, gb2,
):
    c = lax.axis_index("col")
    out[...] = out_i[...]
    count = sv_i[7:8, 0:1] * 0.25
    factor = SLOTS / count
    loss[0] = jnp.sum(sv_i[6:7, 0:1] / (2.0 * D * count))
    gi[...] = gi_i[...] * factor
    low, high = dqkv_i[0] * factor, dqkv_i[1] * factor
    gwq[...] = low[:, 0:C]
    gwk[...] = jnp.concatenate([low[:, C:QH], high[:, 0 : QH - C]], axis=1)
    gwv[...] = high[:, QH - C : QH]
    gbq[...] = jnp.concatenate([low[0:1, QH:], low[1:2, QH:]], axis=1)
    gbv[...] = jnp.concatenate([high[1:2, QH:], high[2:3, QH:]], axis=1)
    gwo[...] = dwo_i[...] * factor
    for i, ref in enumerate((gup, gdn)):
        ref[:, 0:FA] = dwa_i[i] * factor
        ref[:, FA:] = dwb_i[i] * factor
    sums = sv_i[...] * factor
    for j in range(4):

        @pl.when(c == j)
        def _(j=j):
            for i in range(4):
                gub[i : i + 1] = sums[8 + j : 9 + j, i * 128 : (i + 1) * 128]
            for i in range(2):
                at = (j % 2) * FB + i * 128
                gub[4 + i : 5 + i] = sums[12 + j // 2 : 13 + j // 2, at : at + 128]
            for i, ref in enumerate((gob, gg1, gb1, gdb, gg2, gb2)):
                ref[...] = sums[i : i + 1, j * C : (j + 1) * C]


def local_step(
    inputs, teacher, lengths, query_weight, query_bias, key_weight, value_weight, value_bias,
    output_weight, output_bias, first_gain, first_shift, up_weight, up_bias, down_weight,
    down_bias, second_gain, second_shift,
):
    anyspec = pl.BlockSpec(memory_space=pl.ANY)
    vm = pl.BlockSpec(memory_space=pltpu.VMEM)
    sds = jax.ShapeDtypeStruct
    V = pltpu.VMEM
    vectors = [
        v.reshape(1, -1)
        for v in (
            output_bias, first_gain, first_shift, down_bias, second_gain, second_shift,
            query_bias, value_bias,
        )
    ]
    vectors.append(up_bias.reshape(6, 128))
    got = pl.pallas_call(
        layer,
        name="layer",
        out_shape=(
            sds((C, LEN), bf16),
            sds((C, LEN), f32),
            sds((2, RB, FA), f32),
            sds((2, RB, FB), f32),
            sds((RB, C), f32),
            sds((2, RB, HW), f32),
            sds((16, D), f32),
        ),
        in_specs=[anyspec, anyspec, pl.BlockSpec(memory_space=pltpu.SMEM)]
        + [vm] * 4
        + [anyspec] * 2
        + [vm] * 9,
        out_specs=(anyspec, vm, vm, vm, vm, vm, vm),
        scratch_shapes=[
            V((D, LEN), bf16),
            V((4, C, TOK), bf16),
            V((2, 16, RB, 4 * FA), bf16),
            V((2, 16, RB, 4 * FB), bf16),
            V((2, 16, RB, HW), bf16),
            V((2, 16, RB, HW), bf16),
            V((4, RB, C), bf16),
            V((D, 3 * C), bf16),
            V((4, 16, C), f32),
            V((4, 8, D), f32),
            V((D, 128), f32),
            V((2 * C, LEN), bf16),
            V((HEADS, LEN, 2 * HD), bf16),
            V((HEADS, 2 * HD, LEN), bf16),
            V((HEADS, HD + 16, LEN), bf16),
            V((HEADS, LEN, 2 * HD), bf16),
            V((HEADS, LEN, LEN), bf16),
            V((HEADS, 8, LEN), f32),
            V((C, LEN), bf16),
            V((4, C, TOK), bf16),
            V((D, TOK), f32),
            V((D, TOK), f32),
            V((D, TOK), f32),
            V((2, TOK, FF), bf16),
            V((2, D, TOK), bf16),
            V((TOK, FF), bf16),
            V((TOK, FF), bf16),
            V((D, TOK), bf16),
            V((16, RB, 4 * FA), bf16),
            V((16, RB, 4 * FB), bf16),
            V((2, 16, RB, HW), bf16),
            V((16, RB, HW), bf16),
            V((2, 16, RB, HW), bf16),
            V((16, RB, HW), bf16),
            V((C, LEN), bf16),
            V((4, C, TOK), bf16),
            V((TOK, D), bf16),
            V((D, TOK), bf16),
            V((3 * C, LEN), bf16),
            V((3, C, LEN), bf16),
            V((2, C // 2, LEN), bf16),
            V((2, 2, C // 2, LEN), bf16),
            V((4, RB, 4 * FA), bf16),
            V((2, 4, RB, 4 * FA), bf16),
            V((4, RB, 4 * FA), bf16),
            V((3, RB, 4 * FA), bf16),
            V((RB, 4 * FA), bf16),
            V((3, RB, FA), bf16),
            V((2, 8, RB, FB), bf16),
            V((2, 2, 8, RB, FB), bf16),
            V((16, RB, FB), bf16),
            V((4, RB, FB), bf16),
            V((2, 4, RB, FB), bf16),
            V((4, RB, FB), bf16),
            V((3, RB, FB), bf16),
            V((4, RB, HW), bf16),
            V((2, 4, RB, HW), bf16),
            V((4, RB, HW), bf16),
            V((3, RB, HW), bf16),
            V((4, RB, HW), bf16),
            V((2, 4, RB, HW), bf16),
            V((4, RB, HW), bf16),
            V((3, RB, HW), bf16),
            V((2, RB, HW), bf16),
            V((4, RB, C), bf16),
            V((3, RB, C), bf16),
            V((2, RB, FA), f32),
            V((2, RB, FB), f32),
            V((2, RB, HW), f32),
            V((D, 128), f32),
            V((16, D), f32),
            V((10, 16, D), f32),
            V((2, RB, D), bf16),
            pltpu.SemaphoreType.DMA((12,)),
            pltpu.SemaphoreType.DMA((N_SEM,)),
            pltpu.SemaphoreType.DMA((N_SEM,)),
        ],
        compiler_params=pltpu.CompilerParams(
            collective_id=0, has_side_effects=True, vmem_limit_bytes=62 * 2**20
        ),
    )(
        inputs, teacher, lengths, query_weight, key_weight, value_weight, output_weight.T,
        up_weight, down_weight, *vectors,
    )
    vector = sds((1, C), f32)
    weight = sds((RB, C), f32)
    wide = sds((RB, D), f32)
    done = pl.pallas_call(
        finish,
        name="finish",
        out_shape=(
            sds((C, LEN), bf16), sds((1,), f32), sds((C, LEN), f32),
            weight, vector, weight, weight, vector, weight,
            vector, vector, vector, wide, sds((6, 128), f32), wide, vector, vector, vector,
        ),
        in_specs=[vm] * 7,
        out_specs=(vm, pl.BlockSpec(memory_space=pltpu.SMEM)) + (vm,) * 16,
    )(*got)
    shapes = [
        (C, LEN), (), (C, LEN), (RB, C), (C,), (RB, C), (RB, C), (C,), (RB, C), (C,), (C,), (C,),
        (RB, D), (D,), (RB, D), (C,), (C,), (C,),
    ]
    done = [o.reshape(shape) for o, shape in zip(done, shapes)]
    done[8] = done[8].T
    return tuple(done)


def solution(mesh):
    split = Mesh(
        mesh.devices.reshape(mesh.shape["dp"], 4, 4, mesh.shape["col"]), AXES
    )
    tokens = P("col", DP_ROW)
    weight = P(ROW, "col")
    vector = P("col")
    return jax.shard_map(
        local_step,
        mesh=split,
        in_specs=(
            tokens, tokens, P(DP_ROW), weight, vector, weight, weight, vector,
            P("col", ROW), vector, vector, vector, weight, vector, weight,
            vector, vector, vector,
        ),
        out_specs=(
            tokens, P(), tokens, weight, vector, weight, weight, vector,
            P("col", ROW), vector, vector, vector, weight, vector, weight,
            vector, vector, vector,
        ),
        check_vma=False,
    )
```

time: 130 us -> 114 us (0.88)
  Pallas kernels: 128 us -> 112 us
    pallas_call x1, Pallas kernels: 125 us -> 109 us  [local_step(): pl.pallas_call(layer, name='layer', out_shape=(sds((C, LEN), bf16), sds((...]
where the time goes in v4:
time: 114 us; the launch traced here: 113 us
  Pallas kernels  112 us (98%)
  between operations  1.48 us (1%)
    pallas_call x1, Pallas kernels, local_step(): pl.pallas_call(layer, name='layer', out_shape=(sds((C, LEN), bf16), sds((...  109 us
    pallas_call x1, Pallas kernels, local_step(): pl.pallas_call(finish, name='finish', out_shape=(sds((C, LEN), bf16), sds...  2.89 us

profile of v4, /device:TPU:1, one launch (start us, length us, event | category | flops | bytes accessed | tf_op | source)
XLA Modules:
  0.0 113.5 jit_solution(10631877877085336887)
XLA Ops:
  1.3 109.1 %layer.1 = (bf16[192,1024]{1,0:T(8,128)(2,1)}, f32[192,1024]{1,0:T(8,128)}, f32[2,48,512]{2,1,0:T(8,128)}, f32[2,48,256]{2,1,0:T(8,128)}, f32[48,192]{1,0:T(8,12...) custom-call(bf16[192,1024]{1,0:T(8,128)(2,1)} %x_in.1, bf16[192,1024]{1,0:T(8,128)(2,1)} %t_in.1, s32[1]{0:T(128)S(6)} %copy.36.len_in, ...), custom_call_target="tpu_custom_call" | custom-call | tf_op jit(solution)/shard_map/layer/pallas_call | solution.py:928
  110.4 2.9 %finish.1 = (bf16[192,1024]{1,0:T(8,128)(2,1)}, f32[1]{0:T(128)}, f32[192,1024]{1,0:T(8,128)}, f32[48,192]{1,0:T(8,128)}, f32[1,192]{1,0:T(1,128)}, /*index=5*/f...) custom-call(bf16[192,1024]{1,0:T(8,128)(2,1)} %get-tuple-element.43., ...), custom_call_target="tpu_custom_call" | custom-call | tf_op jit(solution)/shard_map/finish/pallas_call | solution.py:1033

commit v5 on v4

v5 whole, which is shorter than its diff:
```python
import jax
import jax.numpy as jnp
from jax import lax
from jax.experimental import pallas as pl
from jax.experimental.pallas import tpu as pltpu
from jax.sharding import Mesh
from jax.sharding import PartitionSpec as P

D = 768
FF = 3072
LEN = 1024
HD = 64
HEADS = 3
C = 192
TOK = 256
RB = 48
SLOTS = 32768
EPS = 1e-12
MASK = -1e30
ROOT_HALF = 0.7071067811865476
INV_ROOT_TAU = 0.3989422804014327
AXES = ("dp", "row_0", "row_1", "col")
ROW = ("row_0", "row_1")
DP_ROW = ("dp", "row_0", "row_1")
N_SEM = 96
HL = 128
QC = 96
FA = 512
FB = 256
WT = 512
WF = 1024
QH = 288
HW = 384
f32 = jnp.float32
bf16 = jnp.bfloat16


def mm(a, b):
    return lax.dot_general(a, b, (((1,), (0,)), ((), ())), preferred_element_type=f32)


def mt(a, b):
    return lax.dot_general(a, b, (((1,), (1,)), ((), ())), preferred_element_type=f32)


def transposed(a):
    return jnp.transpose(a, (1, 0))


class Sent:
    def __init__(self, copy):
        self.copy, self.open_send, self.open_recv = copy, True, True

    def wait_send(self):
        if self.open_send:
            self.copy.wait_send()
        self.open_send = False

    def wait_recv(self):
        if self.open_recv:
            self.copy.wait_recv()
        self.open_recv = False

    def wait(self):
        self.wait_send()
        self.wait_recv()


class Batch(Sent):
    def __init__(self, ssem, rsem, whole):
        self.ssem, self.rsem, self.whole, self.dev = ssem, rsem, whole, None
        super().__init__(None)

    def copy_of(self, src, dst):
        return pltpu.make_async_remote_copy(
            src_ref=src,
            dst_ref=dst,
            send_sem=self.ssem,
            recv_sem=self.rsem,
            device_id=self.dev,
            device_id_type=pl.DeviceIdType.MESH,
        )

    def send(self, src, dst, dev):
        self.dev = dev
        self.copy_of(src, dst).start()

    def wait_send(self):
        if self.open_send:
            self.copy = self.copy_of(self.whole, self.whole)
        super().wait_send()

    def wait_recv(self):
        if self.open_recv:
            self.copy = self.copy_of(self.whole, self.whole)
        super().wait_recv()


class Links:
    def __init__(self, ssem, rsem):
        self.ssem, self.rsem, self.n, self.all = ssem, rsem, 0, []

    def send(self, src, dst, dev):
        copy = pltpu.make_async_remote_copy(
            src_ref=src,
            dst_ref=dst,
            send_sem=self.ssem.at[self.n],
            recv_sem=self.rsem.at[self.n],
            device_id=dev,
            device_id_type=pl.DeviceIdType.MESH,
        )
        copy.start()
        self.n += 1
        self.all.append(Sent(copy))
        return self.all[-1]

    def batch(self, whole):
        self.all.append(Batch(self.ssem.at[self.n], self.rsem.at[self.n], whole))
        self.n += 1
        return self.all[-1]


class RingGather:
    def __init__(self, links, ref, whole, plus, minus, plus_parts, minus_parts):
        self.ref, self.plus, self.minus = ref, plus, minus
        self.plus_parts, self.minus_parts = plus_parts, minus_parts
        half = len(plus_parts)
        self.left_on, self.left_end = links.batch(whole(half)), links.batch(whole(half))
        self.right_on, self.right_end = links.batch(whole(half)), links.batch(whole(half))
        self.far = links.batch(whole(2 * half))

    def send_plus(self, part):
        own = self.ref("me", part)
        batch = self.left_on if part in self.plus_parts else self.left_end
        batch.send(own, own, self.plus)

    def send_minus(self, part):
        own = self.ref("me", part)
        batch = self.right_on if part in self.minus_parts else self.right_end
        batch.send(own, own, self.minus)

    def send(self, part):
        self.send_plus(part)
        self.send_minus(part)

    def first(self):
        for part in self.plus_parts:
            self.send_plus(part)
        for part in self.minus_parts:
            self.send_minus(part)

    def rest(self):
        for part in self.minus_parts:
            self.send_plus(part)
        for part in self.plus_parts:
            self.send_minus(part)

    def forward(self):
        self.left_on.wait_recv()
        for part in self.plus_parts:
            ref = self.ref("left", part)
            self.far.send(ref, ref, self.plus)
        self.right_on.wait_recv()
        for part in self.minus_parts:
            ref = self.ref("right", part)
            self.far.send(ref, ref, self.minus)

    def wait(self, at):
        batches = {
            "left": (self.left_on, self.left_end),
            "right": (self.right_on, self.right_end),
            "far": (self.far,),
        }
        for batch in batches[at]:
            batch.wait_recv()


class DirectGather:
    def __init__(self, links, ref, whole, devs):
        self.ref, self.devs, self.batch = ref, devs, links.batch(whole(12))

    def send(self, part):
        own = self.ref("me", part)
        for dev in self.devs:
            self.batch.send(own, own, dev)


class DirectSum:
    def __init__(self, links, own, recv, devs):
        self.own, self.recv, self.devs, self.batch = own, recv, devs, links.batch(recv)

    def start(self):
        for i, at in enumerate(("right", "left", "far")):
            for p in range(4):
                self.batch.send(self.own(at, p), self.recv.at[i, p], self.devs[i])

    def total(self, p):
        self.batch.wait_recv()
        total = self.own("me", p)[...].astype(f32)
        for i in range(3):
            total = total + self.recv[i, p].astype(f32)
        return total


class RingSum:
    def __init__(self, links, own, mid, recv, plus, minus, parts):
        self.own, self.mid, self.recv, self.plus, self.minus = own, mid, recv, plus, minus
        half = parts // 2
        self.low, self.high = range(half), range(half, parts)
        self.mid_left = links.batch(mid.at[pl.ds(0, half)])
        self.mid_right = links.batch(mid.at[pl.ds(half, half)])
        self.left, self.right = links.batch(recv.at[0]), links.batch(recv.at[1])

    def first(self):
        for p in self.low:
            self.mid_left.send(self.own("far", p), self.mid.at[p], self.plus)
        for p in self.high:
            self.mid_right.send(self.own("far", p), self.mid.at[p], self.minus)

    def direct_right(self):
        for p in self.high:
            self.left.send(self.own("right", p), self.recv.at[0, p], self.plus)

    def direct_left(self):
        for p in self.low:
            self.right.send(self.own("left", p), self.recv.at[1, p], self.minus)

    def direct(self):
        self.direct_right()
        self.direct_left()

    def middle(self):
        self.mid_left.wait_recv()
        for p in self.low:
            self.mid[p] = self.plus_f32(self.own("right", p)[...], self.mid[p])
            self.left.send(self.mid.at[p], self.recv.at[0, p], self.plus)
        self.mid_right.wait_recv()
        for p in self.high:
            self.mid[p] = self.plus_f32(self.own("left", p)[...], self.mid[p])
            self.right.send(self.mid.at[p], self.recv.at[1, p], self.minus)

    @staticmethod
    def plus_f32(a, b):
        return (a.astype(f32) + b.astype(f32)).astype(bf16)

    def wait(self):
        self.left.wait_recv()
        self.right.wait_recv()

    def total(self, p):
        self.wait()
        total = self.own("me", p)[...].astype(f32)
        return total + self.recv[0, p].astype(f32) + self.recv[1, p].astype(f32)


def layer(
    x_in, t_in, len_in, wq_in, wk_in, wv_in, wo_in, up_in, down_in,
    ob_in, g1_in, b1_in, db_in, g2_in, b2_in, qb_in, vb_in, ub_in,
    out_o, gi_o, dwa_o, dwb_o, dwo_o, dqkv_o, sv_o,
    xf, tf, wa, wb, wq2, wo2, wo4, wqkv, vec, ub, vcol, qkvt, ktm, qaug, vaug, vtm, pst, linv,
    ctxt, ctxa, hid, nrm, sg, bstore, astore, slope, brecv, arecv,
    ga, gb, gqa, gqb, gra, grb, gao, gor, dctx, dct, outt, delta,
    dqkvt, dxp, rxi, rx, im, rm, s1, r2, s2, r3, zi, zr, sb0, br, sb1, rb2,
    rqa, rqb, sqa, sqb, ra2, rb3, ro, so1, ro2, so2, so4, ro3,
    x1, xb1, xq1, gcol, sv, rsv, wown,
    lsem, ssem, rsem,
):
    d = lax.axis_index("dp")
    y = lax.axis_index("row_0")
    x = lax.axis_index("row_1")
    c = lax.axis_index("col")
    e = 1 - d
    r = 4 * y + x
    a_me = x * e + y * d
    b_me = y * e + x * d

    def around(me):
        return {
            "me": me,
            "left": lax.rem(me + 3, 4),
            "right": lax.rem(me + 1, 4),
            "far": lax.rem(me + 2, 4),
        }

    b_at, c_at = around(b_me), around(c)

    def ridx(a, b):
        return (4 * b + a) * e + (4 * a + b) * d

    def zdev(k):
        return {"col": lax.rem(c + k, 4)}

    def adev(k):
        return {"row_0": lax.rem(y + k * d, 4), "row_1": lax.rem(x + k * e, 4)}

    def bdev(k):
        return {"row_0": lax.rem(y + k * e, 4), "row_1": lax.rem(x + k * d, 4)}

    sib = {"dp": e}
    links = Links(ssem, rsem)

    def wait_all(copies):
        for copy in copies:
            copy.wait_recv()

    def triple(whole, src, dst, dev):
        batch = links.batch(whole)
        for k in (1, 3, 2):
            batch.send(src(k), dst(k), dev(k))
        return batch

    def unrolled(n, body, carry):
        for i in range(n):
            carry = body(i, carry)
        return carry

    def cols(i, width):
        if isinstance(i, int):
            return pl.ds(i * width, width)
        return pl.ds(pl.multiple_of(i * width, 128), width)

    def rows(i, height):
        if isinstance(i, int):
            return pl.ds(i * height, height)
        return pl.ds(pl.multiple_of(i * height, 16), height)

    n_local = [0]

    def local(src, dst):
        copy = pltpu.make_async_copy(src, dst, lsem.at[n_local[0]])
        copy.start()
        n_local[0] += 1
        return copy

    xrows = rows(c, C)
    tcols = cols(c, TOK)
    bar = pltpu.get_barrier_semaphore()
    for k in (1, 2, 3):
        for dev in (zdev(k), adev(k), bdev(k)):
            pl.semaphore_signal(bar, inc=1, device_id=dev, device_id_type=pl.DeviceIdType.MESH)
    pl.semaphore_signal(bar, inc=1, device_id=sib, device_id_type=pl.DeviceIdType.MESH)
    cup = local(up_in, wown.at[0])
    cdn = local(down_in, wown.at[1])
    cx = local(x_in, xf.at[xrows])
    ct = local(t_in.at[:, tcols], tf.at[c])
    wo4[c] = wo_in[...]
    for i, ref in enumerate((ob_in, g1_in, b1_in, db_in, g2_in, b2_in, qb_in, vb_in)):
        vec[c, i : i + 1, :] = ref[...].reshape(1, C)
    ub[c, 0:1, :] = jnp.concatenate([ub_in[i : i + 1] for i in range(6)], axis=1)
    own_qkv = [w[...] for w in (wq_in, wk_in, wv_in)]
    own_qkv = jnp.concatenate(
        [w[:, h * HD : (h + 1) * HD] for h in range(HEADS) for w in own_qkv], axis=1
    )
    own_qkv = jnp.where(d == 0, own_qkv[:, 0:QH], own_qkv[:, QH:])
    wq2[d, r] = jnp.concatenate([own_qkv, jnp.zeros((RB, HW - QH), bf16)], axis=1)
    pl.semaphore_wait(bar, 10)

    def along_a(ref, whole):
        return triple(whole, lambda k: ref, lambda k: ref, adev)

    def of_b(ref):
        return lambda at, k: ref(ridx(lax.rem(a_me + 4 - k, 4), b_at[at]))

    def direct_b(ref, whole):
        return DirectGather(links, of_b(ref), whole, (bdev(1), bdev(3), bdev(2)))

    def wq_ref(i):
        return wq2.at[d, i]

    def wo_ref(i):
        return wo2.at[d, i]

    def wa_ref(i):
        return wa.at[d, i]

    def wb_ref(i):
        return wb.at[d, i, :, cols(c, FB)]

    def some(buf):
        return lambda n: buf.at[d, pl.ds(0, n)]

    def some_b(n):
        return wb.at[d, pl.ds(0, n), :, cols(c, FB)]

    class ToSibling:
        def __init__(self, whole):
            self.batch = links.batch(whole)

        def send(self, ref):
            self.batch.send(ref, ref, sib)

        def wait(self):
            self.batch.wait_recv()

    wq_a = along_a(wq_ref(r), some(wq2)(3))
    wq_b = direct_b(wq_ref, some(wq2))
    wq_b.send(0)
    cup.wait()
    cdn.wait()
    wz = triple(
        wa.at[d, 0, :, pl.ds(0, 3 * FA)],
        lambda k: wown.at[d, :, pl.ds(0, FA)],
        lambda k: wa.at[d, r, :, cols(c, FA)],
        zdev,
    )
    cx.wait()
    x_z = RingGather(
        links,
        lambda at, half: xf.at[rows(2 * c_at[at] + half, C // 2)],
        lambda n: xf.at[pl.ds(0, n * C // 2)],
        zdev(1), zdev(3), (0,), (1,),
    )
    x_z.first()
    oz = triple(wo4.at[pl.ds(0, 3)], lambda k: wo4.at[c], lambda k: wo4.at[c], zdev)
    vz = triple(vec.at[pl.ds(0, 3)], lambda k: vec.at[c], lambda k: vec.at[c], zdev)
    uz = triple(
        ub.at[pl.ds(0, 3), 0:1], lambda k: ub.at[c, 0:1], lambda k: ub.at[c, 0:1], zdev
    )
    wa[d, r, :, cols(c, FA)] = wown[d, :, 0:FA]
    wb[d, r, :, cols(c, FB)] = wown[d, :, FA:]
    wb_a = along_a(wb_ref(r), some_b(3))
    wb_b = direct_b(wb_ref, some_b)
    wb_b.send(0)

    wq_a.wait_recv()
    for k in (1, 3, 2):
        wq_b.send(k)
    wq_s = ToSibling(wq2.at[d])
    for j in range(4):
        wq_s.send(wq_ref(ridx(j, b_me)))
    wb_a.wait_recv()
    for k in (1, 3, 2):
        wb_b.send(k)
    x_z.rest()
    wz.wait_recv()
    wa_a = [links.batch(wa_ref(0)) for _ in range(3)]
    for i, k in enumerate((1, 3, 2)):
        wa_a[i].send(wa_ref(r), wa_ref(r), adev(k))
    wa_b = RingGather(links, of_b(wa_ref), some(wa), bdev(1), bdev(3), (0, 2), (1, 3))
    wa_b.send(0)
    oz.wait_recv()
    own_wo = jnp.concatenate([wo4[j] for j in range(4)], axis=1)
    wo2[d, r] = jnp.where(d == 0, own_wo[:, 0:HW], own_wo[:, HW:])
    wo_a = along_a(wo_ref(r), some(wo2)(3))
    wo_b = direct_b(wo_ref, some(wo2))
    wo_b.send(0)
    wq_b.batch.wait_recv()
    for at in ("left", "right", "far"):
        for k in range(4):
            wq_s.send(wq_b.ref(at, k))
    x_z.forward()
    wo_s = ToSibling(wo2.at[d])
    wo_s.send(wo_ref(r))
    wa_s = ToSibling(wa.at[d])
    wa_s.send(wa_ref(r))
    for i, k in enumerate((1, 3, 2)):
        wa_a[i].wait_recv()
        wa_b.send(k)
        wa_s.send(wa_b.ref("me", k))
    wo_a.wait_recv()
    for k in (1, 3, 2):
        wo_b.send(k)
        wo_s.send(wo_b.ref("me", k))
    vown = transposed(vec[c])
    length = len_in[0]

    for at in ("left", "right", "far"):
        x_z.wait(at)
    wb_b.batch.wait_recv()

    def wb_z(at, half):
        return wb.at[d, pl.ds(half * 8, 8), :, cols(c_at[at], FB)]

    def some_z(n):
        return wb.at[d, pl.ds(0, 8), :, pl.ds(0, n * FB)]

    wb_zg = RingGather(links, wb_z, some_z, zdev(1), zdev(3), (0,), (1,))
    wb_zg.first()
    wb_s = ToSibling(wb.at[d])
    wb_s.send(wb.at[d, :, :, cols(c, FB)])
    wq_s.wait()
    w_low = transposed(wq2[0].reshape(D, HW))[0:QH]
    w_high = transposed(wq2[1].reshape(D, HW))[0:QH]
    dxp[0, :, 0:D] = w_low[0:C]
    dxp[1, 0 : QH - C, 0:D] = w_low[C:]
    dxp[1, QH - C :, 0:D] = w_high[0 : QH - C]
    dxp[2, :, 0:D] = w_high[QH - C :]
    q_bias = vown[:, 6:7]
    v_bias = vown[:, 7:8]
    lane_iota = lax.broadcasted_iota(jnp.int32, (1, TOK), 1)
    first_row = lax.broadcasted_iota(jnp.int32, (HD, TOK), 0) == 0

    def qkv_chunk(i, carry):
        at = cols(i, TOK)
        tok = xf[:, at]
        qkv = mm(dxp[:, :, 0:D].reshape(3 * C, D), tok)
        bias = jnp.where(lane_iota + i * TOK < length, 0.0, MASK)
        bias = jnp.where(first_row, jnp.broadcast_to(bias, (HD, TOK)), 0.0).astype(bf16)
        ones = jnp.where(first_row, 1.0, 0.0).astype(bf16)
        for h in range(HEADS):
            hs = slice(h * HD, (h + 1) * HD)
            of = h * C
            q = (qkv[of : of + HD] + q_bias[hs]).astype(bf16)
            q = (q.astype(f32) * (HD**-0.5)).astype(bf16)
            k = qkv[of + HD : of + 2 * HD].astype(bf16)
            v = (qkv[of + 2 * HD : of + 3 * HD] + v_bias[hs]).astype(bf16)
            qkvt[h * HD : (h + 1) * HD, at] = q
            qkvt[C + h * HD : C + (h + 1) * HD, at] = k
            qaug[h, 0:HD, at] = q
            qaug[h, HD : 2 * HD, at] = ones
            vaug[h, 0:HD, at] = v
            vaug[h, HD : HD + 16, at] = ones[0:16]
            ktm[h, at, :] = transposed(jnp.concatenate([k, bias], axis=0))
            vtm[h, at, :] = transposed(jnp.concatenate([v, ones], axis=0))
        return carry

    unrolled(4, qkv_chunk, 0)
    wb_zg.rest()

    def fwd_head(h):
        score = mm(ktm[h], qaug[h, :, 0:WT])
        for n in range(LEN // WT):
            at = cols(n, WT)
            later = mm(ktm[h], qaug[h, :, cols(n + 1, WT)]) if (n + 1) * WT < LEN else None
            top = jnp.max(score, axis=0, keepdims=True)
            probs = jnp.exp(score - top).astype(bf16)
            pst[h, :, at] = probs
            both = mm(vaug[h], probs)
            inv = 1.0 / both[HD : HD + 1]
            linv[h, 0:1, at] = inv
            ctxt[h * HD : (h + 1) * HD, at] = (both[0:HD] * inv).astype(bf16)
            score = later

    cc = links.batch(ctxa.at[pl.ds(0, 3)])

    def context_out(h):
        hrow = pl.ds(h * HD, HD)
        ctxa[c, hrow] = ctxt[hrow, tcols]
        for k in (1, 3, 2):
            there = cols(lax.rem(c + k, 4), TOK)
            cc.send(ctxt.at[hrow, there], ctxa.at[c, hrow], zdev(k))

    def pass_on(ring, sent, at):
        ring.wait(at)
        for k in range(4):
            sent.send(ring.ref(at, k))

    fwd_head(0)
    context_out(0)
    wa_b.forward()
    pass_on(wa_b, wa_s, "left")
    pass_on(wa_b, wa_s, "right")
    fwd_head(1)
    context_out(1)
    wo_b.batch.wait_recv()
    for at in ("left", "right", "far"):
        for k in range(4):
            wo_s.send(wo_b.ref(at, k))
    wait_all((vz, uz))
    for i in range(4):
        vcol[i * C : (i + 1) * C, 0:16] = transposed(vec[i])
    fwd_head(2)
    context_out(2)
    wb_zg.forward()
    pass_on(wa_b, wa_s, "far")
    for i in range(2):
        wqkv[:, i * QH : (i + 1) * QH] = wq2[i].reshape(D, HW)[:, 0:QH]
    wo_s.wait()
    cc.wait_recv()
    ct.wait()
    tt = triple(
        tf.at[pl.ds(0, 3)],
        lambda k: t_in.at[:, cols(lax.rem(c + k, 4), TOK)],
        lambda k: tf.at[c],
        zdev,
    )

    acc = xf[:, tcols].astype(f32) + vcol[:, 0:1]
    for j in range(2):
        w = wo2[j].reshape(D, HW)
        acc = acc + mm(w, ctxa[2 * j : 2 * j + 2].reshape(HW, TOK))
    hid[...] = acc

    def norm_stats(ref):
        v = ref[...]
        mean = jnp.sum(v, axis=0, keepdims=True) * (1.0 / D)
        square = jnp.sum(v * v, axis=0, keepdims=True) * (1.0 / D)
        return mean, lax.rsqrt(square - mean * mean + EPS)

    mean1, inv1 = norm_stats(hid)

    def norm1(i, carry):
        row = rows(i, C)
        n = (hid[row] - mean1) * inv1
        nrm[row] = n
        h = n * vcol[row, 1:2] + vcol[row, 2:3]
        hid[row] = h + vcol[row, 3:4]
        astore[0, row] = h.astype(bf16)
        return carry

    unrolled(4, norm1, 0)
    outt[...] = transposed(astore[0])
    for at in ("left", "right"):
        wb_zg.wait(at)
        wb_s.send(wb.at[d, :, :, cols(c_at[at], FB)])

    wa_s.wait()

    def w_chunk(ref, i):
        return ref[:, :, cols(i, WF)].reshape(D, WF)

    def store_halves(w, chunk, v):
        if isinstance(chunk, int) and chunk == 2:
            for j in range(4):
                for half in range(2):
                    at = j * FB + half * FB // 2
                    to = 4 * FA // 2 + j * FB // 2
                    bstore[w, half, :, to : to + FB // 2] = v[:, at : at + FB // 2]
        else:
            for j in range(2):
                for half in range(2):
                    at = j * FA + half * FA // 2
                    bstore[w, half, :, cols(2 * chunk + j, FA // 2)] = v[:, at : at + FA // 2]

    def load_halves(w, chunk):
        if isinstance(chunk, int) and chunk == 2:
            return jnp.concatenate(
                [
                    bstore[w, half, :, 2 * FA + j * FB // 2 : 2 * FA + (j + 1) * FB // 2]
                    for j in range(4)
                    for half in range(2)
                ],
                axis=1,
            )
        return jnp.concatenate(
            [bstore[w, half, :, cols(2 * chunk + j, FA // 2)] for j in range(2) for half in range(2)],
            axis=1,
        )

    def up_of(ref, bias, first):
        def up_chunk(i, carry):
            at = cols(first + i, WF)
            pre = mm(outt[...], w_chunk(ref, i)) + bias(i)
            half = 0.5 * (1.0 + lax.erf(pre * ROOT_HALF))
            store_halves(1, first + i, (pre * half).astype(bf16))
            slope[:, at] = (half + pre * jnp.exp(-0.5 * pre * pre) * INV_ROOT_TAU).astype(bf16)
            return carry

        return up_chunk

    def bias_a(i):
        return jnp.concatenate([ub[2 * i, 0:1, 0:FA], ub[2 * i + 1, 0:1, 0:FA]], axis=1)

    def bias_b(i):
        return jnp.concatenate([ub[j, 0:1, FA:] for j in range(4)], axis=1)

    lax.fori_loop(0, 2, up_of(wa.at[0], bias_a, 0), 0)
    wb_zg.wait("far")
    wb_s.send(wb.at[d, :, :, cols(c_at["far"], FB)])

    def down_of(ref, first):
        def down_chunk(i, carry):
            hid[...] = hid[...] + mt(w_chunk(ref, i), load_halves(1, first + i))
            return carry

        return down_chunk

    lax.fori_loop(0, 2, down_of(wa.at[1], 0), 0)
    wb_s.wait()
    unrolled(1, up_of(wb.at[0], bias_b, 2), 0)
    unrolled(1, down_of(wb.at[1], 2), 0)

    mean2, inv2 = norm_stats(hid)
    tt.wait_recv()
    valid = lane_iota + c * TOK < length
    gcol[...] = jnp.zeros(gcol.shape, f32)
    sv[...] = jnp.zeros(sv.shape, f32)

    def norm2(i, carry):
        total, crossed, loss = carry
        row = rows(i, C)
        n = (hid[row] - mean2) * inv2
        hid[row] = n
        final = n * vcol[row, 4:5] + vcol[row, 5:6]
        delta[row] = final.astype(bf16)
        g = jnp.where(valid, final - tf[i].astype(f32), 0.0)
        gcol[row, 4:5] = jnp.sum(g * n, axis=1, keepdims=True)
        gcol[row, 5:6] = jnp.sum(g, axis=1, keepdims=True)
        s = g * vcol[row, 4:5]
        sg[row] = s
        return (
            total + jnp.sum(s, axis=0, keepdims=True),
            crossed + jnp.sum(s * n, axis=0, keepdims=True),
            loss + jnp.sum(g * g, axis=0, keepdims=True),
        )

    zero = jnp.zeros((1, TOK), f32)
    total2, crossed2, loss_row = unrolled(4, norm2, (zero, zero, zero))
    out_o_own = local(delta.at[xrows], out_o.at[:, tcols])
    fo = triple(
        delta.at[pl.ds(0, 3 * C)],
        lambda k: delta.at[rows(lax.rem(c + k, 4), C)],
        lambda k: out_o.at[:, tcols],
        zdev,
    )

    def norm2_back(i, carry):
        row = rows(i, C)
        s = inv2 * (sg[row] - total2 * (1.0 / D) - hid[row] * (crossed2 * (1.0 / D)))
        sg[row] = s
        low = s.astype(bf16)
        astore[1, row] = low
        gcol[row, 3:4] = jnp.sum(low.astype(f32), axis=1, keepdims=True)
        return carry

    unrolled(4, norm2_back, 0)

    def exchange(w):
        return [
            links.send(astore.at[w], arecv.at[w], sib),
            links.send(bstore.at[w, e], brecv.at[w], sib),
        ]

    ex_down = exchange(1)
    outt[...] = transposed(astore[1])

    def act_of(ref, first):
        def act_chunk(i, carry):
            at = cols(first + i, WF)
            g = mm(outt[...], w_chunk(ref, i)) * slope[:, at].astype(f32)
            low = g.astype(bf16)
            store_halves(0, first + i, low)
            total = jnp.sum(low.astype(f32), axis=0, keepdims=True)
            sv[pl.ds(8 + 2 * (first + i), 1), 0:FA] = total[:, 0:FA]
            sv[pl.ds(9 + 2 * (first + i), 1), 0:FA] = total[:, FA:]
            return carry

        return act_chunk

    unrolled(1, act_of(wb.at[1], 2), 0)
    lax.fori_loop(0, 2, act_of(wa.at[1], 0), 0)
    ex_up = exchange(0)

    def back_of(ref, first):
        def back_chunk(i, carry):
            sg[...] = sg[...] + mt(w_chunk(ref, i), load_halves(0, first + i))
            return carry

        return back_chunk

    def sum_b(own, mid, recv):
        return RingSum(
            links, lambda at, j: own(ridx(j, b_at[at])), mid, recv, bdev(1), bdev(3), 4
        )

    def direct_sum(own, recv):
        return DirectSum(
            links, lambda at, j: own(ridx(j, b_at[at])), recv, (bdev(1), bdev(3), bdev(2))
        )

    def end_b(ring, summed, peer_recv):
        for j in range(4):
            summed[j] = ring.total(j).astype(bf16)
        return triple(
            peer_recv,
            lambda k: summed.at[lax.rem(a_me + k, 4)],
            lambda k: peer_recv.at[k - 1],
            adev,
        )

    def end_a(sends, summed, recv):
        sends.wait_recv()
        total = summed[a_me].astype(f32)
        for k in range(3):
            total = total + recv[k].astype(f32)
        return total

    def add_sibling(ref, other):
        def add(i, carry):
            ref[d, i] = (ref[d, i].astype(f32) + other[i].astype(f32)).astype(bf16)
            return carry

        unrolled(16, add, 0)

    def weight_grad(w):
        for at, ref in ((0, ga), (2 * FA, gb)):
            for lo in range(0, ref.shape[3], FA):
                cut = pl.ds(at + lo, FA)
                g = mm(astore[w], bstore[w, d, :, cut]) + mm(arecv[w], brecv[w, :, cut])
                ref[w, :, :, lo : lo + FA] = g.astype(bf16).reshape(16, RB, FA)

        def z_own(at, half):
            return gb.at[w, pl.ds(half * 8, 8), :, cols(c_at[at], FB // 2)]

        a_ring = sum_b(lambda i: ga.at[w, i], im.at[w], rm.at[w])
        b_ring = RingSum(links, z_own, zi.at[w], zr.at[w], zdev(1), zdev(3), 2)
        a_ring.first()
        b_ring.first()
        return a_ring, b_ring

    unrolled(1, back_of(wb.at[0], 2), 0)
    wait_all(ex_down)
    wd_a, wd_b = weight_grad(1)
    lax.fori_loop(0, 2, back_of(wa.at[0], 0), 0)

    def hidden_back(i, carry):
        total, crossed = carry
        row = rows(i, C)
        g = sg[row]
        n = nrm[row]
        gcol[row, 1:2] = jnp.sum(g * n, axis=1, keepdims=True)
        gcol[row, 2:3] = jnp.sum(g, axis=1, keepdims=True)
        s = g * vcol[row, 1:2]
        sg[row] = s
        return (
            total + jnp.sum(s, axis=0, keepdims=True),
            crossed + jnp.sum(s * n, axis=0, keepdims=True),
        )

    total1, crossed1 = unrolled(4, hidden_back, (zero, zero))

    def norm1_back(i, carry):
        row = rows(i, C)
        s = inv1 * (sg[row] - total1 * (1.0 / D) - nrm[row] * (crossed1 * (1.0 / D)))
        sg[row] = s
        low = s.astype(bf16)
        delta[row] = low
        gcol[row, 0:1] = jnp.sum(low.astype(f32), axis=1, keepdims=True)
        return carry

    fo.wait_send()
    out_o_own.wait()
    unrolled(4, norm1_back, 0)
    outt[...] = transposed(delta[...])
    wd_a.direct()

    dc = []
    for i in range(2):
        part = transposed(mm(outt[...], wo2[i].reshape(D, HW)).astype(bf16))
        dct[2 * i : 2 * i + 2] = part.reshape(2, C, TOK)
    dctx[:, tcols] = dct[c]
    for h in range(HEADS):
        hrow = pl.ds(h * HD, HD)
        dc.append(
            triple(
                dct.at[0],
                lambda k: dct.at[lax.rem(c + k, 4), hrow],
                lambda k: dctx.at[hrow, tcols],
                zdev,
            )
        )

    sv[0:8] = transposed(gcol[...])[0:8]
    sv[6:7] = jnp.broadcast_to(jnp.sum(loss_row, axis=1, keepdims=True), (1, D))
    sv[7:8] = jnp.broadcast_to(length.astype(f32), (1, D))
    v_sent = [links.send(sv, rsv.at[0], sib)]
    v_from = [(0, 1)]

    def sv_add():
        v_sent.pop().wait()
        lo, n = v_from[-1]
        total = sv[...]
        for i in range(n):
            total = total + rsv[lo + i]
        sv[...] = total

    def sv_send(dev):
        lo = sum(v_from[-1])
        v_from.append((lo, 3))
        v_sent.append(
            triple(
                rsv.at[pl.ds(lo, 3)], lambda k: sv, lambda k: rsv.at[lo + k - 1], dev
            )
        )

    wait_all(ex_up)
    wd_b.direct()
    wu_a, wu_b = weight_grad(0)
    sv_add()
    sv_send(bdev)
    g = mt(delta[...], ctxa[...].reshape(D, TOK)).astype(bf16)
    for i in range(2):
        gao[i] = g[:, i * HW : (i + 1) * HW].reshape(16, RB, HW)
    go_x = links.send(gao.at[e], gor, sib)
    wd_a.middle()
    wd_b.middle()

    def bwd_head(h, meanwhile=None):
        hrow = pl.ds(h * HD, HD)
        krow = pl.ds(C + h * HD, HD)
        of = h * C

        dk = dv = jnp.zeros((HD, LEN), f32)
        for n in range(LEN // WT):
            at = cols(n, WT)
            inv = linv[h, 0:1, at]
            dc = dctx[hrow, at].astype(f32)
            inner = jnp.sum(dc * ctxt[hrow, at].astype(f32), axis=0, keepdims=True) * inv
            dcs = (dc * inv).astype(bf16)
            probs = pst[h, :, at]
            dv = dv + mt(dcs, probs)
            dp = mm(vtm[h, :, 0:HD], dcs) - inner
            ds = (probs.astype(f32) * dp).astype(bf16)
            dk = dk + mt(qkvt[hrow, at], ds)
            dqkvt[of : of + HD, at] = (mm(qkvt[krow, :], ds) * (HD**-0.5)).astype(bf16)
            if n == 0 and meanwhile is not None:
                meanwhile()
        dqkvt[of + HD : of + 2 * HD] = dk.astype(bf16)
        dqkvt[of + 2 * HD : of + 3 * HD] = dv.astype(bf16)

    spare = HL - QC
    row_iota = lax.broadcasted_iota(jnp.int32, (RB, spare), 0)

    def qkv_grad(h, ref, at):
        of = dqkvt[h * C : (h + 1) * C]
        g = mt(xf[...], of).astype(bf16)
        sums = mt(jnp.ones((8, LEN), bf16), of)[0:1]
        for half in range(2):
            lo = half * QC
            part_rows = jnp.zeros((RB, spare), f32)
            for j in range(3):
                part = sums[:, lo + j * spare : lo + (j + 1) * spare]
                part_rows = jnp.where(row_iota == j, jnp.broadcast_to(part, (RB, spare)), part_rows)
            ref[half, :, :, at : at + QC] = g[:, lo : lo + QC].reshape(16, RB, QC)
            ref[half, :, :, at + QC : at + HL] = jnp.broadcast_to(
                part_rows.astype(bf16)[None], (16, RB, spare)
            )

    dc[0].wait_recv()
    bwd_head(0)
    wu_a.direct()
    wu_b.direct()
    go_x.wait_recv()
    add_sibling(gao, gor)
    o_sum = direct_sum(lambda i: gao.at[d, i], ro)
    o_sum.start()
    dc[1].wait_recv()
    bwd_head(1, lambda: qkv_grad(0, gqa, 0))
    wd_sends = end_b(wd_a, s1.at[1], r2.at[1])
    wu_a.middle()
    wu_b.middle()

    def total_z(w, ring):
        for half in range(2):
            sb0[w, half * 8 : half * 8 + 8] = ring.total(half).astype(bf16)
        ring_b = direct_sum(lambda i: sb0.at[w, i], br.at[w])
        ring_b.start()
        return ring_b

    sv_add()
    sv_send(adev)
    dc[2].wait_recv()
    bwd_head(2, lambda: qkv_grad(1, gqa, HL))

    def dx_part(i):
        row = rows(i, C)
        gi_o[...] = mm(wqkv[row], dqkvt[...])
        gi_o[:, tcols] = gi_o[:, tcols] + sg[row]

    SLOT = {"far": 0, "right": 1, "left": 2}

    def dx_own(at, half):
        return dxp.at[SLOT[at], pl.ds(half * (C // 2), C // 2)]

    dx_sum = RingSum(links, dx_own, rxi, rx, zdev(1), zdev(3), 2)
    dx_part(c_at["far"])
    dxp[0] = gi_o[...].astype(bf16)
    dx_sum.first()
    xa = links.send(gqa.at[e], gra, sib)
    qkv_grad(2, gqb, 0)
    xb = links.send(gqb.at[e], grb, sib)

    dx_part(c_at["right"])
    dxp[1] = gi_o[...].astype(bf16)
    dx_sum.direct_right()
    dx_part(c_at["left"])
    dxp[2] = gi_o[...].astype(bf16)
    dx_sum.direct_left()
    xa.wait_recv()
    add_sibling(gqa, gra)
    qa_sum = direct_sum(lambda i: gqa.at[d, i], rqa)
    qa_sum.start()
    xb.wait_recv()
    add_sibling(gqb, grb)
    qb_sum = direct_sum(lambda i: gqb.at[d, i], rqb)
    qb_sum.start()
    bd_sum = total_z(1, wd_b)
    dx_part(c)
    o_sends = end_b(o_sum, so1, ro2)

    def along_z(w, sends):
        s2[w] = end_a(sends, s1.at[w], r2.at[w]).astype(bf16)
        return triple(
            r3.at[w],
            lambda k: s2.at[w, :, cols(lax.rem(c + k, 4), FA // 2)],
            lambda k: r3.at[w, k - 1],
            zdev,
        )

    w3 = {1: along_z(1, wd_sends)}
    wu_sends = end_b(wu_a, s1.at[0], r2.at[0])
    dx_sum.middle()
    bu_sum = total_z(0, wu_b)
    sv_add()
    sv_send(zdev)
    bd_sends = end_b(bd_sum, sb1.at[1], rb2.at[1])
    qa_sends = end_b(qa_sum, sqa, ra2)
    qb_sends = end_b(qb_sum, sqb, rb3)
    so2[0] = end_a(o_sends, so1, ro2).astype(bf16)
    o_x = links.send(so2.at[0], so2.at[1], sib)
    w3[0] = along_z(0, wu_sends)
    bu_sends = end_b(bu_sum, sb1.at[0], rb2.at[0])
    o_x.wait_recv()
    mine, other = so2[0], so2[1]
    low, high = jnp.where(d == 0, mine, other), jnp.where(d == 0, other, mine)
    so4[0], so4[1] = low[:, 0:C], low[:, C:]
    so4[2], so4[3] = high[:, 0:C], high[:, C:]
    o3 = triple(
        ro3, lambda k: so4.at[lax.rem(c + k, 4)], lambda k: ro3.at[k - 1], zdev
    )
    xb1[0, 1] = end_a(bd_sends, sb1.at[1], rb2.at[1])
    xq1[0, :, 0 : 2 * HL] = end_a(qa_sends, sqa, ra2)
    xq1[0, :, 2 * HL :] = end_a(qb_sends, sqb, rb3)
    q3 = links.send(xq1.at[0], xq1.at[1], sib)
    xb1[0, 0] = end_a(bu_sends, sb1.at[0], rb2.at[0])
    wb4 = links.send(xb1.at[0], xb1.at[1], sib)
    wait_all((w3[1], w3[0]))
    x1[0] = s2[:, :, cols(c, FA // 2)].astype(f32)
    for w in range(2):
        for k in range(3):
            x1[0, w] = x1[0, w] + r3[w, k].astype(f32)
    w4 = links.send(x1.at[0], x1.at[1], sib)
    o3.wait_recv()
    ototal = so4[c].astype(f32)
    for k in range(3):
        ototal = ototal + ro3[k].astype(f32)
    dwo_o[...] = ototal
    sv_add()
    sv_o[...] = sv[...]
    w4.wait_recv()
    dwa_o[d] = x1[0]
    dwa_o[e] = x1[1]
    q3.wait_recv()
    dqkv_o[d] = xq1[0]
    dqkv_o[e] = xq1[1]
    wb4.wait_recv()
    dwb_o[d] = xb1[0]
    dwb_o[e] = xb1[1]
    dx_sum.wait()
    for half in range(2):
        row = pl.ds(half * (C // 2), C // 2)
        gi_o[row] = gi_o[row] + rx[0, half].astype(f32) + rx[1, half].astype(f32)
    for copy in links.all:
        copy.wait()


def finish(
    out_i, gi_i, dwa_i, dwb_i, dwo_i, dqkv_i, sv_i,
    out, loss, gi, gwq, gbq, gwk, gwv, gbv, gwo, gob, gg1, gb1, gup, gub, gdn, gdb, gg2, gb2,
):
    c = lax.axis_index("col")
    out[...] = out_i[...]
    count = sv_i[7:8, 0:1] * 0.25
    factor = SLOTS / count
    loss[0] = jnp.sum(sv_i[6:7, 0:1] / (2.0 * D * count))
    gi[...] = gi_i[...] * factor
    low, high = dqkv_i[0] * factor, dqkv_i[1] * factor
    at = [h * HL for h in range(HEADS)]
    gwq[...] = jnp.concatenate([low[:, i : i + HD] for i in at], axis=1)
    parts = []
    for i in at:
        parts += [low[:, i + HD : i + QC], high[:, i : i + QC - HD]]
    gwk[...] = jnp.concatenate(parts, axis=1)
    gwv[...] = jnp.concatenate([high[:, i + QC - HD : i + QC] for i in at], axis=1)
    gbq[...] = jnp.concatenate([low[j : j + 1, i + QC : i + HL] for i in at for j in (0, 1)], axis=1)
    gbv[...] = jnp.concatenate([high[j : j + 1, i + QC : i + HL] for i in at for j in (1, 2)], axis=1)
    gwo[...] = dwo_i[...] * factor
    for i, ref in enumerate((gup, gdn)):
        for half in range(2):
            ref[:, half * FA // 2 : (half + 1) * FA // 2] = dwa_i[half, i] * factor
            at = FA + half * FB // 2
            ref[:, at : at + FB // 2] = dwb_i[half, i] * factor
    sums = sv_i[...] * factor
    for j in range(4):

        @pl.when(c == j)
        def _(j=j):
            for i in range(4):
                gub[i : i + 1] = sums[8 + j : 9 + j, i * 128 : (i + 1) * 128]
            for i in range(2):
                at = (j % 2) * FB + i * 128
                gub[4 + i : 5 + i] = sums[12 + j // 2 : 13 + j // 2, at : at + 128]
            for i, ref in enumerate((gob, gg1, gb1, gdb, gg2, gb2)):
                ref[...] = sums[i : i + 1, j * C : (j + 1) * C]


def local_step(
    inputs, teacher, lengths, query_weight, query_bias, key_weight, value_weight, value_bias,
    output_weight, output_bias, first_gain, first_shift, up_weight, up_bias, down_weight,
    down_bias, second_gain, second_shift,
):
    anyspec = pl.BlockSpec(memory_space=pl.ANY)
    vm = pl.BlockSpec(memory_space=pltpu.VMEM)
    sds = jax.ShapeDtypeStruct
    V = pltpu.VMEM
    vectors = [
        v.reshape(1, -1)
        for v in (
            output_bias, first_gain, first_shift, down_bias, second_gain, second_shift,
            query_bias, value_bias,
        )
    ]
    vectors.append(up_bias.reshape(6, 128))
    got = pl.pallas_call(
        layer,
        name="layer",
        out_shape=(
            sds((C, LEN), bf16),
            sds((C, LEN), f32),
            sds((2, 2, RB, FA // 2), f32),
            sds((2, 2, RB, FB // 2), f32),
            sds((RB, C), f32),
            sds((2, RB, HW), f32),
            sds((16, D), f32),
        ),
        in_specs=[anyspec, anyspec, pl.BlockSpec(memory_space=pltpu.SMEM)]
        + [vm] * 4
        + [anyspec] * 2
        + [vm] * 9,
        out_specs=(anyspec, vm, vm, vm, vm, vm, vm),
        scratch_shapes=[
            V((D, LEN), bf16),
            V((4, C, TOK), bf16),
            V((2, 16, RB, 4 * FA), bf16),
            V((2, 16, RB, 4 * FB), bf16),
            V((2, 16, RB, HW), bf16),
            V((2, 16, RB, HW), bf16),
            V((4, RB, C), bf16),
            V((D, 3 * C), bf16),
            V((4, 16, C), f32),
            V((4, 8, D), f32),
            V((D, 128), f32),
            V((2 * C, LEN), bf16),
            V((HEADS, LEN, 2 * HD), bf16),
            V((HEADS, 2 * HD, LEN), bf16),
            V((HEADS, HD + 16, LEN), bf16),
            V((HEADS, LEN, 2 * HD), bf16),
            V((HEADS, LEN, LEN), bf16),
            V((HEADS, 8, LEN), f32),
            V((C, LEN), bf16),
            V((4, C, TOK), bf16),
            V((D, TOK), f32),
            V((D, TOK), f32),
            V((D, TOK), f32),
            V((2, 2, TOK, FF // 2), bf16),
            V((2, D, TOK), bf16),
            V((TOK, FF), bf16),
            V((2, TOK, FF // 2), bf16),
            V((2, D, TOK), bf16),
            V((2, 16, RB, 2 * FA), bf16),
            V((2, 16, RB, 2 * FB), bf16),
            V((2, 16, RB, 2 * HL), bf16),
            V((2, 16, RB, HL), bf16),
            V((16, RB, 2 * HL), bf16),
            V((16, RB, HL), bf16),
            V((2, 16, RB, HW), bf16),
            V((16, RB, HW), bf16),
            V((C, LEN), bf16),
            V((4, C, TOK), bf16),
            V((TOK, D), bf16),
            V((D, TOK), bf16),
            V((3 * C, LEN), bf16),
            V((3, C, LEN), bf16),
            V((2, C // 2, LEN), bf16),
            V((2, 2, C // 2, LEN), bf16),
            V((2, 4, RB, 2 * FA), bf16),
            V((2, 2, 4, RB, 2 * FA), bf16),
            V((2, 4, RB, 2 * FA), bf16),
            V((2, 3, RB, 2 * FA), bf16),
            V((2, RB, 2 * FA), bf16),
            V((2, 3, RB, FA // 2), bf16),
            V((2, 2, 8, RB, FB // 2), bf16),
            V((2, 2, 2, 8, RB, FB // 2), bf16),
            V((2, 16, RB, FB // 2), bf16),
            V((2, 3, 4, RB, FB // 2), bf16),
            V((2, 4, RB, FB // 2), bf16),
            V((2, 3, RB, FB // 2), bf16),
            V((3, 4, RB, 2 * HL), bf16),
            V((3, 4, RB, HL), bf16),
            V((4, RB, 2 * HL), bf16),
            V((4, RB, HL), bf16),
            V((3, RB, 2 * HL), bf16),
            V((3, RB, HL), bf16),
            V((3, 4, RB, HW), bf16),
            V((4, RB, HW), bf16),
            V((3, RB, HW), bf16),
            V((2, RB, HW), bf16),
            V((4, RB, C), bf16),
            V((3, RB, C), bf16),
            V((2, 2, RB, FA // 2), f32),
            V((2, 2, RB, FB // 2), f32),
            V((2, RB, HW), f32),
            V((D, 128), f32),
            V((16, D), f32),
            V((10, 16, D), f32),
            V((2, RB, D), bf16),
            pltpu.SemaphoreType.DMA((12,)),
            pltpu.SemaphoreType.DMA((N_SEM,)),
            pltpu.SemaphoreType.DMA((N_SEM,)),
        ],
        compiler_params=pltpu.CompilerParams(
            collective_id=0, has_side_effects=True, vmem_limit_bytes=62 * 2**20
        ),
    )(
        inputs, teacher, lengths, query_weight, key_weight, value_weight, output_weight.T,
        up_weight, down_weight, *vectors,
    )
    vector = sds((1, C), f32)
    weight = sds((RB, C), f32)
    wide = sds((RB, D), f32)
    done = pl.pallas_call(
        finish,
        name="finish",
        out_shape=(
            sds((C, LEN), bf16), sds((1,), f32), sds((C, LEN), f32),
            weight, vector, weight, weight, vector, weight,
            vector, vector, vector, wide, sds((6, 128), f32), wide, vector, vector, vector,
        ),
        in_specs=[vm] * 7,
        out_specs=(vm, pl.BlockSpec(memory_space=pltpu.SMEM)) + (vm,) * 16,
    )(*got)
    shapes = [
        (C, LEN), (), (C, LEN), (RB, C), (C,), (RB, C), (RB, C), (C,), (RB, C), (C,), (C,), (C,),
        (RB, D), (D,), (RB, D), (C,), (C,), (C,),
    ]
    done = [o.reshape(shape) for o, shape in zip(done, shapes)]
    done[8] = done[8].T
    return tuple(done)


def solution(mesh):
    split = Mesh(
        mesh.devices.reshape(mesh.shape["dp"], 4, 4, mesh.shape["col"]), AXES
    )
    tokens = P("col", DP_ROW)
    weight = P(ROW, "col")
    vector = P("col")
    return jax.shard_map(
        local_step,
        mesh=split,
        in_specs=(
            tokens, tokens, P(DP_ROW), weight, vector, weight, weight, vector,
            P("col", ROW), vector, vector, vector, weight, vector, weight,
            vector, vector, vector,
        ),
        out_specs=(
            tokens, P(), tokens, weight, vector, weight, weight, vector,
            P("col", ROW), vector, vector, vector, weight, vector, weight,
            vector, vector, vector,
        ),
        check_vma=False,
    )
```

time: 114 us -> 102 us (0.89)
  Pallas kernels: 112 us -> 99.8 us
    pallas_call x1, Pallas kernels: 109 us -> 96.9 us  [local_step(): pl.pallas_call(layer, name='layer', out_shape=(sds((C, LEN), bf16), sds((...]
where the time goes in v5:
time: 102 us; the launch traced here: 101 us
  Pallas kernels  99.8 us (98%)
  between operations  1.5 us (1%)
    pallas_call x1, Pallas kernels, local_step(): pl.pallas_call(layer, name='layer', out_shape=(sds((C, LEN), bf16), sds((...  96.9 us
    pallas_call x1, Pallas kernels, local_step(): pl.pallas_call(finish, name='finish', out_shape=(sds((C, LEN), bf16), sds...  2.9 us

profile of v5, /device:TPU:1, one launch (start us, length us, event | category | flops | bytes accessed | tf_op | source)
XLA Modules:
  0.0 101.3 jit_solution(3636714936910718970)
XLA Ops:
  1.3 96.9 %layer.1 = (bf16[192,1024]{1,0:T(8,128)(2,1)}, f32[192,1024]{1,0:T(8,128)}, f32[2,2,48,256]{3,2,1,0:T(8,128)}, f32[2,2,48,128]{3,2,1,0:T(8,128)}, f32[48,192]{1,...) custom-call(bf16[192,1024]{1,0:T(8,128)(2,1)} %x_in.1, bf16[192,1024]{1,0:T(8,128)(2,1)} %t_in.1, ...), custom_call_target="tpu_custom_call" | custom-call | tf_op jit(solution)/shard_map/layer/pallas_call | solution.py:1114
  98.3 2.9 %finish.1 = (bf16[192,1024]{1,0:T(8,128)(2,1)}, f32[1]{0:T(128)}, f32[192,1024]{1,0:T(8,128)}, f32[48,192]{1,0:T(8,128)}, f32[1,192]{1,0:T(1,128)}, /*index=5*/f...) custom-call(bf16[192,1024]{1,0:T(8,128)(2,1)} %get-tuple-element.43., ...), custom_call_target="tpu_custom_call" | custom-call | tf_op jit(solution)/shard_map/finish/pallas_call | solution.py:1221

commit v6 on v5

--- a/solution.py
+++ b/solution.py
@@ -28,7 +28,6 @@
 FA = 512
 FB = 256
 WT = 512
-WF = 1024
 QH = 288
 HW = 384
 f32 = jnp.float32
@@ -262,7 +261,7 @@
     ga, gb, gqa, gqb, gra, grb, gao, gor, dctx, dct, outt, delta,
     dqkvt, dxp, rxi, rx, im, rm, s1, r2, s2, r3, zi, zr, sb0, br, sb1, rb2,
     rqa, rqb, sqa, sqb, ra2, rb3, ro, so1, ro2, so2, so4, ro3,
-    x1, xb1, xq1, gcol, sv, rsv, wown,
+    x1, xb1, xq1, stat, gcol, sv, rsv, wown, wqs, vrow, ubs,
     lsem, ssem, rsem,
 ):
     d = lax.axis_index("dp")
@@ -309,6 +308,11 @@
             batch.send(src(k), dst(k), dev(k))
         return batch
 
+    def region(body):
+        @pl.when(e + d == 1 + d * e)
+        def _():
+            body()
+
     def unrolled(n, body, carry):
         for i in range(n):
             carry = body(i, carry)
@@ -339,15 +343,20 @@
         for dev in (zdev(k), adev(k), bdev(k)):
             pl.semaphore_signal(bar, inc=1, device_id=dev, device_id_type=pl.DeviceIdType.MESH)
     pl.semaphore_signal(bar, inc=1, device_id=sib, device_id_type=pl.DeviceIdType.MESH)
+    cw = [local(ref, wqs.at[i]) for i, ref in enumerate((wq_in, wk_in, wv_in))]
     cup = local(up_in, wown.at[0])
     cdn = local(down_in, wown.at[1])
     cx = local(x_in, xf.at[xrows])
     ct = local(t_in.at[:, tcols], tf.at[c])
-    wo4[c] = wo_in[...]
-    for i, ref in enumerate((ob_in, g1_in, b1_in, db_in, g2_in, b2_in, qb_in, vb_in)):
-        vec[c, i : i + 1, :] = ref[...].reshape(1, C)
-    ub[c, 0:1, :] = jnp.concatenate([ub_in[i : i + 1] for i in range(6)], axis=1)
-    own_qkv = [w[...] for w in (wq_in, wk_in, wv_in)]
+    cwo = local(wo_in, wo4.at[c])
+    cv = [
+        local(ref, vrow.at[i])
+        for i, ref in enumerate((ob_in, g1_in, b1_in, db_in, g2_in, b2_in, qb_in, vb_in))
+    ]
+    cub = local(ub_in, ubs)
+    for copy in cw:
+        copy.wait()
+    own_qkv = [wqs[i] for i in range(3)]
     own_qkv = jnp.concatenate(
         [w[:, h * HD : (h + 1) * HD] for h in range(HEADS) for w in own_qkv], axis=1
     )
@@ -411,6 +420,12 @@
         zdev(1), zdev(3), (0,), (1,),
     )
     x_z.first()
+    cwo.wait()
+    for i, copy in enumerate(cv):
+        copy.wait()
+        vec[c, i : i + 1, :] = vrow[i]
+    cub.wait()
+    ub[c, 0:1, :] = jnp.concatenate([ubs[i : i + 1] for i in range(6)], axis=1)
     oz = triple(wo4.at[pl.ds(0, 3)], lambda k: wo4.at[c], lambda k: wo4.at[c], zdev)
     vz = triple(vec.at[pl.ds(0, 3)], lambda k: vec.at[c], lambda k: vec.at[c], zdev)
     uz = triple(
@@ -479,12 +494,6 @@
     wb_s = ToSibling(wb.at[d])
     wb_s.send(wb.at[d, :, :, cols(c, FB)])
     wq_s.wait()
-    w_low = transposed(wq2[0].reshape(D, HW))[0:QH]
-    w_high = transposed(wq2[1].reshape(D, HW))[0:QH]
-    dxp[0, :, 0:D] = w_low[0:C]
-    dxp[1, 0 : QH - C, 0:D] = w_low[C:]
-    dxp[1, QH - C :, 0:D] = w_high[0 : QH - C]
-    dxp[2, :, 0:D] = w_high[QH - C :]
     q_bias = vown[:, 6:7]
     v_bias = vown[:, 7:8]
     lane_iota = lax.broadcasted_iota(jnp.int32, (1, TOK), 1)
@@ -514,7 +523,14 @@
             vtm[h, at, :] = transposed(jnp.concatenate([v, ones], axis=0))
         return carry
 
+    w_low = transposed(wq2[0].reshape(D, HW))[0:QH]
+    w_high = transposed(wq2[1].reshape(D, HW))[0:QH]
+    dxp[0, :, 0:D] = w_low[0:C]
+    dxp[1, 0 : QH - C, 0:D] = w_low[C:]
+    dxp[1, QH - C :, 0:D] = w_high[0 : QH - C]
+    dxp[2, :, 0:D] = w_high[QH - C :]
     unrolled(4, qkv_chunk, 0)
+
     wb_zg.rest()
 
     def fwd_head(h):
@@ -575,31 +591,35 @@
         zdev,
     )
 
-    acc = xf[:, tcols].astype(f32) + vcol[:, 0:1]
-    for j in range(2):
-        w = wo2[j].reshape(D, HW)
-        acc = acc + mm(w, ctxa[2 * j : 2 * j + 2].reshape(HW, TOK))
-    hid[...] = acc
-
     def norm_stats(ref):
         v = ref[...]
         mean = jnp.sum(v, axis=0, keepdims=True) * (1.0 / D)
         square = jnp.sum(v * v, axis=0, keepdims=True) * (1.0 / D)
         return mean, lax.rsqrt(square - mean * mean + EPS)
 
-    mean1, inv1 = norm_stats(hid)
-
-    def norm1(i, carry):
-        row = rows(i, C)
-        n = (hid[row] - mean1) * inv1
-        nrm[row] = n
-        h = n * vcol[row, 1:2] + vcol[row, 2:3]
-        hid[row] = h + vcol[row, 3:4]
-        astore[0, row] = h.astype(bf16)
-        return carry
-
-    unrolled(4, norm1, 0)
-    outt[...] = transposed(astore[0])
+
+    @region
+    def _():
+        acc = xf[:, tcols].astype(f32) + vcol[:, 0:1]
+        for j in range(2):
+            w = wo2[j].reshape(D, HW)
+            acc = acc + mm(w, ctxa[2 * j : 2 * j + 2].reshape(HW, TOK))
+        hid[...] = acc
+        mean1, inv1 = norm_stats(hid)
+        stat[0:1] = inv1
+
+        def norm1(i, carry):
+            row = rows(i, C)
+            n = (hid[row] - mean1) * inv1
+            nrm[row] = n
+            h = n * vcol[row, 1:2] + vcol[row, 2:3]
+            hid[row] = h + vcol[row, 3:4]
+            astore[0, row] = h.astype(bf16)
+            return carry
+
+        unrolled(4, norm1, 0)
+        outt[...] = transposed(astore[0])
+
     for at in ("left", "right"):
         wb_zg.wait(at)
         wb_s.send(wb.at[d, :, :, cols(c_at[at], FB)])
@@ -607,39 +627,28 @@
     wa_s.wait()
 
     def w_chunk(ref, i):
-        return ref[:, :, cols(i, WF)].reshape(D, WF)
+        return ref[:, :, cols(i, FA)].reshape(D, FA)
+
+    def halves(chunk):
+        if chunk < 4:
+            return [(half, chunk * FA // 2, FA // 2) for half in range(2)]
+        pairs = [(half, j) for j in (2 * chunk - 8, 2 * chunk - 7) for half in range(2)]
+        return [(half, 2 * FA + j * FB // 2, FB // 2) for half, j in pairs]
 
     def store_halves(w, chunk, v):
-        if isinstance(chunk, int) and chunk == 2:
-            for j in range(4):
-                for half in range(2):
-                    at = j * FB + half * FB // 2
-                    to = 4 * FA // 2 + j * FB // 2
-                    bstore[w, half, :, to : to + FB // 2] = v[:, at : at + FB // 2]
-        else:
-            for j in range(2):
-                for half in range(2):
-                    at = j * FA + half * FA // 2
-                    bstore[w, half, :, cols(2 * chunk + j, FA // 2)] = v[:, at : at + FA // 2]
+        at = 0
+        for half, to, width in halves(chunk):
+            bstore[w, half, :, to : to + width] = v[:, at : at + width]
+            at += width
 
     def load_halves(w, chunk):
-        if isinstance(chunk, int) and chunk == 2:
-            return jnp.concatenate(
-                [
-                    bstore[w, half, :, 2 * FA + j * FB // 2 : 2 * FA + (j + 1) * FB // 2]
-                    for j in range(4)
-                    for half in range(2)
-                ],
-                axis=1,
-            )
         return jnp.concatenate(
-            [bstore[w, half, :, cols(2 * chunk + j, FA // 2)] for j in range(2) for half in range(2)],
-            axis=1,
+            [bstore[w, half, :, to : to + width] for half, to, width in halves(chunk)], axis=1
         )
 
     def up_of(ref, bias, first):
         def up_chunk(i, carry):
-            at = cols(first + i, WF)
+            at = cols(first + i, FA)
             pre = mm(outt[...], w_chunk(ref, i)) + bias(i)
             half = 0.5 * (1.0 + lax.erf(pre * ROOT_HALF))
             store_halves(1, first + i, (pre * half).astype(bf16))
@@ -649,14 +658,12 @@
         return up_chunk
 
     def bias_a(i):
-        return jnp.concatenate([ub[2 * i, 0:1, 0:FA], ub[2 * i + 1, 0:1, 0:FA]], axis=1)
+        return ub[i, 0:1, 0:FA]
 
     def bias_b(i):
-        return jnp.concatenate([ub[j, 0:1, FA:] for j in range(4)], axis=1)
-
-    lax.fori_loop(0, 2, up_of(wa.at[0], bias_a, 0), 0)
-    wb_zg.wait("far")
-    wb_s.send(wb.at[d, :, :, cols(c_at["far"], FB)])
+        return jnp.concatenate([ub[2 * i, 0:1, FA:], ub[2 * i + 1, 0:1, FA:]], axis=1)
+
+    region(lambda: unrolled(4, up_of(wa.at[0], bias_a, 0), 0))
 
     def down_of(ref, first):
         def down_chunk(i, carry):
@@ -665,37 +672,51 @@
 
         return down_chunk
 
-    lax.fori_loop(0, 2, down_of(wa.at[1], 0), 0)
+    region(lambda: unrolled(4, down_of(wa.at[1], 0), 0))
+    wb_zg.wait("far")
+    wb_s.send(wb.at[d, :, :, cols(c_at["far"], FB)])
     wb_s.wait()
-    unrolled(1, up_of(wb.at[0], bias_b, 2), 0)
-    unrolled(1, down_of(wb.at[1], 2), 0)
-
-    mean2, inv2 = norm_stats(hid)
+
+    @region
+    def _():
+        unrolled(2, up_of(wb.at[0], bias_b, 4), 0)
+        unrolled(2, down_of(wb.at[1], 4), 0)
+
+    ex_down = [links.send(bstore.at[1, e], brecv.at[1], sib)]
+
     tt.wait_recv()
     valid = lane_iota + c * TOK < length
-    gcol[...] = jnp.zeros(gcol.shape, f32)
-    sv[...] = jnp.zeros(sv.shape, f32)
-
-    def norm2(i, carry):
-        total, crossed, loss = carry
-        row = rows(i, C)
-        n = (hid[row] - mean2) * inv2
-        hid[row] = n
-        final = n * vcol[row, 4:5] + vcol[row, 5:6]
-        delta[row] = final.astype(bf16)
-        g = jnp.where(valid, final - tf[i].astype(f32), 0.0)
-        gcol[row, 4:5] = jnp.sum(g * n, axis=1, keepdims=True)
-        gcol[row, 5:6] = jnp.sum(g, axis=1, keepdims=True)
-        s = g * vcol[row, 4:5]
-        sg[row] = s
-        return (
-            total + jnp.sum(s, axis=0, keepdims=True),
-            crossed + jnp.sum(s * n, axis=0, keepdims=True),
-            loss + jnp.sum(g * g, axis=0, keepdims=True),
-        )
 
     zero = jnp.zeros((1, TOK), f32)
-    total2, crossed2, loss_row = unrolled(4, norm2, (zero, zero, zero))
+
+    @region
+    def _():
+        mean2, inv2 = norm_stats(hid)
+        gcol[...] = jnp.zeros(gcol.shape, f32)
+        sv[...] = jnp.zeros(sv.shape, f32)
+
+        def norm2(i, carry):
+            total, crossed, loss = carry
+            row = rows(i, C)
+            n = (hid[row] - mean2) * inv2
+            hid[row] = n
+            final = n * vcol[row, 4:5] + vcol[row, 5:6]
+            delta[row] = final.astype(bf16)
+            g = jnp.where(valid, final - tf[i].astype(f32), 0.0)
+            gcol[row, 4:5] = jnp.sum(g * n, axis=1, keepdims=True)
+            gcol[row, 5:6] = jnp.sum(g, axis=1, keepdims=True)
+            s = g * vcol[row, 4:5]
+            sg[row] = s
+            return (
+                total + jnp.sum(s, axis=0, keepdims=True),
+                crossed + jnp.sum(s * n, axis=0, keepdims=True),
+                loss + jnp.sum(g * g, axis=0, keepdims=True),
+            )
+
+        total2, crossed2, loss_row = unrolled(4, norm2, (zero, zero, zero))
+        for i, row in enumerate((inv2, total2, crossed2, loss_row)):
+            stat[1 + i : 2 + i] = row
+
     out_o_own = local(delta.at[xrows], out_o.at[:, tcols])
     fo = triple(
         delta.at[pl.ds(0, 3 * C)],
@@ -706,40 +727,42 @@
 
     def norm2_back(i, carry):
         row = rows(i, C)
-        s = inv2 * (sg[row] - total2 * (1.0 / D) - hid[row] * (crossed2 * (1.0 / D)))
+        s = stat[1:2] * (sg[row] - stat[2:3] * (1.0 / D) - hid[row] * (stat[3:4] * (1.0 / D)))
         sg[row] = s
         low = s.astype(bf16)
         astore[1, row] = low
         gcol[row, 3:4] = jnp.sum(low.astype(f32), axis=1, keepdims=True)
         return carry
 
-    unrolled(4, norm2_back, 0)
-
-    def exchange(w):
-        return [
-            links.send(astore.at[w], arecv.at[w], sib),
-            links.send(bstore.at[w, e], brecv.at[w], sib),
-        ]
-
-    ex_down = exchange(1)
-    outt[...] = transposed(astore[1])
+    @region
+    def _():
+        unrolled(4, norm2_back, 0)
+        outt[...] = transposed(astore[1])
+
+
+    ex_down.append(links.send(astore.at[1], arecv.at[1], sib))
 
     def act_of(ref, first):
         def act_chunk(i, carry):
-            at = cols(first + i, WF)
+            at = cols(first + i, FA)
             g = mm(outt[...], w_chunk(ref, i)) * slope[:, at].astype(f32)
             low = g.astype(bf16)
             store_halves(0, first + i, low)
             total = jnp.sum(low.astype(f32), axis=0, keepdims=True)
-            sv[pl.ds(8 + 2 * (first + i), 1), 0:FA] = total[:, 0:FA]
-            sv[pl.ds(9 + 2 * (first + i), 1), 0:FA] = total[:, FA:]
+            sv[8 + first + i : 9 + first + i, 0:FA] = total
             return carry
 
         return act_chunk
 
-    unrolled(1, act_of(wb.at[1], 2), 0)
-    lax.fori_loop(0, 2, act_of(wa.at[1], 0), 0)
-    ex_up = exchange(0)
+    @region
+    def _():
+        unrolled(2, act_of(wb.at[1], 4), 0)
+        unrolled(4, act_of(wa.at[1], 0), 0)
+
+    ex_up = [
+        links.send(astore.at[0], arecv.at[0], sib),
+        links.send(bstore.at[0, e], brecv.at[0], sib),
+    ]
 
     def back_of(ref, first):
         def back_chunk(i, carry):
@@ -783,11 +806,13 @@
         unrolled(16, add, 0)
 
     def weight_grad(w):
-        for at, ref in ((0, ga), (2 * FA, gb)):
-            for lo in range(0, ref.shape[3], FA):
-                cut = pl.ds(at + lo, FA)
-                g = mm(astore[w], bstore[w, d, :, cut]) + mm(arecv[w], brecv[w, :, cut])
-                ref[w, :, :, lo : lo + FA] = g.astype(bf16).reshape(16, RB, FA)
+        @region
+        def _():
+            for at, ref in ((0, ga), (2 * FA, gb)):
+                for lo in range(0, ref.shape[3], FA):
+                    cut = pl.ds(at + lo, FA)
+                    g = mm(astore[w], bstore[w, d, :, cut]) + mm(arecv[w], brecv[w, :, cut])
+                    ref[w, :, :, lo : lo + FA] = g.astype(bf16).reshape(16, RB, FA)
 
         def z_own(at, half):
             return gb.at[w, pl.ds(half * 8, 8), :, cols(c_at[at], FB // 2)]
@@ -798,10 +823,10 @@
         b_ring.first()
         return a_ring, b_ring
 
-    unrolled(1, back_of(wb.at[0], 2), 0)
+    region(lambda: unrolled(2, back_of(wb.at[0], 4), 0))
     wait_all(ex_down)
     wd_a, wd_b = weight_grad(1)
-    lax.fori_loop(0, 2, back_of(wa.at[0], 0), 0)
+    region(lambda: unrolled(4, back_of(wa.at[0], 0), 0))
 
     def hidden_back(i, carry):
         total, crossed = carry
@@ -817,28 +842,33 @@
             crossed + jnp.sum(s * n, axis=0, keepdims=True),
         )
 
-    total1, crossed1 = unrolled(4, hidden_back, (zero, zero))
-
-    def norm1_back(i, carry):
-        row = rows(i, C)
-        s = inv1 * (sg[row] - total1 * (1.0 / D) - nrm[row] * (crossed1 * (1.0 / D)))
-        sg[row] = s
-        low = s.astype(bf16)
-        delta[row] = low
-        gcol[row, 0:1] = jnp.sum(low.astype(f32), axis=1, keepdims=True)
-        return carry
 
     fo.wait_send()
     out_o_own.wait()
-    unrolled(4, norm1_back, 0)
-    outt[...] = transposed(delta[...])
     wd_a.direct()
 
+    @region
+    def _():
+        total1, crossed1 = unrolled(4, hidden_back, (zero, zero))
+
+        def norm1_back(i, carry):
+            row = rows(i, C)
+            s = stat[0:1] * (sg[row] - total1 * (1.0 / D) - nrm[row] * (crossed1 * (1.0 / D)))
+            sg[row] = s
+            low = s.astype(bf16)
+            delta[row] = low
+            gcol[row, 0:1] = jnp.sum(low.astype(f32), axis=1, keepdims=True)
+            return carry
+
+        unrolled(4, norm1_back, 0)
+        outt[...] = transposed(delta[...])
+        for i in range(2):
+            part = transposed(mm(outt[...], wo2[i].reshape(D, HW)).astype(bf16))
+            dct[2 * i : 2 * i + 2] = part.reshape(2, C, TOK)
+        dctx[:, tcols] = dct[c]
+
+
     dc = []
-    for i in range(2):
-        part = transposed(mm(outt[...], wo2[i].reshape(D, HW)).astype(bf16))
-        dct[2 * i : 2 * i + 2] = part.reshape(2, C, TOK)
-    dctx[:, tcols] = dct[c]
     for h in range(HEADS):
         hrow = pl.ds(h * HD, HD)
         dc.append(
@@ -851,7 +881,7 @@
         )
 
     sv[0:8] = transposed(gcol[...])[0:8]
-    sv[6:7] = jnp.broadcast_to(jnp.sum(loss_row, axis=1, keepdims=True), (1, D))
+    sv[6:7] = jnp.broadcast_to(jnp.sum(stat[4:5], axis=1, keepdims=True), (1, D))
     sv[7:8] = jnp.broadcast_to(length.astype(f32), (1, D))
     v_sent = [links.send(sv, rsv.at[0], sib)]
     v_from = [(0, 1)]
@@ -878,9 +908,13 @@
     wu_a, wu_b = weight_grad(0)
     sv_add()
     sv_send(bdev)
-    g = mt(delta[...], ctxa[...].reshape(D, TOK)).astype(bf16)
-    for i in range(2):
-        gao[i] = g[:, i * HW : (i + 1) * HW].reshape(16, RB, HW)
+
+    @region
+    def _():
+        g = mt(delta[...], ctxa[...].reshape(D, TOK)).astype(bf16)
+        for i in range(2):
+            gao[i] = g[:, i * HW : (i + 1) * HW].reshape(16, RB, HW)
+
     go_x = links.send(gao.at[e], gor, sib)
     wd_a.middle()
     wd_b.middle()
@@ -937,9 +971,6 @@
     dc[1].wait_recv()
     bwd_head(1, lambda: qkv_grad(0, gqa, 0))
     wd_sends = end_b(wd_a, s1.at[1], r2.at[1])
-    wu_a.middle()
-    wu_b.middle()
-
     def total_z(w, ring):
         for half in range(2):
             sb0[w, half * 8 : half * 8 + 8] = ring.total(half).astype(bf16)
@@ -947,15 +978,23 @@
         ring_b.start()
         return ring_b
 
+    wu_a.middle()
+    wu_b.middle()
+
+
     sv_add()
     sv_send(adev)
     dc[2].wait_recv()
     bwd_head(2, lambda: qkv_grad(1, gqa, HL))
 
-    def dx_part(i):
-        row = rows(i, C)
-        gi_o[...] = mm(wqkv[row], dqkvt[...])
-        gi_o[:, tcols] = gi_o[:, tcols] + sg[row]
+    def dx_part(i, slot=None):
+        @region
+        def _():
+            row = rows(i, C)
+            gi_o[...] = mm(wqkv[row], dqkvt[...])
+            gi_o[:, tcols] = gi_o[:, tcols] + sg[row]
+            if slot is not None:
+                dxp[slot] = gi_o[...].astype(bf16)
 
     SLOT = {"far": 0, "right": 1, "left": 2}
 
@@ -963,18 +1002,16 @@
         return dxp.at[SLOT[at], pl.ds(half * (C // 2), C // 2)]
 
     dx_sum = RingSum(links, dx_own, rxi, rx, zdev(1), zdev(3), 2)
-    dx_part(c_at["far"])
-    dxp[0] = gi_o[...].astype(bf16)
+    dx_part(c_at["far"], 0)
     dx_sum.first()
+    bd_sum = total_z(1, wd_b)
     xa = links.send(gqa.at[e], gra, sib)
-    qkv_grad(2, gqb, 0)
+    region(lambda: qkv_grad(2, gqb, 0))
     xb = links.send(gqb.at[e], grb, sib)
 
-    dx_part(c_at["right"])
-    dxp[1] = gi_o[...].astype(bf16)
+    dx_part(c_at["right"], 1)
     dx_sum.direct_right()
-    dx_part(c_at["left"])
-    dxp[2] = gi_o[...].astype(bf16)
+    dx_part(c_at["left"], 2)
     dx_sum.direct_left()
     xa.wait_recv()
     add_sibling(gqa, gra)
@@ -984,7 +1021,6 @@
     add_sibling(gqb, grb)
     qb_sum = direct_sum(lambda i: gqb.at[d, i], rqb)
     qb_sum.start()
-    bd_sum = total_z(1, wd_b)
     dx_part(c)
     o_sends = end_b(o_sum, so1, ro2)
 
@@ -1003,9 +1039,9 @@
     bu_sum = total_z(0, wu_b)
     sv_add()
     sv_send(zdev)
-    bd_sends = end_b(bd_sum, sb1.at[1], rb2.at[1])
     qa_sends = end_b(qa_sum, sqa, ra2)
     qb_sends = end_b(qb_sum, sqb, rb3)
+    bd_sends = end_b(bd_sum, sb1.at[1], rb2.at[1])
     so2[0] = end_a(o_sends, so1, ro2).astype(bf16)
     o_x = links.send(so2.at[0], so2.at[1], sib)
     w3[0] = along_z(0, wu_sends)
@@ -1018,18 +1054,18 @@
     o3 = triple(
         ro3, lambda k: so4.at[lax.rem(c + k, 4)], lambda k: ro3.at[k - 1], zdev
     )
-    xb1[0, 1] = end_a(bd_sends, sb1.at[1], rb2.at[1])
     xq1[0, :, 0 : 2 * HL] = end_a(qa_sends, sqa, ra2)
     xq1[0, :, 2 * HL :] = end_a(qb_sends, sqb, rb3)
     q3 = links.send(xq1.at[0], xq1.at[1], sib)
-    xb1[0, 0] = end_a(bu_sends, sb1.at[0], rb2.at[0])
-    wb4 = links.send(xb1.at[0], xb1.at[1], sib)
     wait_all((w3[1], w3[0]))
     x1[0] = s2[:, :, cols(c, FA // 2)].astype(f32)
     for w in range(2):
         for k in range(3):
             x1[0, w] = x1[0, w] + r3[w, k].astype(f32)
     w4 = links.send(x1.at[0], x1.at[1], sib)
+    xb1[0, 1] = end_a(bd_sends, sb1.at[1], rb2.at[1])
+    xb1[0, 0] = end_a(bu_sends, sb1.at[0], rb2.at[0])
+    wb4 = links.send(xb1.at[0], xb1.at[1], sib)
     o3.wait_recv()
     ototal = so4[c].astype(f32)
     for k in range(3):
@@ -1123,10 +1159,7 @@
             sds((2, RB, HW), f32),
             sds((16, D), f32),
         ),
-        in_specs=[anyspec, anyspec, pl.BlockSpec(memory_space=pltpu.SMEM)]
-        + [vm] * 4
-        + [anyspec] * 2
-        + [vm] * 9,
+        in_specs=[anyspec, anyspec, pl.BlockSpec(memory_space=pltpu.SMEM)] + [anyspec] * 15,
         out_specs=(anyspec, vm, vm, vm, vm, vm, vm),
         scratch_shapes=[
             V((D, LEN), bf16),
@@ -1200,11 +1233,15 @@
             V((2, 2, RB, FA // 2), f32),
             V((2, 2, RB, FB // 2), f32),
             V((2, RB, HW), f32),
+            V((8, TOK), f32),
             V((D, 128), f32),
             V((16, D), f32),
             V((10, 16, D), f32),
             V((2, RB, D), bf16),
-            pltpu.SemaphoreType.DMA((12,)),
+            V((3, RB, C), bf16),
+            V((8, 1, C), f32),
+            V((6, 128), f32),
+            pltpu.SemaphoreType.DMA((20,)),
             pltpu.SemaphoreType.DMA((N_SEM,)),
             pltpu.SemaphoreType.DMA((N_SEM,)),
         ],

time: 102 us -> 99.3 us (0.974)
  Pallas kernels: 99.8 us -> 97.6 us
    pallas_call x1, Pallas kernels: 96.9 us -> 94.7 us  [local_step(): pl.pallas_call(layer, name='layer', out_shape=(sds((C, LEN), bf16), sds((...]
where the time goes in v6:
time: 99.3 us; the launch traced here: 99.1 us
  Pallas kernels  97.6 us (98%)
  between operations  1.5 us (2%)
    pallas_call x1, Pallas kernels, local_step(): pl.pallas_call(layer, name='layer', out_shape=(sds((C, LEN), bf16), sds((...  94.7 us
    pallas_call x1, Pallas kernels, local_step(): pl.pallas_call(finish, name='finish', out_shape=(sds((C, LEN), bf16), sds...  2.9 us

profile of v6, /device:TPU:1, one launch (start us, length us, event | category | flops | bytes accessed | tf_op | source)
XLA Modules:
  0.0 99.1 jit_solution(16111913585579362000)
XLA Ops:
  1.3 94.7 %layer.1 = (bf16[192,1024]{1,0:T(8,128)(2,1)}, f32[192,1024]{1,0:T(8,128)}, f32[2,2,48,256]{3,2,1,0:T(8,128)}, f32[2,2,48,128]{3,2,1,0:T(8,128)}, f32[48,192]{1,...) custom-call(bf16[192,1024]{1,0:T(8,128)(2,1)} %x_in.1, bf16[192,1024]{1,0:T(8,128)(2,1)} %t_in.1, ...), custom_call_target="tpu_custom_call" | custom-call | tf_op jit(solution)/shard_map/layer/pallas_call | solution.py:1150
  96.1 2.9 %finish.1 = (bf16[192,1024]{1,0:T(8,128)(2,1)}, f32[1]{0:T(128)}, f32[192,1024]{1,0:T(8,128)}, f32[48,192]{1,0:T(8,128)}, f32[1,192]{1,0:T(1,128)}, /*index=5*/f...) custom-call(bf16[192,1024]{1,0:T(8,128)(2,1)} %get-tuple-element.43., ...), custom_call_target="tpu_custom_call" | custom-call | tf_op jit(solution)/shard_map/finish/pallas_call | solution.py:1258

commit v7 on v6

--- a/solution.py
+++ b/solution.py
@@ -22,7 +22,7 @@
 AXES = ("dp", "row_0", "row_1", "col")
 ROW = ("row_0", "row_1")
 DP_ROW = ("dp", "row_0", "row_1")
-N_SEM = 96
+N_SEM = 90
 HL = 128
 QC = 96
 FA = 512
@@ -261,7 +261,7 @@
     ga, gb, gqa, gqb, gra, grb, gao, gor, dctx, dct, outt, delta,
     dqkvt, dxp, rxi, rx, im, rm, s1, r2, s2, r3, zi, zr, sb0, br, sb1, rb2,
     rqa, rqb, sqa, sqb, ra2, rb3, ro, so1, ro2, so2, so4, ro3,
-    x1, xb1, xq1, stat, gcol, sv, rsv, wown, wqs, vrow, ubs,
+    x1, xb1, xq1, stat, gcol, sv, rs0, rsv, wown, wqs, vrow, ubs,
     lsem, ssem, rsem,
 ):
     d = lax.axis_index("dp")
@@ -883,23 +883,31 @@
     sv[0:8] = transposed(gcol[...])[0:8]
     sv[6:7] = jnp.broadcast_to(jnp.sum(stat[4:5], axis=1, keepdims=True), (1, D))
     sv[7:8] = jnp.broadcast_to(length.astype(f32), (1, D))
-    v_sent = [links.send(sv, rsv.at[0], sib)]
-    v_from = [(0, 1)]
+    v_sent = [links.send(sv, rs0, sib)]
+    v_from = [(0, 0)]
+    half8 = pl.ds(pl.multiple_of(8 * d, 8), 8)
+    other8 = pl.ds(pl.multiple_of(8 * e, 8), 8)
 
     def sv_add():
         v_sent.pop().wait()
         lo, n = v_from[-1]
-        total = sv[...]
-        for i in range(n):
-            total = total + rsv[lo + i]
-        sv[...] = total
+        if n == 0:
+            sv[...] = sv[...] + rs0[...]
+        else:
+            total = sv[half8]
+            for i in range(n):
+                total = total + rsv[lo + i]
+            sv[half8] = total
 
     def sv_send(dev):
         lo = sum(v_from[-1])
         v_from.append((lo, 3))
         v_sent.append(
             triple(
-                rsv.at[pl.ds(lo, 3)], lambda k: sv, lambda k: rsv.at[lo + k - 1], dev
+                rsv.at[pl.ds(lo, 3)],
+                lambda k: sv.at[half8],
+                lambda k: rsv.at[lo + k - 1],
+                dev,
             )
         )
 
@@ -1040,11 +1048,11 @@
     sv_add()
     sv_send(zdev)
     qa_sends = end_b(qa_sum, sqa, ra2)
+    w3[0] = along_z(0, wu_sends)
     qb_sends = end_b(qb_sum, sqb, rb3)
     bd_sends = end_b(bd_sum, sb1.at[1], rb2.at[1])
     so2[0] = end_a(o_sends, so1, ro2).astype(bf16)
     o_x = links.send(so2.at[0], so2.at[1], sib)
-    w3[0] = along_z(0, wu_sends)
     bu_sends = end_b(bu_sum, sb1.at[0], rb2.at[0])
     o_x.wait_recv()
     mine, other = so2[0], so2[1]
@@ -1058,6 +1066,8 @@
     xq1[0, :, 2 * HL :] = end_a(qb_sends, sqb, rb3)
     q3 = links.send(xq1.at[0], xq1.at[1], sib)
     wait_all((w3[1], w3[0]))
+    sv_add()
+    v_other = links.send(sv.at[half8], rsv.at[9], sib)
     x1[0] = s2[:, :, cols(c, FA // 2)].astype(f32)
     for w in range(2):
         for k in range(3):
@@ -1071,8 +1081,9 @@
     for k in range(3):
         ototal = ototal + ro3[k].astype(f32)
     dwo_o[...] = ototal
-    sv_add()
-    sv_o[...] = sv[...]
+    sv_o[half8] = sv[half8]
+    v_other.wait_recv()
+    sv_o[other8] = rsv[9]
     w4.wait_recv()
     dwa_o[d] = x1[0]
     dwa_o[e] = x1[1]
@@ -1236,12 +1247,13 @@
             V((8, TOK), f32),
             V((D, 128), f32),
             V((16, D), f32),
-            V((10, 16, D), f32),
+            V((16, D), f32),
+            V((10, 8, D), f32),
             V((2, RB, D), bf16),
             V((3, RB, C), bf16),
             V((8, 1, C), f32),
             V((6, 128), f32),
-            pltpu.SemaphoreType.DMA((20,)),
+            pltpu.SemaphoreType.DMA((18,)),
             pltpu.SemaphoreType.DMA((N_SEM,)),
             pltpu.SemaphoreType.DMA((N_SEM,)),
         ],

time: 99.3 us -> 98.1 us (0.988)
  Pallas kernels: 97.6 us -> 96.4 us
    pallas_call x1, Pallas kernels: 94.7 us -> 93.5 us  [local_step(): pl.pallas_call(layer, name='layer', out_shape=(sds((C, LEN), bf16), sds((...]
where the time goes in v7:
time: 98.1 us; the launch traced here: 97.9 us
  Pallas kernels  96.4 us (98%)
  between operations  1.5 us (2%)
    pallas_call x1, Pallas kernels, local_step(): pl.pallas_call(layer, name='layer', out_shape=(sds((C, LEN), bf16), sds((...  93.5 us
    pallas_call x1, Pallas kernels, local_step(): pl.pallas_call(finish, name='finish', out_shape=(sds((C, LEN), bf16), sds...  2.9 us

profile of v7, /device:TPU:1, one launch (start us, length us, event | category | flops | bytes accessed | tf_op | source)
XLA Modules:
  0.0 97.9 jit_solution(5030130244525459375)
XLA Ops:
  1.3 93.5 %layer.1 = (bf16[192,1024]{1,0:T(8,128)(2,1)}, f32[192,1024]{1,0:T(8,128)}, f32[2,2,48,256]{3,2,1,0:T(8,128)}, f32[2,2,48,128]{3,2,1,0:T(8,128)}, f32[48,192]{1,...) custom-call(bf16[192,1024]{1,0:T(8,128)(2,1)} %x_in.1, bf16[192,1024]{1,0:T(8,128)(2,1)} %t_in.1, ...), custom_call_target="tpu_custom_call" | custom-call | tf_op jit(solution)/shard_map/layer/pallas_call | solution.py:1161
  94.8 2.9 %finish.1 = (bf16[192,1024]{1,0:T(8,128)(2,1)}, f32[1]{0:T(128)}, f32[192,1024]{1,0:T(8,128)}, f32[48,192]{1,0:T(8,128)}, f32[1,192]{1,0:T(1,128)}, /*index=5*/f...) custom-call(bf16[192,1024]{1,0:T(8,128)(2,1)} %get-tuple-element.43., ...), custom_call_target="tpu_custom_call" | custom-call | tf_op jit(solution)/shard_map/finish/pallas_call | solution.py:1270

commit v8 on v7

--- a/solution.py
+++ b/solution.py
@@ -427,10 +427,6 @@
     cub.wait()
     ub[c, 0:1, :] = jnp.concatenate([ubs[i : i + 1] for i in range(6)], axis=1)
     oz = triple(wo4.at[pl.ds(0, 3)], lambda k: wo4.at[c], lambda k: wo4.at[c], zdev)
-    vz = triple(vec.at[pl.ds(0, 3)], lambda k: vec.at[c], lambda k: vec.at[c], zdev)
-    uz = triple(
-        ub.at[pl.ds(0, 3), 0:1], lambda k: ub.at[c, 0:1], lambda k: ub.at[c, 0:1], zdev
-    )
     wa[d, r, :, cols(c, FA)] = wown[d, :, 0:FA]
     wb[d, r, :, cols(c, FB)] = wown[d, :, FA:]
     wb_a = along_a(wb_ref(r), some_b(3))
@@ -490,6 +486,12 @@
         return wb.at[d, pl.ds(0, 8), :, pl.ds(0, n * FB)]
 
     wb_zg = RingGather(links, wb_z, some_z, zdev(1), zdev(3), (0,), (1,))
+    vz = triple(
+        vec.at[pl.ds(0, 3), 0:8], lambda k: vec.at[c, 0:8], lambda k: vec.at[c, 0:8], zdev
+    )
+    uz = triple(
+        ub.at[pl.ds(0, 3), 0:1], lambda k: ub.at[c, 0:1], lambda k: ub.at[c, 0:1], zdev
+    )
     wb_zg.first()
     wb_s = ToSibling(wb.at[d])
     wb_s.send(wb.at[d, :, :, cols(c, FB)])

time: 98.1 us -> 98.2 us (level)
  no operation moved by 1% of the time
where the time goes in v8:
time: 98.2 us; the launch traced here: 98 us
  Pallas kernels  96.5 us (98%)
  between operations  1.5 us (2%)
    pallas_call x1, Pallas kernels, local_step(): pl.pallas_call(layer, name='layer', out_shape=(sds((C, LEN), bf16), sds((...  93.6 us
    pallas_call x1, Pallas kernels, local_step(): pl.pallas_call(finish, name='finish', out_shape=(sds((C, LEN), bf16), sds...  2.9 us

profile of v8, /device:TPU:1, one launch (start us, length us, event | category | flops | bytes accessed | tf_op | source)
XLA Modules:
  0.0 98.0 jit_solution(11034768091184531284)
XLA Ops:
  1.3 93.6 %layer.1 = (bf16[192,1024]{1,0:T(8,128)(2,1)}, f32[192,1024]{1,0:T(8,128)}, f32[2,2,48,256]{3,2,1,0:T(8,128)}, f32[2,2,48,128]{3,2,1,0:T(8,128)}, f32[48,192]{1,...) custom-call(bf16[192,1024]{1,0:T(8,128)(2,1)} %x_in.1, bf16[192,1024]{1,0:T(8,128)(2,1)} %t_in.1, ...), custom_call_target="tpu_custom_call" | custom-call | tf_op jit(solution)/shard_map/layer/pallas_call | solution.py:1163
  94.9 2.9 %finish.1 = (bf16[192,1024]{1,0:T(8,128)(2,1)}, f32[1]{0:T(128)}, f32[192,1024]{1,0:T(8,128)}, f32[48,192]{1,0:T(8,128)}, f32[1,192]{1,0:T(1,128)}, /*index=5*/f...) custom-call(bf16[192,1024]{1,0:T(8,128)(2,1)} %get-tuple-element.43., ...), custom_call_target="tpu_custom_call" | custom-call | tf_op jit(solution)/shard_map/finish/pallas_call | solution.py:1272
